TPU v7x, 128 devices: a whole 4x4x4 slice. The times are simulated.
128 devices in a mesh: tm: 8 (over x, core), tile: 16 (over z, y).
Axes of the slice: x: 4, y: 4, z: 4, core: 2. Of those that a mesh axis runs over, the one named last changes fastest.
Arguments:
- basis: float32 [256, 256, 512], P(None, 'tile'), may hold values from -6 to 6
- diffusion: float32 [8, 256, 512], P('tm', 'tile'), may hold values from 0.12 to 0.24
- drift_x: float32 [8, 256, 512], P('tm', 'tile'), may hold values from -1 to 1
- drift_y: float32 [8, 256, 512], P('tm', 'tile'), may hold values from -1 to 1
- land_sea: int32 [256, 512], P('tile'), may hold values from 0 to 1, as said below
- obs_cells: int32 [8, 512], P('tm'), may hold values from 0 to 131071
- obs_values: float32 [8, 512], P('tm'), may hold values from -72 to 72
Outputs:
- group_coeffs: float32 [8, 2, 256], P('tm')
- end_fields: float32 [8, 256, 512], P('tm', 'tile')
Inputs may be any that keep to these rules, and one draw needn't show every extreme that they name: `land_sea`: only 0 and 1; both occur. `obs_cells`: cells may repeat within and across groups.
All inputs are finite; a program needn't handle non-finite values.
Results may differ from a plain program's by a relative error of at most 0.0003.
Values sent between devices are 32-bit elements; how exact they have to be, the bound alone decides.
No kernel may reach another device: no remote copies, remote signals or barrier semaphores. Data moves between devices by JAX's collectives and lax.ppermute only.
A program may use at most 128 MiB of HBM per device.

v0:
```python
import jax
import jax.numpy as jnp
from jax import lax
from jax.sharding import PartitionSpec as P

STEPS = 6
NOBS = 512


q_inverse = 10.0
ridge = 0.1


def padded(cells, sides, width):
    for axis, dim in sides:
        count = lax.axis_size(axis)
        ends = count - 1
        head = lax.slice_in_dim(cells, 0, width, axis=dim)
        tail = lax.slice_in_dim(cells, cells.shape[dim] - width, cells.shape[dim], axis=dim)
        cells = jnp.concatenate(
            [
                lax.ppermute(tail, axis, [(i, (i + 1) % count) for i in range(ends)]),
                cells,
                lax.ppermute(head, axis, [((i + 1) % count, i) for i in range(ends)]),
            ],
            axis=dim,
        )
    return cells


def partner(block, axis, bit):
    count = lax.axis_size(axis)
    route = []
    for low in range(count):
        high = low | 1 << bit
        if high != low and high < count:
            route += [(low, high), (high, low)]
    return lax.ppermute(block, axis, route)


def precise_dot(first, second):
    return jnp.dot(first, second, precision=lax.Precision.HIGHEST)


def gain_fields(diffusion, drift_x, drift_y, sea_mask):
    return (
        1.0 - 4.0 * diffusion,
        diffusion * (1.0 - drift_x),
        diffusion * (1.0 + drift_x),
        diffusion * (1.0 - drift_y),
        diffusion * (1.0 + drift_y),
        sea_mask,
    )


def tangent_step(widened, gains):
    center_gain, east_gain, west_gain, north_gain, south_gain, sea_mask = gains
    center = widened[:, 1:-1]
    padded_y = jnp.pad(center, ((0, 0), (0, 0), (1, 1)))
    return sea_mask * (
        center_gain * center
        + east_gain * widened[:, 2:]
        + west_gain * widened[:, :-2]
        + north_gain * padded_y[:, :, 2:]
        + south_gain * padded_y[:, :, :-2]
    )


def chol_solve(factor, right):
    inner = lax.linalg.triangular_solve(factor, right, left_side=True, lower=True)
    return lax.linalg.triangular_solve(factor, inner, left_side=True, lower=True, transpose_a=True)


def merge_pair(left, right):
    left_upper, left_cross, left_lower, left_first, left_second = left
    right_upper, right_cross, right_lower, right_first, right_second = right
    width = left_upper.shape[0]
    factor = jnp.linalg.cholesky(left_lower + right_upper)
    both = chol_solve(factor, jnp.concatenate([left_cross.T, right_cross], axis=1))
    back_left = both[:, :width]
    back_right = both[:, width:]
    back_rhs = chol_solve(factor, (left_second + right_first)[:, None])[:, 0]
    merged = (
        left_upper - precise_dot(left_cross, back_left),
        -precise_dot(left_cross, back_right),
        right_lower - precise_dot(right_cross.T, back_right),
        left_first - precise_dot(left_cross, back_rhs),
        right_second - precise_dot(right_cross.T, back_rhs),
    )
    return (merged, (back_left, back_right, back_rhs))


def solve_root(block):
    upper, cross, lower, first, second = block
    width = upper.shape[0]
    system = jnp.concatenate(
        [jnp.concatenate([upper, cross], axis=1), jnp.concatenate([cross.T, lower], axis=1)], axis=0
    )
    factor = jnp.linalg.cholesky(system)
    answer = chol_solve(factor, jnp.concatenate([first, second])[:, None])[:, 0]
    return (answer[:width], answer[width:])


def shards(basis, diffusion, drift_x, drift_y, land_sea, obs_cells, obs_values):
    width = basis.shape[0]
    rows = basis.shape[1]
    columns = basis.shape[2]
    sea_mask = land_sea.astype(jnp.float32)
    gains = gain_fields(diffusion[0], drift_x[0], drift_y[0], sea_mask)
    field = basis
    for section in range(STEPS):
        widened = padded(field, (("tile", 1),), 1)
        field = tangent_step(widened, gains)
    flat_basis = basis.reshape(width, rows * columns)
    local_prop = precise_dot(flat_basis, field.reshape(width, rows * columns).T)
    offset = lax.axis_index("tile") * (rows * columns)
    local_cells = obs_cells[0] - offset
    inside = ((local_cells >= 0) & (local_cells < rows * columns)).astype(jnp.float32)
    obs_rows = (
        jnp.take(flat_basis, jnp.clip(local_cells, 0, rows * columns - 1), axis=1) * inside[None, :]
    )
    local_info = precise_dot(obs_rows, obs_rows.T)
    local_rhs = precise_dot(obs_rows, obs_values[0])
    prop_sum, info_sum, rhs_sum = lax.psum((local_prop, local_info, local_rhs), "tile")
    propagator = prop_sum / float(rows * columns * lax.axis_size("tile"))
    obs_info = info_sum / float(NOBS)
    obs_rhs = rhs_sum / float(NOBS)
    identity = jnp.eye(width, dtype=jnp.float32)
    block = (
        q_inverse * precise_dot(propagator.T, propagator) + ridge * identity,
        -q_inverse * propagator.T,
        (q_inverse + ridge) * identity + obs_info,
        jnp.zeros((width,), jnp.float32),
        obs_rhs,
    )
    group = lax.axis_index("tm")
    levels = lax.axis_size("tm").bit_length() - 1
    saved = []
    for level in range(levels):
        other = partner((block[0], block[1], block[2], block[3], block[4]), "tm", level)
        upper_half = group >> level & 1 == 1
        left = jax.tree.map(
            lambda first, second: jnp.where(upper_half, second, first), block, other
        )
        right = jax.tree.map(
            lambda first, second: jnp.where(upper_half, first, second), block, other
        )
        block, kept = merge_pair(left, right)
        saved.append(kept)
    start_state, end_state = solve_root(block)
    for level in reversed(range(levels)):
        back_left, back_right, back_rhs = saved[level]
        middle = back_rhs - precise_dot(back_left, start_state) - precise_dot(back_right, end_state)
        upper_half = group >> level & 1 == 1
        start_state = jnp.where(upper_half, middle, start_state)
        end_state = jnp.where(upper_half, end_state, middle)
    group_coeffs = jnp.stack([start_state, end_state])[None]
    end_fields = jnp.tensordot(end_state, basis, axes=1, precision=lax.Precision.HIGHEST)[None]
    return (group_coeffs, end_fields)


def solution(mesh):
    in_specs = (
        P(None, "tile", None),
        P("tm", "tile", None),
        P("tm", "tile", None),
        P("tm", "tile", None),
        P("tile", None),
        P("tm", None),
        P("tm", None),
    )
    out_specs = (P("tm", None, None), P("tm", "tile", None))
    return jax.shard_map(shards, mesh=mesh, in_specs=in_specs, out_specs=out_specs, check_vma=False)
```

profile of v0, /device:TPU:1, one launch (start us, length us, event | category | flops | bytes accessed | tf_op | source)
XLA Modules:
  0.0 793.8 jit_solution(13216752730702053456)
XLA Ops:
  35.0 19.7 %fusion.3 = f32[256,16,512]{2,0,1:T(8,128)} fusion(f32[256,16,512]{2,0,1:T(8,128)} %copy-done.1, f32[256,1,512]{2,0,1:T(8,128)S(1)} %collective-permute-done.2, f32[256,1,512]{2,0,1:T(8,128)S(1)} %collective-permute-done.1, f32[16,512]{1,0:T(8,128)S(1)} %get-tuple-element.191, f32[16,512]{1,0:T(8,128)S(1)} %get-tuple-element.192, ...), kind=kLoop, calls=%fused_computation.24 | loop fusion | flops 25165824 | bytes 18022400 | tf_op jit(solution)/shard_map/mul | solution.py:60
  71.4 19.7 %fusion.8 = f32[256,16,512]{2,0,1:T(8,128)} fusion(f32[256,16,512]{2,0,1:T(8,128)} %fusion.3, f32[256,1,512]{2,0,1:T(8,128)S(1)} %collective-permute-done.4, f32[256,1,512]{2,0,1:T(8,128)S(1)} %collective-permute-done.3, f32[16,512]{1,0:T(8,128)S(1)} %get-tuple-element.191, f32[16,512]{1,0:T(8,128)S(1)} %get-tuple-element.192, ...), kind=kLoop, calls=%fused_computation.29 | loop fusion | flops 25165824 | bytes 18022400 | tf_op jit(solution)/shard_map/mul | solution.py:60
  107.2 19.7 %fusion.13 = f32[256,16,512]{2,0,1:T(8,128)} fusion(f32[256,16,512]{2,0,1:T(8,128)} %fusion.8, f32[256,1,512]{2,0,1:T(8,128)S(1)} %collective-permute-done.6, f32[256,1,512]{2,0,1:T(8,128)S(1)} %collective-permute-done.5, f32[16,512]{1,0:T(8,128)S(1)} %get-tuple-element.191, f32[16,512]{1,0:T(8,128)S(1)} %get-tuple-element.192, ...), kind=kLoop, calls=%fused_computation.34 | loop fusion | flops 25165824 | bytes 18022400 | tf_op jit(solution)/shard_map/mul | solution.py:60
  142.0 19.7 %fusion.18 = f32[256,16,512]{2,0,1:T(8,128)} fusion(f32[256,16,512]{2,0,1:T(8,128)} %fusion.13, f32[256,1,512]{2,0,1:T(8,128)S(1)} %collective-permute-done.8, f32[256,1,512]{2,0,1:T(8,128)S(1)} %collective-permute-done.7, f32[16,512]{1,0:T(8,128)S(1)} %get-tuple-element.191, f32[16,512]{1,0:T(8,128)S(1)} %get-tuple-element.192, ...), kind=kLoop, calls=%fused_computation.39 | loop fusion | flops 25165824 | bytes 18022400 | tf_op jit(solution)/shard_map/mul | solution.py:60
  182.5 19.7 %fusion.23 = f32[256,16,512]{2,0,1:T(8,128)} fusion(f32[256,16,512]{2,0,1:T(8,128)} %fusion.18, f32[256,1,512]{2,0,1:T(8,128)S(1)} %collective-permute-done.10, f32[256,1,512]{2,0,1:T(8,128)S(1)} %collective-permute-done.9, f32[16,512]{1,0:T(8,128)S(1)} %get-tuple-element.191, f32[16,512]{1,0:T(8,128)S(1)} %get-tuple-element.192, ...), kind=kLoop, calls=%fused_computation.44 | loop fusion | flops 25165824 | bytes 18022400 | tf_op jit(solution)/shard_map/mul | solution.py:60
  228.7 43.2 %fusion.69 = f32[256,256]{0,1:T(8,128)} fusion(f32[256,16,512]{2,0,1:T(8,128)} %fusion.23, f32[256,1,512]{2,0,1:T(8,128)S(1)} %collective-permute-done.12, f32[256,1,512]{2,0,1:T(8,128)S(1)} %collective-permute-done.11, f32[16,512]{1,0:T(8,128)S(1)} %get-tuple-element.191, f32[16,512]{1,0:T(8,128)S(1)} %get-tuple-element.192, ...), kind=kOutput, calls=%fused_computation.106 | convolution fusion | flops 6467616768 | bytes 18284544 | tf_op jit(solution)/shard_map/dot_general | solution.py:42
  272.3 36.8 %psum.23 = f32[256]{0:T(256)S(1)} all-reduce(f32[256]{0:T(256)S(1)} %bitcast.511), channel_id=1, replica_groups=mesh['tm'=8,'tile'=16] {'tile'}, use_global_device_ids=true, to_apply=%region_6.9 | all-reduce | flops 256 | bytes 2048 | tf_op jit(solution)/shard_map/psum | solution.py:124
  309.1 12.7 %collective-permute-start.14 = (f32[256]{0:T(256)S(1)}, f32[256]{0:T(256)S(1)}, u32[]{:S(2)}, u32[]{:S(2)}) collective-permute-start(f32[256]{0:T(256)S(1)} %broadcast_multiply_fusion), channel_id=1, source_target_pairs={{0,16},{16,0},{32,48},{48,32},{64,80},{80,64},{96,112},{112,96},{1... | collective-permute-start | bytes 3080 | tf_op jit(solution)/shard_map/ppermute | solution.py:38
  322.5 49.0 %all-reduce.11.cloned.1.call-done = (f32[256,256]{0,1:T(8,128)}, f32[256,256]{0,1:T(8,128)}) async-done(((f32[256,256]{0,1:T(8,128)}, f32[256,256]{0,1:T(8,128)}), (f32[256,256]{0,1:T(8,128)}, f32[256,256]{0,1:T(8,128)})) %all-reduce.11.cloned.1.call-update) | async-done | bytes 524304 | tf_op jit(solution)/shard_map/psum | solution.py:124
  379.3 11.7 %cholesky.392 = f32[128,128]{1,0:T(8,128)S(1)} custom-call(f32[128,128]{1,0:T(8,128)S(1)} %cholesky.469), custom_call_target="Cholesky" | custom-call | tf_op jit(solution)/shard_map/jit(cholesky)/cholesky | solution.py:78
  401.4 11.7 %cholesky.402 = f32[128,128]{1,0:T(8,128)S(1)} custom-call(f32[128,128]{1,0:T(8,128)S(1)} %convolution_subtract_fusion.7), custom_call_target="Cholesky" | custom-call | tf_op jit(solution)/shard_map/jit(cholesky)/cholesky | solution.py:78
  419.4 19.7 %custom-call.65 = f32[2,128,128]{1,2,0:T(8,128)S(1)} custom-call(f32[2,128,128]{2,1,0:T(8,128)S(1)} %get-tuple-element.97), custom_call_target="InvertDiagBlocksLowerTriangular" | custom-call | tf_op jit(solution)/shard_map/triangular_solve/custom-call.10 | solution.py:71
  459.7 11.7 %cholesky.419 = f32[128,128]{1,0:T(8,128)S(1)} custom-call(f32[128,128]{1,0:T(8,128)S(1)} %cholesky.472), custom_call_target="Cholesky" | custom-call | tf_op jit(solution)/shard_map/jit(cholesky)/cholesky | solution.py:78
  481.8 11.7 %cholesky.429 = f32[128,128]{1,0:T(8,128)S(1)} custom-call(f32[128,128]{1,0:T(8,128)S(1)} %convolution_subtract_fusion.6), custom_call_target="Cholesky" | custom-call | tf_op jit(solution)/shard_map/jit(cholesky)/cholesky | solution.py:78
  500.4 19.7 %custom-call.70 = f32[2,128,128]{1,2,0:T(8,128)S(1)} custom-call(f32[2,128,128]{2,1,0:T(8,128)S(1)} %get-tuple-element.101), custom_call_target="InvertDiagBlocksLowerTriangular" | custom-call | tf_op jit(solution)/shard_map/triangular_solve/custom-call.10 | solution.py:71
  542.4 11.7 %cholesky.446 = f32[128,128]{1,0:T(8,128)S(1)} custom-call(f32[128,128]{1,0:T(8,128)S(1)} %cholesky.475), custom_call_target="Cholesky" | custom-call | tf_op jit(solution)/shard_map/jit(cholesky)/cholesky | solution.py:78
  566.1 11.7 %cholesky.456 = f32[128,128]{1,0:T(8,128)S(1)} custom-call(f32[128,128]{1,0:T(8,128)S(1)} %convolution_subtract_fusion.5), custom_call_target="Cholesky" | custom-call | tf_op jit(solution)/shard_map/jit(cholesky)/cholesky | solution.py:78
  585.9 20.1 %custom-call.75 = f32[2,128,128]{1,2,0:T(8,128)S(1)} custom-call(f32[2,128,128]{2,1,0:T(8,128)S(1)} %get-tuple-element.105), custom_call_target="InvertDiagBlocksLowerTriangular" | custom-call | tf_op jit(solution)/shard_map/triangular_solve/custom-call.10 | solution.py:71
  619.8 11.7 %cholesky.167 = f32[128,128]{1,0:T(8,128)S(1)} custom-call(f32[128,128]{1,0:T(8,128)S(1)} %cholesky.478), custom_call_target="Cholesky" | custom-call | tf_op jit(solution)/shard_map/jit(cholesky)/cholesky | solution.py:99
  644.1 11.7 %cholesky.190 = f32[128,128]{1,0:T(8,128)S(1)} custom-call(f32[128,128]{1,0:T(8,128)S(1)} %cholesky.482), custom_call_target="Cholesky" | custom-call | tf_op jit(solution)/shard_map/jit(cholesky)/cholesky | solution.py:99
  668.6 11.7 %cholesky.294 = f32[128,128]{1,0:T(8,128)S(1)} custom-call(f32[128,128]{1,0:T(8,128)S(1)} %cholesky.487), custom_call_target="Cholesky" | custom-call | tf_op jit(solution)/shard_map/jit(cholesky)/cholesky | solution.py:99
  708.7 14.2 %while.25 = (s32[]{:T(128)}, f32[512,512]{1,0:T(8,128)}, s32[4,2]{0,1:T(2,128)S(1)}, f32[4,128,128]{2,1,0:T(8,128)}, s32[]{:T(128)}) while((s32[]{:T(128)}, f32[512,512]{1,0:T(8,128)}, s32[4,2]{0,1:T(2,128)S(1)}, f32[4,128,128]{2,1,0:T(8,128)}, s32[]{:T(128)}) %tuple.143), condition=%wide.while_cond.4, body=%wide.while_body.4.sunk | while | flops 2 | bytes 132705 | solution.py:71
  722.9 40.4 %custom-call.48 = f32[4,128,128]{1,2,0:T(8,128)S(1)} custom-call(f32[4,128,128]{2,1,0:T(8,128)} %get-tuple-element.47), custom_call_target="InvertDiagBlocksLowerTriangular" | custom-call | tf_op jit(solution)/shard_map/triangular_solve | solution.py:71
  773.6 11.7 %fusion.263 = f32[1,16,512]{2,0,1:T(1,128)S(1)} fusion(f32[256,1,1]{0,1,2:T(1,128)S(1)} %bitcast.497, f32[256,16,512]{2,1,0:T(8,128)} %param.18), kind=kOutput, calls=%fused_computation.450 | convolution fusion | flops 25165824 | bytes 8422400 | tf_op jit(solution)/shard_map/dot_general | solution.py:158
  (329 shorter events, 327.5 us)
Async XLA Ops:
  7.2 364.3 %all-reduce.11.cloned.1.call-start = ((), (), s32[]{:S(2)}) async-start(), calls=%async_computation | async-start | bytes 1048576 | tf_op jit(solution)/shard_map/psum | solution.py:124
  18.8 15.3 %collective-permute-start.1 = (f32[256,1,512]{2,0,1:T(8,128)S(1)}, f32[256,1,512]{2,0,1:T(8,128)S(1)}, u32[]{:S(2)}, u32[]{:S(2)}) collective-permute-start(f32[256,1,512]{2,0,1:T(8,128)S(1)} %get-tuple-element.162), channel_id=1, source_target_pairs={{1,0},{2,1},{3,2},{4,3},{5,4},{6,5},{7,6},{8,7},{9,8},{10,9},{11,1... | collective-permute-start | bytes 1572872 | tf_op jit(solution)/shard_map/ppermute | solution.py:24
  20.1 14.9 %collective-permute-start.2 = (f32[256,1,512]{2,0,1:T(8,128)S(1)}, f32[256,1,512]{2,0,1:T(8,128)S(1)}, u32[]{:S(2)}, u32[]{:S(2)}) collective-permute-start(f32[256,1,512]{2,0,1:T(8,128)S(1)} %get-tuple-element.163), channel_id=1, source_target_pairs={{0,1},{1,2},{2,3},{3,4},{4,5},{5,6},{6,7},{7,8},{8,9},{9,10},{10,1... | collective-permute-start | bytes 1572872 | tf_op jit(solution)/shard_map/ppermute | solution.py:22
  56.0 14.5 %collective-permute-start.3 = (f32[256,1,512]{2,0,1:T(8,128)S(1)}, f32[256,1,512]{2,0,1:T(8,128)S(1)}, u32[]{:S(2)}, u32[]{:S(2)}) collective-permute-start(f32[256,1,512]{2,0,1:T(8,128)S(1)} %get-tuple-element.160), channel_id=1, source_target_pairs={{1,0},{2,1},{3,2},{4,3},{5,4},{6,5},{7,6},{8,7},{9,8},{10,9},{11,1... | collective-permute-start | bytes 1572872 | tf_op jit(solution)/shard_map/ppermute | solution.py:24
  57.3 14.1 %collective-permute-start.4 = (f32[256,1,512]{2,0,1:T(8,128)S(1)}, f32[256,1,512]{2,0,1:T(8,128)S(1)}, u32[]{:S(2)}, u32[]{:S(2)}) collective-permute-start(f32[256,1,512]{2,0,1:T(8,128)S(1)} %get-tuple-element.161), channel_id=1, source_target_pairs={{0,1},{1,2},{2,3},{3,4},{4,5},{5,6},{6,7},{7,8},{8,9},{9,10},{10,1... | collective-permute-start | bytes 1572872 | tf_op jit(solution)/shard_map/ppermute | solution.py:22
  92.4 13.7 %collective-permute-start.5 = (f32[256,1,512]{2,0,1:T(8,128)S(1)}, f32[256,1,512]{2,0,1:T(8,128)S(1)}, u32[]{:S(2)}, u32[]{:S(2)}) collective-permute-start(f32[256,1,512]{2,0,1:T(8,128)S(1)} %get-tuple-element.158), channel_id=1, source_target_pairs={{1,0},{2,1},{3,2},{4,3},{5,4},{6,5},{7,6},{8,7},{9,8},{10,9},{11,1... | collective-permute-start | bytes 1572872 | tf_op jit(solution)/shard_map/ppermute | solution.py:24
  93.7 13.5 %collective-permute-start.6 = (f32[256,1,512]{2,0,1:T(8,128)S(1)}, f32[256,1,512]{2,0,1:T(8,128)S(1)}, u32[]{:S(2)}, u32[]{:S(2)}) collective-permute-start(f32[256,1,512]{2,0,1:T(8,128)S(1)} %get-tuple-element.159), channel_id=1, source_target_pairs={{0,1},{1,2},{2,3},{3,4},{4,5},{5,6},{6,7},{7,8},{8,9},{9,10},{10,1... | collective-permute-start | bytes 1572872 | tf_op jit(solution)/shard_map/ppermute | solution.py:22
  128.2 12.8 %collective-permute-start.7 = (f32[256,1,512]{2,0,1:T(8,128)S(1)}, f32[256,1,512]{2,0,1:T(8,128)S(1)}, u32[]{:S(2)}, u32[]{:S(2)}) collective-permute-start(f32[256,1,512]{2,0,1:T(8,128)S(1)} %get-tuple-element.156), channel_id=1, source_target_pairs={{1,0},{2,1},{3,2},{4,3},{5,4},{6,5},{7,6},{8,7},{9,8},{10,9},{11,1... | collective-permute-start | bytes 1572872 | tf_op jit(solution)/shard_map/ppermute | solution.py:24
  129.5 12.4 %collective-permute-start.8 = (f32[256,1,512]{2,0,1:T(8,128)S(1)}, f32[256,1,512]{2,0,1:T(8,128)S(1)}, u32[]{:S(2)}, u32[]{:S(2)}) collective-permute-start(f32[256,1,512]{2,0,1:T(8,128)S(1)} %get-tuple-element.157), channel_id=1, source_target_pairs={{0,1},{1,2},{2,3},{3,4},{4,5},{5,6},{6,7},{7,8},{8,9},{9,10},{10,1... | collective-permute-start | bytes 1572872 | tf_op jit(solution)/shard_map/ppermute | solution.py:22
  163.0 12.6 %collective-permute-start.10 = (f32[256,1,512]{2,0,1:T(8,128)S(1)}, f32[256,1,512]{2,0,1:T(8,128)S(1)}, u32[]{:S(2)}, u32[]{:S(2)}) collective-permute-start(f32[256,1,512]{2,0,1:T(8,128)S(1)} %get-tuple-element.155), channel_id=1, source_target_pairs={{0,1},{1,2},{2,3},{3,4},{4,5},{5,6},{6,7},{7,8},{8,9},{9,10},{10,1... | collective-permute-start | bytes 1572872 | tf_op jit(solution)/shard_map/ppermute | solution.py:22
  168.7 13.8 %collective-permute-start.9 = (f32[256,1,512]{2,0,1:T(8,128)S(1)}, f32[256,1,512]{2,0,1:T(8,128)S(1)}, u32[]{:S(2)}, u32[]{:S(2)}) collective-permute-start(f32[256,1,512]{2,0,1:T(8,128)S(1)} %get-tuple-element.154), channel_id=1, source_target_pairs={{1,0},{2,1},{3,2},{4,3},{5,4},{6,5},{7,6},{8,7},{9,8},{10,9},{11,1... | collective-permute-start | bytes 1572872 | tf_op jit(solution)/shard_map/ppermute | solution.py:24
  203.5 25.2 %collective-permute-start.11 = (f32[256,1,512]{2,0,1:T(8,128)S(1)}, f32[256,1,512]{2,0,1:T(8,128)S(1)}, u32[]{:S(2)}, u32[]{:S(2)}) collective-permute-start(f32[256,1,512]{2,0,1:T(8,128)S(1)} %get-tuple-element.152), channel_id=1, source_target_pairs={{1,0},{2,1},{3,2},{4,3},{5,4},{6,5},{7,6},{8,7},{9,8},{10,9},{11,1... | collective-permute-start | bytes 1572872 | tf_op jit(solution)/shard_map/ppermute | solution.py:24
  204.8 23.9 %collective-permute-start.12 = (f32[256,1,512]{2,0,1:T(8,128)S(1)}, f32[256,1,512]{2,0,1:T(8,128)S(1)}, u32[]{:S(2)}, u32[]{:S(2)}) collective-permute-start(f32[256,1,512]{2,0,1:T(8,128)S(1)} %get-tuple-element.153), channel_id=1, source_target_pairs={{0,1},{1,2},{2,3},{3,4},{4,5},{5,6},{6,7},{7,8},{8,9},{9,10},{10,1... | collective-permute-start | bytes 1572872 | tf_op jit(solution)/shard_map/ppermute | solution.py:22
  309.1 67.3 %collective-permute-start.14 = (f32[256]{0:T(256)S(1)}, f32[256]{0:T(256)S(1)}, u32[]{:S(2)}, u32[]{:S(2)}) collective-permute-start(f32[256]{0:T(256)S(1)} %broadcast_multiply_fusion), channel_id=1, source_target_pairs={{0,16},{16,0},{32,48},{48,32},{64,80},{80,64},{96,112},{112,96},{1... | collective-permute-start | bytes 3080 | tf_op jit(solution)/shard_map/ppermute | solution.py:38
  321.8 54.6 %collective-permute-start.15 = (f32[256]{0:T(256)S(1)}, f32[256]{0:T(256)S(1)}, u32[]{:S(2)}, u32[]{:S(2)}) collective-permute-start(f32[256]{0:T(256)S(1)} %broadcast_in_dim.22), channel_id=1, source_target_pairs={{0,16},{16,0},{32,48},{48,32},{64,80},{80,64},{96,112},{112,96},{1... | collective-permute-start | bytes 3080 | tf_op jit(solution)/shard_map/ppermute | solution.py:38
  377.4 62.9 %collective-permute-start.16 = (f32[256,256]{1,0:T(8,128)S(1)}, f32[256,256]{1,0:T(8,128)S(1)}, u32[]{:S(2)}, u32[]{:S(2)}) collective-permute-start(f32[256,256]{1,0:T(8,128)S(1)} %multiply_bitcast_fusion), channel_id=1, source_target_pairs={{0,16},{16,0},{32,48},{48,32},{64,80},{80,64},{96,112},{112,96},{1... | collective-permute-start | bytes 786440 | tf_op jit(solution)/shard_map/ppermute | solution.py:38
  440.8 10.9 %collective-permute-start.19 = (f32[256]{0:T(256)S(1)}, f32[256]{0:T(256)S(1)}, u32[]{:S(2)}, u32[]{:S(2)}) collective-permute-start(f32[256]{0:T(256)S(1)} %select_subtract_fusion.11), channel_id=1, source_target_pairs={{0,32},{32,0},{16,48},{48,16},{64,96},{96,64},{80,112},{112,80},{1... | collective-permute-start | bytes 3080 | tf_op jit(solution)/shard_map/ppermute | solution.py:38
  442.5 9.2 %collective-permute-start.20 = (f32[256]{0:T(256)S(1)}, f32[256]{0:T(256)S(1)}, u32[]{:S(2)}, u32[]{:S(2)}) collective-permute-start(f32[256]{0:T(256)S(1)} %select_subtract_fusion.10), channel_id=1, source_target_pairs={{0,32},{32,0},{16,48},{48,16},{64,96},{96,64},{80,112},{112,80},{1... | collective-permute-start | bytes 3080 | tf_op jit(solution)/shard_map/ppermute | solution.py:38
  448.4 11.1 %collective-permute-start.17 = (f32[256,256]{0,1:T(8,128)S(1)}, f32[256,256]{0,1:T(8,128)S(1)}, u32[]{:S(2)}, u32[]{:S(2)}) collective-permute-start(f32[256,256]{0,1:T(8,128)S(1)} %select_subtract_fusion.5), channel_id=1, source_target_pairs={{0,32},{32,0},{16,48},{48,16},{64,96},{96,64},{80,112},{112,80},{1... | collective-permute-start | bytes 786440 | tf_op jit(solution)/shard_map/ppermute | solution.py:38
  449.3 71.9 %collective-permute-start.21 = (f32[256,256]{1,0:T(8,128)S(1)}, f32[256,256]{1,0:T(8,128)S(1)}, u32[]{:S(2)}, u32[]{:S(2)}) collective-permute-start(f32[256,256]{1,0:T(8,128)S(1)} %convolution_negate_fusion.2), channel_id=1, source_target_pairs={{0,32},{32,0},{16,48},{48,16},{64,96},{96,64},{80,112},{112,80},{1... | collective-permute-start | bytes 786440 | tf_op jit(solution)/shard_map/ppermute | solution.py:38
  521.8 14.5 %collective-permute-start.24 = (f32[256]{0:T(256)S(1)}, f32[256]{0:T(256)S(1)}, u32[]{:S(2)}, u32[]{:S(2)}) collective-permute-start(f32[256]{0:T(256)S(1)} %select_subtract_fusion.9), channel_id=1, source_target_pairs={{0,64},{64,0},{16,80},{80,16},{32,96},{96,32},{48,112},{112,48},{1... | collective-permute-start | bytes 3080 | tf_op jit(solution)/shard_map/ppermute | solution.py:38
  524.9 11.9 %collective-permute-start.25 = (f32[256]{0:T(256)S(1)}, f32[256]{0:T(256)}, u32[]{:S(2)}, u32[]{:S(2)}) collective-permute-start(f32[256]{0:T(256)S(1)} %select_subtract_fusion.8), channel_id=1, source_target_pairs={{0,64},{64,0},{16,80},{80,16},{32,96},{96,32},{48,112},{112,48},{1... | collective-permute-start | bytes 3080 | tf_op jit(solution)/shard_map/ppermute | solution.py:38
  532.3 9.8 %collective-permute-start.22 = (f32[256,256]{0,1:T(8,128)S(1)}, f32[256,256]{0,1:T(8,128)S(1)}, u32[]{:S(2)}, u32[]{:S(2)}) collective-permute-start(f32[256,256]{0,1:T(8,128)S(1)} %select_subtract_fusion.3), channel_id=1, source_target_pairs={{0,64},{64,0},{16,80},{80,16},{32,96},{96,32},{48,112},{112,48},{1... | collective-permute-start | bytes 786440 | tf_op jit(solution)/shard_map/ppermute | solution.py:38
  533.2 74.0 %collective-permute-start.26 = (f32[256,256]{1,0:T(8,128)S(1)}, f32[256,256]{1,0:T(8,128)S(1)}, u32[]{:S(2)}, u32[]{:S(2)}) collective-permute-start(f32[256,256]{1,0:T(8,128)S(1)} %convolution_negate_fusion.1), channel_id=1, source_target_pairs={{0,64},{64,0},{16,80},{80,16},{32,96},{96,32},{48,112},{112,48},{1... | collective-permute-start | bytes 786440 | tf_op jit(solution)/shard_map/ppermute | solution.py:38
  (26 other events, 1353.1 us)
Sparse Core Ops, SparseCore 0:
  272.0 99.4 all-reduce.10
where the time goes:
time: 810 us; the launch traced here: 794 us
  other arithmetic  392 us (48%)
  waiting for transfers between devices  110 us (14%)
  matrix products  96.9 us (12%)
  starting transfers between devices  69.3 us (9%)
  local copies, waits for them, and re-layouts  67 us (8%)
  blocking collectives  36.8 us (5%)
  between operations  22.2 us (3%)
    another operation x20, other arithmetic, merge_pair(): factor = jnp.linalg.cholesky(left_lower + right_upper)  103 us
    another operation x15, other arithmetic, chol_solve(): lax.linalg.triangular_solve(factor, inner, left_side=True, lower=True, tr...  103 us
    mul x5, other arithmetic, tangent_step(): sea_mask * (center_gain * center + east_gain * widened[:, 2:] + west_gain...  98.6 us
    another operation x15, other arithmetic, solve_root(): factor = jnp.linalg.cholesky(system)  79.3 us
    dot_general x25, matrix products, precise_dot(): return jnp.dot(first, second, precision=lax.Precision.HIGHEST)  57.2 us
    psum x1, waiting for transfers between devices, shards(): lax.psum((local_prop, local_info, local_rhs), 'tile')  49 us
    ppermute x6, waiting for transfers between devices, padded(): lax.ppermute(head, axis, [((i + 1) % count, i) for i in range(ends)])  38.8 us
    psum x1, blocking collectives, shards(): lax.psum((local_prop, local_info, local_rhs), 'tile')  36.8 us
  transfers between devices with their start and end apart: 28, of which 14 were waited for; matrix products, arithmetic and copies ran while one was open for 27% of the time, Pallas kernels for 0%

commit v1 on v0

v1 whole, which is shorter than its diff:
```python
import functools

import jax
import jax.numpy as jnp
from jax import lax
from jax.experimental import pallas as pl
from jax.experimental.pallas import tpu as pltpu
from jax.sharding import PartitionSpec as P

STEPS = 6
REACH = STEPS // 2
NOBS = 512
Q = 10.0
RIDGE = 0.1
SUB = 8
LANES = 128
SLICE = 40
TAIL = 8


def split(value):
    high = value.astype(jnp.bfloat16)
    low = (value - high.astype(jnp.float32)).astype(jnp.bfloat16)
    return high, low


def dot3(left, right):
    lh, ll = split(left)
    rh, rl = split(right)
    return lax.dot_general(
        jnp.concatenate([lh, lh, ll], axis=1),
        jnp.concatenate([rh, rl, rh], axis=1),
        (((1,), (1,)), ((), ())),
        preferred_element_type=jnp.float32,
    )


def full(left, right, contract=(1, 0)):
    return lax.dot_general(
        left,
        right,
        (((contract[0],), (contract[1],)), ((), ())),
        precision=lax.Precision.HIGHEST,
        preferred_element_type=jnp.float32,
    )


def deal_matrix(columns, copies):
    strips = columns // LANES
    source = lax.broadcasted_iota(jnp.int32, (columns, columns), 0)
    target = lax.broadcasted_iota(jnp.int32, (columns, columns), 1)
    wanted = (target % LANES) * strips + target // LANES
    one = jnp.where(source == wanted, 1.0, 0.0).astype(jnp.bfloat16)
    return jnp.concatenate([one] * copies, axis=0)


def dealt(value, deal):
    parts, rest = [], value
    for _ in range(deal.shape[0] // deal.shape[1]):
        part = rest.astype(jnp.bfloat16)
        parts.append(part)
        rest = rest - part.astype(jnp.float32)
    return jnp.dot(jnp.concatenate(parts, axis=1), deal, preferred_element_type=jnp.float32)


def strips_of(value):
    return [value[:, c : c + LANES] for c in range(0, value.shape[1], LANES)]


def after(strips):
    return strips[1:] + [pltpu.roll(strips[0], LANES - 1, 1)]


def before(strips):
    return [pltpu.roll(strips[-1], 1, 1)] + strips[:-1]


def lay_kernel(rows, count_ref, value_ref, *refs):
    basis_refs, (field_ref, out_ref, deal, held) = refs[:-4], refs[-4:]
    step_id = pl.program_id(0)
    width = held.shape[1]
    block = basis_refs[0].shape[0] // rows

    @pl.when(step_id == 0)
    def _():
        deal[...] = deal_matrix(deal.shape[1], 2)

    lines = []
    for i in range(rows):
        span = pl.ds(i, block, stride=rows)
        lines.append(jnp.concatenate([ref[span, :] for ref in basis_refs], axis=1))
    laid = dealt(jnp.concatenate(lines, axis=0), deal[...])
    at = pl.ds(pl.multiple_of(step_id * block, block), block)
    for i in range(rows):
        line = laid[i * block : (i + 1) * block]
        field_ref[i] = line
        held[i, at, :] = line

    @pl.when(step_id == pl.num_programs(0) - 1)
    def _():
        out_ref[...] = jnp.zeros_like(out_ref)

        def body(i, carry):
            field = held[i]
            count = count_ref[pl.ds(i, 1), :]
            value = jnp.broadcast_to(value_ref[pl.ds(i, 1), :], (TAIL, count.shape[1]))
            out_ref[...] += dot3(jnp.concatenate([field * count, value], axis=0), field)
            return carry

        lax.fori_loop(0, rows, body, 0)


def lay_basis(basis2, count, value, width, rows):
    columns = basis2.shape[1]
    block = 32
    strips = columns // LANES
    return pl.pallas_call(
        functools.partial(lay_kernel, rows),
        grid=(width // block,),
        in_specs=[
            pl.BlockSpec((rows, columns), lambda k: (0, 0)),
            pl.BlockSpec((rows, columns), lambda k: (0, 0)),
            *[pl.BlockSpec((block * rows, LANES), lambda k, c=c: (k, c)) for c in range(strips)],
        ],
        out_specs=[
            pl.BlockSpec((rows, block, columns), lambda k: (0, k, 0)),
            pl.BlockSpec((width + TAIL, width), lambda k: (0, 0)),
        ],
        out_shape=[
            jax.ShapeDtypeStruct((rows, width, columns), jnp.float32),
            jax.ShapeDtypeStruct((width + TAIL, width), jnp.float32),
        ],
        scratch_shapes=[
            pltpu.VMEM((2 * columns, columns), jnp.bfloat16),
            pltpu.VMEM((rows, width, columns), jnp.float32),
        ],
        name="lay_basis",
    )(count, value, *[basis2] * strips)


def prop_kernel(
    place_ref, model_ref, field_ref, low_mine, low_theirs, high_mine, high_theirs, obs_ref,
    out_ref, deal, model, wide, edges, fore, back,
):
    step_id = pl.program_id(0)
    steps = pl.num_programs(0)
    rows, block, columns = field_ref.shape
    ext = rows + 2 * REACH
    width = fore.shape[1]
    half = width // 2
    core, tile, last_tile = place_ref[0], place_ref[1], place_ref[2]
    turn = lax.rem(step_id + core * (steps // 2), steps)

    @pl.when(step_id == 0)
    def _():
        deal[...] = deal_matrix(columns, 3)
        model[...] = jnp.zeros_like(model)
        for f in range(4):
            for r in range(REACH):
                model[f, r : r + 1, :] = low_mine[r, half + f : half + f + 1, :]
                at = REACH + rows + r
                model[f, at : at + 1, :] = high_mine[r, half + f : half + f + 1, :]
            for r in range(rows):
                model[f, REACH + r : REACH + r + 1, :] = model_ref[f, r : r + 1, :]
        tall = model.shape[1]
        together = dealt(model[...].reshape(4 * tall, columns), deal[...])
        lines = lax.broadcasted_iota(jnp.int32, (tall, LANES), 0)
        lanes = lax.broadcasted_iota(jnp.int32, (tall, LANES), 1)
        no_west = jnp.logical_and(tile == 0, lines == REACH)
        no_east = jnp.logical_and(tile == last_tile, lines == REACH + rows - 1)
        diffusion, drift_x, drift_y, sea = (
            strips_of(together[f * tall : (f + 1) * tall]) for f in range(4)
        )
        center, east, west, north, south = [], [], [], [], []
        for c in range(len(sea)):
            center.append(sea[c] * (1.0 - 4.0 * diffusion[c]))
            east.append(jnp.where(no_east, 0.0, sea[c] * (diffusion[c] * (1.0 - drift_x[c]))))
            west.append(jnp.where(no_west, 0.0, sea[c] * (diffusion[c] * (1.0 + drift_x[c]))))
            up = sea[c] * (diffusion[c] * (1.0 - drift_y[c]))
            down = sea[c] * (diffusion[c] * (1.0 + drift_y[c]))
            if c == len(sea) - 1:
                up = jnp.where(lanes == LANES - 1, 0.0, up)
            if c == 0:
                down = jnp.where(lanes == 0, 0.0, down)
            north.append(up)
            south.append(down)
        sets = (
            (center, 0), (east, 0), (west, 0), (north, 0), (south, 0),
            (west, 1), (east, -1), (after(south), 0), (before(north), 0),
        )
        for g, (values, move) in enumerate(sets):
            for r in range(ext):
                if not 0 <= r + move < ext:
                    continue
                line = jnp.concatenate([v[r + move : r + move + 1] for v in values], axis=1)
                wide[g * ext + r] = jnp.broadcast_to(line, (SUB, columns))

    def deal_edges(low, high):
        count = REACH * half
        low_rows = low[:, :half, :].reshape(count, columns)
        high_rows = high[:, :half, :].reshape(count, columns)
        twice = deal[: 2 * columns, :]
        edges[:REACH] = dealt(low_rows, twice).reshape(REACH, half, columns)
        edges[REACH:] = dealt(high_rows, twice).reshape(REACH, half, columns)

    @pl.when(step_id == 0)
    def _():
        deal_edges(low_mine, high_mine)

    @pl.when(step_id == steps // 2)
    def _():
        deal_edges(low_theirs, high_theirs)

    def one(kt, carry):
        near = pl.ds(pl.multiple_of(kt * SUB, SUB), SUB)
        edge = pl.ds(pl.multiple_of(lax.rem(step_id, steps // 2) * block + kt * SUB, SUB), SUB)
        store = pl.ds(pl.multiple_of(turn * block + kt * SUB, SUB), SUB)

        def start(i):
            if i < 0:
                return strips_of(edges[i + REACH, edge, :])
            if i >= rows:
                return strips_of(edges[i - rows + REACH, edge, :])
            return strips_of(field_ref[i, near, :])

        for target, sets in ((fore, (0, 1, 2, 3, 4)), (back, (0, 5, 6, 7, 8))):
            levels = [{} for _ in range(REACH + 1)]
            for lead in range(-REACH, rows + REACH):
                levels[0][lead] = start(lead)
                for s in range(1, REACH + 1):
                    i = lead - s
                    if -REACH + s <= i < rows + REACH - s:
                        prev = levels[s - 1]
                        gains = [wide[g * ext + i + REACH] for g in sets]
                        shifted = (
                            prev[i], prev[i + 1], prev[i - 1], after(prev[i]), before(prev[i])
                        )
                        levels[s][i] = []
                        for c in range(columns // LANES):
                            terms = [
                                gain[:, c * LANES : (c + 1) * LANES] * value[c]
                                for gain, value in zip(gains, shifted)
                            ]
                            levels[s][i].append(
                                (terms[0] + (terms[1] + terms[2])) + (terms[3] + terms[4])
                            )
                i = lead - REACH
                if 0 <= i < rows:
                    target[i, store, :] = jnp.concatenate(levels[REACH][i], axis=1)
        return carry

    lax.fori_loop(0, block // SUB, one, 0)

    @pl.when(step_id == steps - 1)
    def _():
        count = out_ref.shape[0]
        part = width // count

        def body(i, carry):
            product = dot3(back[i], fore[i])
            fresh = i == 0
            for t in range(count):
                piece = product[t * part : (t + 1) * part]
                out_ref[t, :part, :] = jnp.where(fresh, 0.0, out_ref[t, :part, :]) + piece
            return carry

        lax.fori_loop(0, rows, body, 0)
        for t in range(count):
            out_ref[t, part : 2 * part, :] = obs_ref[t * part : (t + 1) * part, :]
            out_ref[t, 2 * part :, :] = obs_ref[width : width + SLICE - 2 * part, :]


def prop_terms(place, model, field, edges, obs, count):
    rows, width, columns = field.shape
    block = 32
    steps = width // block
    ext = rows + 2 * REACH
    vmem = pl.BlockSpec(memory_space=pltpu.VMEM)
    return pl.pallas_call(
        prop_kernel,
        grid_spec=pltpu.PrefetchScalarGridSpec(
            num_scalar_prefetch=1,
            grid=(steps,),
            in_specs=[
                vmem,
                pl.BlockSpec(
                    (rows, block, columns),
                    lambda k, place: (0, lax.rem(k + place[0] * (steps // 2), steps), 0),
                ),
                vmem,
                vmem,
                vmem,
                vmem,
                vmem,
            ],
            out_specs=pl.BlockSpec((count, SLICE, width), lambda k, place: (0, 0, 0)),
            scratch_shapes=[
                pltpu.VMEM((3 * columns, columns), jnp.bfloat16),
                pltpu.VMEM((4, -(-ext // SUB) * SUB, columns), jnp.float32),
                pltpu.VMEM((9 * ext, SUB, columns), jnp.float32),
                pltpu.VMEM((2 * REACH, width // 2, columns), jnp.float32),
                pltpu.VMEM((rows, width, columns), jnp.float32),
                pltpu.VMEM((rows, width, columns), jnp.float32),
            ],
        ),
        out_shape=jax.ShapeDtypeStruct((count, SLICE, width), jnp.float32),
        name="prop_terms",
    )(place, model, field, *edges, obs)


def eye_mask(width):
    row = lax.broadcasted_iota(jnp.int32, (width, width), 0)
    col = lax.broadcasted_iota(jnp.int32, (width, width), 1)
    return row, col


def product(left, right, passes):
    if passes == 1:
        return jnp.dot(
            left.astype(jnp.bfloat16),
            right.astype(jnp.bfloat16),
            preferred_element_type=jnp.float32,
        )
    if passes == 3:
        lh, ll = split(left)
        rh, rl = split(right)
        return jnp.dot(
            jnp.concatenate([lh, lh, ll], axis=1),
            jnp.concatenate([rh, rl, rh], axis=0),
            preferred_element_type=jnp.float32,
        )
    return full(left, right)


def inverses(mats):
    width = mats[0].shape[0]
    row, col = eye_mask(width)
    identity = jnp.where(row == col, 1.0, 0.0).astype(jnp.float32)
    guesses = []
    for mat in mats:
        bound = jnp.max(jnp.sum(jnp.abs(mat), axis=0, keepdims=True), axis=1, keepdims=True)
        guesses.append(identity * (1.7 / bound))

    def stage(state, passes, goal, slowest):
        def more(state):
            turn, error, last = state[0], state[1], state[2]
            going = jnp.logical_and(error > goal, turn < 100)
            return jnp.logical_and(going, jnp.logical_or(error < slowest * last, last == 0.0))

        def improve(state):
            error = jnp.float32(0.0)
            found = []
            for mat, guess in zip(mats, state[3:]):
                rest = identity - product(mat, guess, passes[0])
                found.append(guess + product(guess, rest, passes[1]))
                error = jnp.maximum(error, jnp.sum(rest * rest))
            return (state[0] + 1, error, state[1], *found)

        return lax.while_loop(more, improve, state)

    found = guesses
    turn = jnp.int32(0)
    large = jnp.float32(1e30)
    for passes, goal, slowest in (((1, 1), 2.0, 0.5), ((3, 1), 1e-3, 0.5), ((6, 3), 1e-6, 2.0)):
        state = stage((turn, large, jnp.float32(0.0), *found), passes, goal, slowest)
        turn, found = state[0], state[3:]
    return found


def pair_kernel(core_ref, own_ref, other_ref, both_ref, send_ref, left_ref, right_ref, mid_ref, prop, info):
    count, _, width = own_ref.shape
    part = width // count
    first = core_ref[0] == 0
    row, col = eye_mask(width)
    identity = jnp.where(row == col, 1.0, 0.0).astype(jnp.float32)
    for t in range(count):
        span = pl.ds(t * part, part)
        for slot, lead in ((0, True), (1, False)):
            mine, theirs = own_ref[t], other_ref[t]
            chosen = jnp.where(first, mine, theirs) if lead else jnp.where(first, theirs, mine)
            prop[slot, span, :] = chosen[:part]
            info[slot, span, :] = chosen[part : 2 * part]
    rhs_own, rhs_other = own_ref[0, 2 * part :, :], other_ref[0, 2 * part :, :]
    rhs_left = jnp.where(first, rhs_own, rhs_other)
    rhs_right = jnp.where(first, rhs_other, rhs_own)
    p_left, p_right = prop[0], prop[1]
    square_left = full(p_left, p_left, (0, 0))
    square_right = full(p_right, p_right, (0, 0))
    middle = (Q + 2 * RIDGE) * identity + info[0] + Q * square_right
    (back,) = inverses([middle])
    toward_left = full(p_left, back, (0, 0))
    toward_right = full(jnp.concatenate([p_right, rhs_left], axis=0), back)
    mid = toward_right[width:]
    toward_right = toward_right[:width]
    by_left = full(jnp.concatenate([toward_left, mid], axis=0), p_left)
    by_right = full(jnp.concatenate([toward_left, toward_right, mid], axis=0), p_right, (1, 1))
    upper = Q * square_left + RIDGE * identity - (Q * Q) * by_left[:width]
    cross = -(Q * Q) * by_right[:width]
    lower = (Q + RIDGE) * identity + info[1] - (Q * Q) * by_right[width : 2 * width]
    head = Q * by_left[width:]
    tail = rhs_right + Q * by_right[2 * width :]
    lower_diag = jnp.sum(jnp.where(row == col, lower, 0.0), axis=0, keepdims=True)
    both_ref[0, :width, :] = jnp.where(row >= col, upper, lower)
    small = lax.broadcasted_iota(jnp.int32, (TAIL, width), 0)
    both_ref[0, width:, :] = jnp.where(small == 0, lower_diag, jnp.where(small == 1, head, tail))
    both_ref[1, :width, :] = cross
    both_ref[1, width:, :] = jnp.zeros((TAIL, width), jnp.float32)
    send_ref[...] = jnp.where(first, both_ref[0], both_ref[1])
    left_ref[...] = Q * toward_left
    right_ref[...] = Q * toward_right
    mid_ref[...] = mid


def merge_pair(core, own, other):
    count, _, width = own.shape
    vmem = pl.BlockSpec(memory_space=pltpu.VMEM)
    block = jax.ShapeDtypeStruct((width, width), jnp.float32)
    return pl.pallas_call(
        pair_kernel,
        in_specs=[pl.BlockSpec(memory_space=pltpu.SMEM), vmem, vmem],
        out_specs=[vmem] * 5,
        out_shape=[
            jax.ShapeDtypeStruct((2, width + TAIL, width), jnp.float32),
            jax.ShapeDtypeStruct((width + TAIL, width), jnp.float32),
            block,
            block,
            jax.ShapeDtypeStruct((TAIL, width), jnp.float32),
        ],
        scratch_shapes=[pltpu.VMEM((2, width, width), jnp.float32)] * 2,
        name="merge_pair",
    )(core, own, other)


def chain_kernel(
    place_ref, both_ref, m_prev, o_prev, m_next, o_next, m_far, o_far, left_ref, right_ref, mid_ref,
    coeff_ref, blocks, states,
):
    core, chip = place_ref[0], place_ref[1]
    width = both_ref.shape[2]
    row, col = eye_mask(width)
    blocks[chip] = both_ref[...]
    for mine, theirs, move in ((m_prev, o_prev, 3), (m_next, o_next, 1), (m_far, o_far, 2)):
        at = lax.rem(chip + move, 4)
        blocks[at, core] = mine[...]
        blocks[at, 1 - core] = theirs[...]
    upper, lower, cross, head, tail = [], [], [], [], []
    for c in range(4):
        packed = blocks[c, 0, :width, :]
        turned = packed.T
        small = blocks[c, 0, width:, :]
        upper.append(jnp.where(row >= col, packed, turned))
        off = jnp.where(row < col, packed, turned)
        lower.append(jnp.where(row == col, jnp.broadcast_to(small[0:1], (width, width)), off))
        head.append(jnp.broadcast_to(small[1:2], (TAIL, width)))
        tail.append(jnp.broadcast_to(small[2:3], (TAIL, width)))
        cross.append(blocks[c, 1, :width, :])
    diag = [upper[0], lower[0] + upper[1], lower[1] + upper[2], lower[2] + upper[3], lower[3]]
    rhs = [head[0], tail[0] + head[1], tail[1] + head[2], tail[2] + head[3], tail[3]]
    inv0, inv2, inv4 = inverses([diag[0], diag[2], diag[4]])
    t10 = full(cross[0], inv0, (0, 0))
    t12 = full(cross[1], inv2)
    t32 = full(cross[2], inv2, (0, 0))
    t34 = full(cross[3], inv4)
    z0, z2, z4 = full(rhs[0], inv0), full(rhs[2], inv2), full(rhs[4], inv4)
    diag1 = diag[1] - full(t10, cross[0]) - full(t12, cross[1], (1, 1))
    diag3 = diag[3] - full(t32, cross[2]) - full(t34, cross[3], (1, 1))
    link = -full(t12, cross[2])
    rhs1 = rhs[1] - full(z0, cross[0]) - full(z2, cross[1], (1, 1))
    rhs3 = rhs[3] - full(z2, cross[2]) - full(z4, cross[3], (1, 1))
    (inv1,) = inverses([diag1])
    t31 = full(link, inv1, (0, 0))
    z1 = full(rhs1, inv1)
    diag3 = diag3 - full(t31, link)
    rhs3 = rhs3 - full(z1, link)
    (inv3,) = inverses([diag3])
    y3 = full(rhs3, inv3)
    y1 = z1 - full(y3, t31)
    y0 = z0 - full(y1, t10)
    y2 = z2 - full(y1, t12) - full(y3, t32)
    y4 = z4 - full(y3, t34)
    for c, state in enumerate((y0, y1, y2, y3, y4)):
        states[c] = state
    begin, finish = states[chip], states[chip + 1]
    inner = mid_ref[...] + full(begin, left_ref[...]) + full(finish, right_ref[...])
    first = core == 0
    start = jnp.where(first, begin, inner)
    end = jnp.where(first, inner, finish)
    pick = lax.broadcasted_iota(jnp.int32, (TAIL, width), 0)
    coeff_ref[...] = jnp.where(pick == 0, start, end)


def solve_chain(place, both, received, left, right, mid):
    width = both.shape[2]
    vmem = pl.BlockSpec(memory_space=pltpu.VMEM)
    return pl.pallas_call(
        chain_kernel,
        in_specs=[pl.BlockSpec(memory_space=pltpu.SMEM)] + [vmem] * 10,
        out_specs=vmem,
        out_shape=jax.ShapeDtypeStruct((TAIL, width), jnp.float32),
        scratch_shapes=[
            pltpu.VMEM((4, 2, width + TAIL, width), jnp.float32),
            pltpu.VMEM((5, TAIL, width), jnp.float32),
        ],
        name="solve_chain",
    )(place, both, *received, left, right, mid)


def shift(value, axis, step, wrap):
    size = lax.axis_size(axis)
    pairs = [(i, (i + step) % size) for i in range(size) if wrap or 0 <= i + step < size]
    return lax.ppermute(value, axis, pairs)


def swap_core(value):
    return lax.ppermute(value, "tm", [(i, i ^ 1) for i in range(lax.axis_size("tm"))])


def edge_rows(basis, model):
    width, rows, columns = basis.shape
    core = lax.axis_index("tm") & 1
    half = lax.dynamic_slice_in_dim(basis, core * (width // 2), width // 2, axis=0)
    half = jnp.concatenate([half, jnp.pad(model, ((0, TAIL - model.shape[0]), (0, 0), (0, 0)))], axis=0)
    low = shift(jnp.swapaxes(half[:, rows - REACH :], 0, 1), "tile", 1, False)
    high = shift(jnp.swapaxes(half[:, :REACH], 0, 1), "tile", -1, False)
    return low, swap_core(low), high, swap_core(high)


def obs_maps(cells, values, rows, columns):
    local = cells - lax.axis_index("tile") * (rows * columns)
    row = local // columns
    col = local & (columns - 1)
    strips = columns // LANES
    col = (col % strips) * LANES + col // strips
    by_row = (row[None, :] == jnp.arange(rows)[:, None]).astype(jnp.float32)
    by_col = (col[:, None] == jnp.arange(columns)[None, :]).astype(jnp.float32)
    both = jnp.concatenate([by_row, by_row * values[None, :]], axis=0)
    maps = jnp.dot(both, by_col, precision=lax.Precision.HIGHEST)
    return maps[:rows], maps[rows:]


def shards(basis, diffusion, drift_x, drift_y, land_sea, obs_cells, obs_values):
    width, rows, columns = basis.shape
    tiles = lax.axis_size("tile")
    group = lax.axis_index("tm")
    core = group & 1
    chip = group >> 1
    basis2 = basis.reshape(width * rows, columns)
    model = jnp.stack([diffusion[0], drift_x[0], drift_y[0], land_sea.astype(jnp.float32)])
    edges = edge_rows(basis, model)
    count, value = obs_maps(obs_cells[0], obs_values[0], rows, columns)
    field, obs = lay_basis(basis2, count, value, width, rows)
    place = jnp.stack([core, lax.axis_index("tile"), jnp.int32(tiles - 1)])
    partial = prop_terms(place, model, field, edges, obs, tiles)

    pieces = lax.all_to_all(partial, "tile", 0, 0, tiled=True)
    reduced = jnp.sum(pieces, axis=0)
    part = width // tiles
    lines = lax.broadcasted_iota(jnp.int32, reduced.shape, 0)
    scale = jnp.where(lines < part, 1.0 / float(tiles * rows * columns), 1.0 / float(NOBS))
    spread = jnp.broadcast_to((reduced * scale)[None], partial.shape)
    own = lax.all_to_all(spread, "tile", 0, 0, tiled=True)
    other = swap_core(own)

    both, send, left, right, mid = merge_pair(core[None], own, other)
    prev_mine = shift(send, "tm", 2, True)
    next_mine = shift(send, "tm", -2, True)
    size = lax.axis_size("tm")
    onward = [(i, (i + (2 if i % 2 == 0 else size - 2)) % size) for i in range(size)]
    far_mine = lax.ppermute(jnp.where(core == 0, prev_mine, next_mine), "tm", onward)
    received = []
    for mine in (prev_mine, next_mine, far_mine):
        received += [mine, swap_core(mine)]
    coeffs = solve_chain(jnp.stack([core, chip]), both, received, left, right, mid)
    group_coeffs = coeffs[:2][None]
    end_fields = jnp.sum(basis * coeffs[1][:, None, None], axis=0)[None]
    return (group_coeffs, end_fields)


def solution(mesh):
    in_specs = (
        P(None, "tile", None),
        P("tm", "tile", None),
        P("tm", "tile", None),
        P("tm", "tile", None),
        P("tile", None),
        P("tm", None),
        P("tm", None),
    )
    out_specs = (P("tm", None, None), P("tm", "tile", None))
    return jax.shard_map(shards, mesh=mesh, in_specs=in_specs, out_specs=out_specs, check_vma=False)
```

time: 810 us -> 196 us (0.24); the launches traced: 794 us -> 195 us
  other arithmetic: 392 us -> 7.59 us
  matrix products: 96.9 us -> 0.53 us
  Pallas kernels: 0 us -> 85.1 us
  waiting for transfers between devices: 110 us -> 43 us
  local copies, waits for them, and re-layouts: 67 us -> 14.1 us
  starting transfers between devices: 69.3 us -> 29.4 us
  blocking collectives: 36.8 us -> 14.9 us
  between operations: 22.2 us -> 0.84 us
    another operation x50 -> x3, other arithmetic: 285 us -> 1.33 us  [the longest x1 0.61 us: shards(): jnp.stack([core, chip])]
    mul x8 -> x2, other arithmetic: 99.6 us -> 0.08 us  [the longest x1 0.07 us: shards(): spread = jnp.broadcast_to((reduced * scale)[None], partial.shape)]
    pallas_call x0 -> x4, Pallas kernels: none -> 85.1 us  [the longest x1 33 us: prop_terms(): pl.pallas_call(prop_kernel, grid_spec=pltpu.PrefetchScalarGridSpec(num_sc...]
    dot_general x26 -> x1, matrix products: 68.9 us -> 0.53 us  [obs_maps(): maps = jnp.dot(both, by_col, precision=lax.Precision.HIGHEST)]
    ppermute x27 -> x11, starting transfers between devices: 69.3 us -> 18.7 us  [the longest x6 10.3 us: swap_core(): lax.ppermute(value, 'tm', [(i, i ^ 1) for i in range(lax.axis_size('tm'))])]
    psum x1 -> x0, waiting for transfers between devices: 49 us -> none  [shards(): lax.psum((local_prop, local_info, local_rhs), 'tile')]
    psum x1 -> x0, blocking collectives: 36.8 us -> none  [shards(): lax.psum((local_prop, local_info, local_rhs), 'tile')]
    ppermute x27 -> x11, waiting for transfers between devices: 60.5 us -> 30.6 us  [the longest x4 24.7 us: shift(): return lax.ppermute(value, axis, pairs)]
  transfers between devices with their start and end apart: 28 -> 12, of which waited for: 14 -> 7; matrix products, arithmetic and copies ran while one was open for 27% -> 2% of each run, Pallas kernels for 0% -> 10%
where the time goes in v1:
time: 196 us; the launch traced here: 195 us
  Pallas kernels  85.1 us (43%)
  waiting for transfers between devices  43 us (22%)
  starting transfers between devices  29.4 us (15%)
  blocking collectives  14.9 us (8%)
  local copies, waits for them, and re-layouts  14.1 us (7%)
  other arithmetic  7.59 us (4%)
    pallas_call x1, Pallas kernels, prop_terms(): pl.pallas_call(prop_kernel, grid_spec=pltpu.PrefetchScalarGridSpec(num_sc...  33 us
    pallas_call x1, Pallas kernels, solve_chain(): pl.pallas_call(chain_kernel, in_specs=[pl.BlockSpec(memory_space=pltpu.SM...  25.7 us
    ppermute x4, waiting for transfers between devices, shift(): return lax.ppermute(value, axis, pairs)  24.7 us
    pallas_call x1, Pallas kernels, lay_basis(): pl.pallas_call(functools.partial(lay_kernel, rows), grid=(width // block,...  18.6 us
    all_to_all x1, blocking collectives, shards(): own = lax.all_to_all(spread, 'tile', 0, 0, tiled=True)  14.9 us
    all_to_all x1, waiting for transfers between devices, shards(): pieces = lax.all_to_all(partial, 'tile', 0, 0, tiled=True)  12.4 us
    all_to_all x1, starting transfers between devices, shards(): pieces = lax.all_to_all(partial, 'tile', 0, 0, tiled=True)  10.7 us
    ppermute x6, starting transfers between devices, swap_core(): lax.ppermute(value, 'tm', [(i, i ^ 1) for i in range(lax.axis_size('tm'))])  10.3 us
  transfers between devices with their start and end apart: 12, of which 7 were waited for; matrix products, arithmetic and copies ran while one was open for 2% of the time, Pallas kernels for 10%

profile of v1, /device:TPU:1, one launch (start us, length us, event | category | flops | bytes accessed | tf_op | source)
XLA Modules:
  0.0 195.4 jit_solution(7672619849259161330)
XLA Ops:
  3.8 3.0 %constant_dynamic-slice_fusion = f32[128,16,512]{2,1,0:T(8,128)S(1)} fusion(f32[256,16,512]{2,1,0:T(8,128)} %param.7, s32[]{:T(128)S(6)} %select_n.44), kind=kLoop, calls=%fused_computation.36 | loop fusion | bytes 8388612 | tf_op jit(solution)/shard_map/dynamic_slice | solution.py:521
  6.9 2.4 %copy.14 = f32[128,16,512]{2,0,1:T(8,128)S(1)} copy(f32[128,16,512]{2,1,0:T(8,128)S(1)} %constant_dynamic-slice_fusion) | data formatting | bytes 8388608
  10.3 1.3 collective-permute-start.2
  11.6 4.7 %collective-permute-start = (f32[3,136,512]{2,1,0:T(8,128)S(1)}, f32[3,136,512]{2,1,0:T(8,128)S(1)}, u32[]{:S(2)}, u32[]{:S(2)}) collective-permute-start(f32[3,136,512]{2,1,0:T(8,128)S(1)} %get-tuple-element.17), channel_id=1, source_target_pairs={{0,1},{1,2},{2,3},{3,4},{4,5},{5,6},{6,7},{7,8},{8,9},{9,10},{10,1... | collective-permute-start | bytes 2506760 | tf_op jit(solution)/shard_map/ppermute | solution.py:511
  16.3 15.9 %collective-permute-done.2.high_mine = f32[3,136,512]{2,1,0:T(8,128)S(1)} collective-permute-done((f32[3,136,512]{2,1,0:T(8,128)S(1)}, f32[3,136,512]{2,1,0:T(8,128)S(1)}, u32[]{:S(2)}, u32[]{:S(2)}) %collective-permute-start.2) | collective-permute-done | bytes 835616 | tf_op jit(solution)/shard_map/ppermute | solution.py:511
  32.3 1.6 collective-permute-start.3
  33.9 1.2 collective-permute-start.1
  36.9 18.6 %lay_basis.1 = (f32[16,256,512]{2,1,0:T(8,128)}, f32[264,256]{1,0:T(8,128)}) custom-call(f32[16,512]{1,0:T(8,128)} %get-tuple-element.19.count_ref, f32[16,512]{1,0:T(8,128)} %get-tuple-element.18.value_ref, f32[4096,512]{1,0:T(8,128)} %bitcast.15, f32[4096,512]{1,0:T(8,128)} %bitcast.16, f32[4096,512]{1,0:T(8,128)} %bitcast.17, f32[4096,512]{1,0:T(8,128)} %bitcast.18), custom_call_target="tpu_custom_call" | custom-call | tf_op jit(solution)/shard_map/lay_basis/pallas_call | solution.py:117
  57.3 33.0 %prop_terms.1 = f32[16,40,256]{2,1,0:T(8,128)} custom-call(s32[3]{0:T(128)} %pad_add_fusion.1.place_ref, f32[4,16,512]{2,1,0:T(8,128)} %copy.13.model_ref, f32[16,256,512]{2,1,0:T(8,128)} %get-tuple-element.9.field_ref, f32[3,136,512]{2,1,0:T(8,128)} %copy-done.4, f32[3,136,512]{2,1,0:T(8,128)} %copy-done.6, f32[3,136,512]{2,1,0:T(8,128)} %copy-done.3, ...), custom_call_target="tpu_custom_call" | custom-call | tf_op jit(solution)/shard_map/prop_terms/pallas_call | solution.py:279
  90.3 10.7 %all-to-all-start = ((f32[16,40,256]{2,1,0:T(8,128)}), f32[16,40,256]{2,1,0:T(8,128)S(1)}, u32[]{:S(2)}, u32[]{:S(2)}) async-start(f32[16,40,256]{2,1,0:T(8,128)} %prop_terms.1), calls=%async_computation | async-start | bytes 1310720 | tf_op jit(solution)/shard_map/all_to_all | solution.py:555
  101.0 12.4 %all-to-all-done = f32[16,40,256]{2,1,0:T(8,128)S(1)} async-done(((f32[16,40,256]{2,1,0:T(8,128)}), f32[16,40,256]{2,1,0:T(8,128)S(1)}, u32[]{:S(2)}, u32[]{:S(2)}) %all-to-all-start) | async-done | bytes 655392 | tf_op jit(solution)/shard_map/all_to_all | solution.py:555
  113.6 14.9 %all_to_all.10.own_ref = f32[16,40,256]{2,1,0:T(8,128)S(1)} all-to-all(f32[16,40,256]{2,1,0:T(8,128)S(1)} %broadcast_in_dim.27), channel_id=1, replica_groups=mesh['tm'=8,'tile'=16] {'tile'}, dimensions={0} | all-to-all | bytes 1310720 | tf_op jit(solution)/shard_map/all_to_all | solution.py:561
  128.4 2.3 %collective-permute-start.4 = (f32[16,40,256]{2,1,0:T(8,128)S(1)}, f32[16,40,256]{2,1,0:T(8,128)S(1)}, u32[]{:S(2)}, u32[]{:S(2)}) collective-permute-start(f32[16,40,256]{2,1,0:T(8,128)S(1)} %all_to_all.10.own_ref), channel_id=1, source_target_pairs={{0,16},{16,0},{32,48},{48,32},{64,80},{80,64},{96,112},{112,96},{1... | collective-permute-start | bytes 1966088 | tf_op jit(solution)/shard_map/ppermute | solution.py:515
  130.7 1.7 collective-permute-done.4.other_ref
  133.3 7.7 %merge_pair.1 = (f32[2,264,256]{2,1,0:T(8,128)}, f32[264,256]{1,0:T(8,128)}, f32[256,256]{1,0:T(8,128)}, f32[256,256]{1,0:T(8,128)}, f32[8,256]{1,0:T(8,128)}) custom-call(s32[1]{0:T(128)} %bitcast.core_ref, f32[16,40,256]{2,1,0:T(8,128)} %copy-done, f32[16,40,256]{2,1,0:T(8,128)} %copy-done.7), custom_call_target="tpu_custom_call" | custom-call | tf_op jit(solution)/shard_map/merge_pair/pallas_call | solution.py:418
  141.0 2.1 %collective-permute-start.7 = (f32[264,256]{1,0:T(8,128)}, f32[264,256]{1,0:T(8,128)S(1)}, u32[]{:S(2)}, u32[]{:S(2)}) collective-permute-start(f32[264,256]{1,0:T(8,128)} %get-tuple-element.12), channel_id=1, source_target_pairs={{0,96},{16,112},{32,0},{48,16},{64,32},{80,48},{96,64},{112,80},{1... | collective-permute-start | bytes 811016 | tf_op jit(solution)/shard_map/ppermute | solution.py:511
  143.1 5.8 %collective-permute-done.7.m_next = f32[264,256]{1,0:T(8,128)S(1)} collective-permute-done((f32[264,256]{1,0:T(8,128)}, f32[264,256]{1,0:T(8,128)S(1)}, u32[]{:S(2)}, u32[]{:S(2)}) %collective-permute-start.7) | collective-permute-done | bytes 270368 | tf_op jit(solution)/shard_map/ppermute | solution.py:511
  148.9 3.0 %collective-permute-done.5.m_prev = f32[264,256]{1,0:T(8,128)S(1)} collective-permute-done((f32[264,256]{1,0:T(8,128)}, f32[264,256]{1,0:T(8,128)S(1)}, u32[]{:S(2)}, u32[]{:S(2)}) %collective-permute-start.5) | collective-permute-done | bytes 270368 | tf_op jit(solution)/shard_map/ppermute | solution.py:511
  152.3 1.3 collective-permute-start.8
  153.7 3.6 %collective-permute-done.9.m_far = f32[264,256]{1,0:T(8,128)S(1)} collective-permute-done((f32[264,256]{1,0:T(8,128)S(1)}, f32[264,256]{1,0:T(8,128)S(1)}, u32[]{:S(2)}, u32[]{:S(2)}) %collective-permute-start.9) | collective-permute-done | bytes 270368 | tf_op jit(solution)/shard_map/ppermute | solution.py:569
  157.3 3.9 %collective-permute-start.10 = (f32[264,256]{1,0:T(8,128)S(1)}, f32[264,256]{1,0:T(8,128)S(1)}, u32[]{:S(2)}, u32[]{:S(2)}) collective-permute-start(f32[264,256]{1,0:T(8,128)S(1)} %collective-permute-done.9.m_far), channel_id=1, source_target_pairs={{0,16},{16,0},{32,48},{48,32},{64,80},{80,64},{96,112},{112,96},{1... | collective-permute-start | bytes 811016 | tf_op jit(solution)/shard_map/ppermute | solution.py:515
  163.1 25.7 %solve_chain.1 = f32[8,256]{1,0:T(8,128)} custom-call(s32[2]{0:T(128)} %pad_add_fusion.place_ref, f32[2,264,256]{2,1,0:T(8,128)} %get-tuple-element.11.both_ref, f32[264,256]{1,0:T(8,128)} %copy-done.2, f32[264,256]{1,0:T(8,128)} %copy-done.10, f32[264,256]{1,0:T(8,128)} %copy-done.1, f32[264,256]{1,0:T(8,128)} %copy-done.9, f32[264,256]{1,0:T(8,128)} %copy-done.8, ...), custom_call_target="tpu_custom_call" | custom-call | tf_op jit(solution)/shard_map/solve_chain/pallas_call | solution.py:495
  189.5 1.3 slice_bitcast_fusion.2
  190.8 4.6 %multiply_reduce_fusion = f32[16,512]{1,0:T(8,128)} fusion(f32[256,16,512]{2,1,0:T(8,128)} %param.7, f32[256]{0:T(256)S(1)} %bitcast.23), kind=kLoop, calls=%fused_computation | loop fusion | flops 4186112 | bytes 8422400 | tf_op jit(solution)/shard_map/reduce_sum | solution.py:575
  (60 shorter events, 11.9 us)
Async XLA Ops:
  9.4 6.9 %copy-start.13 = (s32[1,512]{1,0:T(1,128)S(1)}, s32[1,512]{1,0:T(1,128)}, u32[]{:S(2)}) copy-start(s32[1,512]{1,0:T(1,128)} %param.12) | copy-start | bytes 6148
  9.4 26.3 %copy-start.12 = (f32[1,512]{1,0:T(1,128)S(1)}, f32[1,512]{1,0:T(1,128)}, u32[]{:S(2)}) copy-start(f32[1,512]{1,0:T(1,128)} %param.13) | copy-start | bytes 6148
  10.3 22.0 %collective-permute-start.2 = (f32[3,136,512]{2,1,0:T(8,128)S(1)}, f32[3,136,512]{2,1,0:T(8,128)S(1)}, u32[]{:S(2)}, u32[]{:S(2)}) collective-permute-start(f32[3,136,512]{2,1,0:T(8,128)S(1)} %get-tuple-element.16), channel_id=1, source_target_pairs={{1,0},{2,1},{3,2},{4,3},{5,4},{6,5},{7,6},{8,7},{9,8},{10,9},{11,1... | collective-permute-start | bytes 2506760 | tf_op jit(solution)/shard_map/ppermute | solution.py:511
  11.6 22.3 %collective-permute-start = (f32[3,136,512]{2,1,0:T(8,128)S(1)}, f32[3,136,512]{2,1,0:T(8,128)S(1)}, u32[]{:S(2)}, u32[]{:S(2)}) collective-permute-start(f32[3,136,512]{2,1,0:T(8,128)S(1)} %get-tuple-element.17), channel_id=1, source_target_pairs={{0,1},{1,2},{2,3},{3,4},{4,5},{5,6},{6,7},{7,8},{8,9},{9,10},{10,1... | collective-permute-start | bytes 2506760 | tf_op jit(solution)/shard_map/ppermute | solution.py:511
  32.3 23.3 %copy-start.3 = (f32[3,136,512]{2,1,0:T(8,128)}, f32[3,136,512]{2,1,0:T(8,128)S(1)}, u32[]{:S(2)}) copy-start(f32[3,136,512]{2,1,0:T(8,128)S(1)} %collective-permute-done.2.high_mine) | copy-start | bytes 2506756
  32.3 23.9 %collective-permute-start.3 = (f32[3,136,512]{2,1,0:T(8,128)S(1)}, f32[3,136,512]{2,1,0:T(8,128)S(1)}, u32[]{:S(2)}, u32[]{:S(2)}) collective-permute-start(f32[3,136,512]{2,1,0:T(8,128)S(1)} %collective-permute-done.2.high_mine), channel_id=1, source_target_pairs={{0,16},{16,0},{32,48},{48,32},{64,80},{80,64},{96,112},{112,96},{1... | collective-permute-start | bytes 2506760 | tf_op jit(solution)/shard_map/ppermute | solution.py:515
  33.9 21.7 %copy-start.4 = (f32[3,136,512]{2,1,0:T(8,128)}, f32[3,136,512]{2,1,0:T(8,128)S(1)}, u32[]{:S(2)}) copy-start(f32[3,136,512]{2,1,0:T(8,128)S(1)} %collective-permute-done.low_mine) | copy-start | bytes 2506756
  33.9 22.3 %collective-permute-start.1 = (f32[3,136,512]{2,1,0:T(8,128)S(1)}, f32[3,136,512]{2,1,0:T(8,128)S(1)}, u32[]{:S(2)}, u32[]{:S(2)}) collective-permute-start(f32[3,136,512]{2,1,0:T(8,128)S(1)} %collective-permute-done.low_mine), channel_id=1, source_target_pairs={{0,16},{16,0},{32,48},{48,32},{64,80},{80,64},{96,112},{112,96},{1... | collective-permute-start | bytes 2506760 | tf_op jit(solution)/shard_map/ppermute | solution.py:515
  56.1 0.9 copy-start.5
  56.2 1.1 copy-start.6
  90.3 23.1 %all-to-all-start = ((f32[16,40,256]{2,1,0:T(8,128)}), f32[16,40,256]{2,1,0:T(8,128)S(1)}, u32[]{:S(2)}, u32[]{:S(2)}) async-start(f32[16,40,256]{2,1,0:T(8,128)} %prop_terms.1), calls=%async_computation | async-start | bytes 1310720 | tf_op jit(solution)/shard_map/all_to_all | solution.py:555
  128.4 4.0 %copy-start = (f32[16,40,256]{2,1,0:T(8,128)}, f32[16,40,256]{2,1,0:T(8,128)S(1)}, u32[]{:S(2)}) copy-start(f32[16,40,256]{2,1,0:T(8,128)S(1)} %all_to_all.10.own_ref) | copy-start | bytes 1966084
  128.4 4.0 %collective-permute-start.4 = (f32[16,40,256]{2,1,0:T(8,128)S(1)}, f32[16,40,256]{2,1,0:T(8,128)S(1)}, u32[]{:S(2)}, u32[]{:S(2)}) collective-permute-start(f32[16,40,256]{2,1,0:T(8,128)S(1)} %all_to_all.10.own_ref), channel_id=1, source_target_pairs={{0,16},{16,0},{32,48},{48,32},{64,80},{80,64},{96,112},{112,96},{1... | collective-permute-start | bytes 1966088 | tf_op jit(solution)/shard_map/ppermute | solution.py:515
  132.5 0.9 copy-start.7
  141.0 7.9 %collective-permute-start.7 = (f32[264,256]{1,0:T(8,128)}, f32[264,256]{1,0:T(8,128)S(1)}, u32[]{:S(2)}, u32[]{:S(2)}) collective-permute-start(f32[264,256]{1,0:T(8,128)} %get-tuple-element.12), channel_id=1, source_target_pairs={{0,96},{16,112},{32,0},{48,16},{64,32},{80,48},{96,64},{112,80},{1... | collective-permute-start | bytes 811016 | tf_op jit(solution)/shard_map/ppermute | solution.py:511
  143.1 8.8 %collective-permute-start.5 = (f32[264,256]{1,0:T(8,128)}, f32[264,256]{1,0:T(8,128)S(1)}, u32[]{:S(2)}, u32[]{:S(2)}) collective-permute-start(f32[264,256]{1,0:T(8,128)} %get-tuple-element.12), channel_id=1, source_target_pairs={{0,32},{16,48},{32,64},{48,80},{64,96},{80,112},{96,0},{112,16},{1... | collective-permute-start | bytes 811016 | tf_op jit(solution)/shard_map/ppermute | solution.py:511
  148.9 13.5 %copy-start.1 = (f32[264,256]{1,0:T(8,128)}, f32[264,256]{1,0:T(8,128)S(1)}, u32[]{:S(2)}) copy-start(f32[264,256]{1,0:T(8,128)S(1)} %collective-permute-done.7.m_next) | copy-start | bytes 811012
  151.9 10.5 %copy-start.2 = (f32[264,256]{1,0:T(8,128)}, f32[264,256]{1,0:T(8,128)S(1)}, u32[]{:S(2)}) copy-start(f32[264,256]{1,0:T(8,128)S(1)} %collective-permute-done.5.m_prev) | copy-start | bytes 811012
  152.0 5.4 %collective-permute-start.9 = (f32[264,256]{1,0:T(8,128)S(1)}, f32[264,256]{1,0:T(8,128)S(1)}, u32[]{:S(2)}, u32[]{:S(2)}) collective-permute-start(f32[264,256]{1,0:T(8,128)S(1)} %broadcast_select_fusion), channel_id=1, source_target_pairs={{0,32},{16,112},{32,64},{48,16},{64,96},{80,48},{96,0},{112,80},{1... | collective-permute-start | bytes 811016 | tf_op jit(solution)/shard_map/ppermute | solution.py:569
  152.3 9.5 %collective-permute-start.8 = (f32[264,256]{1,0:T(8,128)S(1)}, f32[264,256]{1,0:T(8,128)S(1)}, u32[]{:S(2)}, u32[]{:S(2)}) collective-permute-start(f32[264,256]{1,0:T(8,128)S(1)} %collective-permute-done.7.m_next), channel_id=1, source_target_pairs={{0,16},{16,0},{32,48},{48,32},{64,80},{80,64},{96,112},{112,96},{1... | collective-permute-start | bytes 811016 | tf_op jit(solution)/shard_map/ppermute | solution.py:515
  153.6 8.2 %collective-permute-start.6 = (f32[264,256]{1,0:T(8,128)S(1)}, f32[264,256]{1,0:T(8,128)S(1)}, u32[]{:S(2)}, u32[]{:S(2)}) collective-permute-start(f32[264,256]{1,0:T(8,128)S(1)} %collective-permute-done.5.m_prev), channel_id=1, source_target_pairs={{0,16},{16,0},{32,48},{48,32},{64,80},{80,64},{96,112},{112,96},{1... | collective-permute-start | bytes 811016 | tf_op jit(solution)/shard_map/ppermute | solution.py:515
  157.3 5.1 %copy-start.8 = (f32[264,256]{1,0:T(8,128)}, f32[264,256]{1,0:T(8,128)S(1)}, u32[]{:S(2)}) copy-start(f32[264,256]{1,0:T(8,128)S(1)} %collective-permute-done.9.m_far) | copy-start | bytes 811012
  157.3 5.0 %collective-permute-start.10 = (f32[264,256]{1,0:T(8,128)S(1)}, f32[264,256]{1,0:T(8,128)S(1)}, u32[]{:S(2)}, u32[]{:S(2)}) collective-permute-start(f32[264,256]{1,0:T(8,128)S(1)} %collective-permute-done.9.m_far), channel_id=1, source_target_pairs={{0,16},{16,0},{32,48},{48,32},{64,80},{80,64},{96,112},{112,96},{1... | collective-permute-start | bytes 811016 | tf_op jit(solution)/shard_map/ppermute | solution.py:515
  161.8 0.8 copy-start.10
  (2 other events, 1.4 us)

commit v2 on v1

--- a/solution.py
+++ b/solution.py
@@ -14,7 +14,6 @@
 RIDGE = 0.1
 SUB = 8
 LANES = 128
-SLICE = 40
 TAIL = 8
 
 
@@ -35,12 +34,13 @@
     )
 
 
-def full(left, right, contract=(1, 0)):
+def dot(left, right, contract=(1, 0)):
+    lh, ll = split(left)
+    rh, rl = split(right)
     return lax.dot_general(
-        left,
-        right,
+        jnp.concatenate([lh, lh, ll], axis=contract[0]),
+        jnp.concatenate([rh, rl, rh], axis=contract[1]),
         (((contract[0],), (contract[1],)), ((), ())),
-        precision=lax.Precision.HIGHEST,
         preferred_element_type=jnp.float32,
     )
 
@@ -73,6 +73,63 @@
 
 def before(strips):
     return [pltpu.roll(strips[-1], 1, 1)] + strips[:-1]
+
+
+def edge_kernel(rows, core_ref, *refs):
+    model_refs, basis_refs, (low_ref, high_ref, model_ref) = refs[:4], refs[4:-3], refs[-3:]
+    step_id = pl.program_id(0)
+    block = basis_refs[0].shape[0] // rows
+    half = low_ref.shape[1] - TAIL
+
+    @pl.when(step_id == 0)
+    def _():
+        for f, ref in enumerate(model_refs):
+            model_ref[f] = ref[0].astype(jnp.float32)
+        for r in range(REACH):
+            low_ref[r, half:, :] = jnp.zeros_like(low_ref[r, half:, :])
+            high_ref[r, half:, :] = jnp.zeros_like(high_ref[r, half:, :])
+            for f in range(4):
+                at = rows - REACH + r
+                low_ref[r, half + f : half + f + 1, :] = model_ref[f, at : at + 1, :]
+                high_ref[r, half + f : half + f + 1, :] = model_ref[f, r : r + 1, :]
+
+    store = pl.ds(pl.multiple_of(step_id * block, block), block)
+    for r in range(REACH):
+        for out, i in ((low_ref, rows - REACH + r), (high_ref, r)):
+            span = pl.ds(i, block, stride=rows)
+            out[r, store, :] = jnp.concatenate([ref[span, :] for ref in basis_refs], axis=1)
+
+
+def edge_terms(core, models, basis2, width, rows):
+    columns = basis2.shape[1]
+    block = 32
+    strips = columns // LANES
+    steps = width // 2 // block
+    own = pl.BlockSpec((1, rows, columns), lambda k, core: (0, 0, 0))
+    edge = (REACH, width // 2 + TAIL, columns)
+    return pl.pallas_call(
+        functools.partial(edge_kernel, rows),
+        grid_spec=pltpu.PrefetchScalarGridSpec(
+            num_scalar_prefetch=1,
+            grid=(steps,),
+            in_specs=[own] * 4
+            + [
+                pl.BlockSpec((block * rows, LANES), lambda k, core, c=c: (k + core[0] * steps, c))
+                for c in range(strips)
+            ],
+            out_specs=[
+                pl.BlockSpec(edge, lambda k, core: (0, 0, 0)),
+                pl.BlockSpec(edge, lambda k, core: (0, 0, 0)),
+                pl.BlockSpec((4, rows, columns), lambda k, core: (0, 0, 0)),
+            ],
+        ),
+        out_shape=[
+            jax.ShapeDtypeStruct(edge, jnp.float32),
+            jax.ShapeDtypeStruct(edge, jnp.float32),
+            jax.ShapeDtypeStruct((4, rows, columns), jnp.float32),
+        ],
+        name="edge_terms",
+    )(core, *models, *[basis2] * strips)
 
 
 def lay_kernel(rows, count_ref, value_ref, *refs):
@@ -99,18 +156,23 @@
     @pl.when(step_id == pl.num_programs(0) - 1)
     def _():
         out_ref[...] = jnp.zeros_like(out_ref)
+        tiles = out_ref.shape[0]
+        part = width // tiles
 
         def body(i, carry):
             field = held[i]
             count = count_ref[pl.ds(i, 1), :]
             value = jnp.broadcast_to(value_ref[pl.ds(i, 1), :], (TAIL, count.shape[1]))
-            out_ref[...] += dot3(jnp.concatenate([field * count, value], axis=0), field)
+            terms = dot3(jnp.concatenate([field * count, value], axis=0), field)
+            for t in range(tiles):
+                out_ref[t, :part, :] += terms[t * part : (t + 1) * part]
+            out_ref[0, part:, :] += terms[width:]
             return carry
 
         lax.fori_loop(0, rows, body, 0)
 
 
-def lay_basis(basis2, count, value, width, rows):
+def lay_basis(basis2, count, value, width, rows, tiles):
     columns = basis2.shape[1]
     block = 32
     strips = columns // LANES
@@ -124,22 +186,23 @@
         ],
         out_specs=[
             pl.BlockSpec((rows, block, columns), lambda k: (0, k, 0)),
-            pl.BlockSpec((width + TAIL, width), lambda k: (0, 0)),
+            pl.BlockSpec((tiles, width // tiles + TAIL, width), lambda k: (0, 0, 0)),
         ],
         out_shape=[
             jax.ShapeDtypeStruct((rows, width, columns), jnp.float32),
-            jax.ShapeDtypeStruct((width + TAIL, width), jnp.float32),
+            jax.ShapeDtypeStruct((tiles, width // tiles + TAIL, width), jnp.float32),
         ],
         scratch_shapes=[
             pltpu.VMEM((2 * columns, columns), jnp.bfloat16),
             pltpu.VMEM((rows, width, columns), jnp.float32),
         ],
+        cost_estimate=pl.CostEstimate(flops=20 * 10**9, bytes_accessed=17 * 10**6, transcendentals=0),
         name="lay_basis",
     )(count, value, *[basis2] * strips)
 
 
 def prop_kernel(
-    place_ref, model_ref, field_ref, low_mine, low_theirs, high_mine, high_theirs, obs_ref,
+    place_ref, model_ref, field_ref, low_mine, low_theirs, high_mine, high_theirs,
     out_ref, deal, model, wide, edges, fore, back,
 ):
     step_id = pl.program_id(0)
@@ -253,24 +316,16 @@
 
     @pl.when(step_id == steps - 1)
     def _():
-        count = out_ref.shape[0]
-        part = width // count
+        out_ref[...] = jnp.zeros_like(out_ref)
 
         def body(i, carry):
-            product = dot3(back[i], fore[i])
-            fresh = i == 0
-            for t in range(count):
-                piece = product[t * part : (t + 1) * part]
-                out_ref[t, :part, :] = jnp.where(fresh, 0.0, out_ref[t, :part, :]) + piece
+            out_ref[...] += dot3(back[i], fore[i])
             return carry
 
         lax.fori_loop(0, rows, body, 0)
-        for t in range(count):
-            out_ref[t, part : 2 * part, :] = obs_ref[t * part : (t + 1) * part, :]
-            out_ref[t, 2 * part :, :] = obs_ref[width : width + SLICE - 2 * part, :]
-
-
-def prop_terms(place, model, field, edges, obs, count):
+
+
+def prop_terms(place, model, field, edges):
     rows, width, columns = field.shape
     block = 32
     steps = width // block
@@ -291,9 +346,8 @@
                 vmem,
                 vmem,
                 vmem,
-                vmem,
             ],
-            out_specs=pl.BlockSpec((count, SLICE, width), lambda k, place: (0, 0, 0)),
+            out_specs=pl.BlockSpec((width, width), lambda k, place: (0, 0)),
             scratch_shapes=[
                 pltpu.VMEM((3 * columns, columns), jnp.bfloat16),
                 pltpu.VMEM((4, -(-ext // SUB) * SUB, columns), jnp.float32),
@@ -303,9 +357,10 @@
                 pltpu.VMEM((rows, width, columns), jnp.float32),
             ],
         ),
-        out_shape=jax.ShapeDtypeStruct((count, SLICE, width), jnp.float32),
+        out_shape=jax.ShapeDtypeStruct((width, width), jnp.float32),
+        cost_estimate=pl.CostEstimate(flops=35 * 10**9, bytes_accessed=12 * 10**6, transcendentals=0),
         name="prop_terms",
-    )(place, model, field, *edges, obs)
+    )(place, model, field, *edges)
 
 
 def eye_mask(width):
@@ -322,14 +377,10 @@
             preferred_element_type=jnp.float32,
         )
     if passes == 3:
-        lh, ll = split(left)
-        rh, rl = split(right)
-        return jnp.dot(
-            jnp.concatenate([lh, lh, ll], axis=1),
-            jnp.concatenate([rh, rl, rh], axis=0),
-            preferred_element_type=jnp.float32,
-        )
-    return full(left, right)
+        return dot(left, right)
+    return jnp.dot(
+        left, right, precision=lax.Precision.HIGHEST, preferred_element_type=jnp.float32
+    )
 
 
 def inverses(mats):
@@ -367,33 +418,34 @@
     return found
 
 
-def pair_kernel(core_ref, own_ref, other_ref, both_ref, send_ref, left_ref, right_ref, mid_ref, prop, info):
-    count, _, width = own_ref.shape
-    part = width // count
+def pair_kernel(
+    core_ref, p_own, p_other, s_own, s_other, both_ref, send_ref, left_ref, right_ref, mid_ref
+):
+    tiles, _, width = s_own.shape
+    part = width // tiles
     first = core_ref[0] == 0
     row, col = eye_mask(width)
     identity = jnp.where(row == col, 1.0, 0.0).astype(jnp.float32)
-    for t in range(count):
-        span = pl.ds(t * part, part)
-        for slot, lead in ((0, True), (1, False)):
-            mine, theirs = own_ref[t], other_ref[t]
-            chosen = jnp.where(first, mine, theirs) if lead else jnp.where(first, theirs, mine)
-            prop[slot, span, :] = chosen[:part]
-            info[slot, span, :] = chosen[part : 2 * part]
-    rhs_own, rhs_other = own_ref[0, 2 * part :, :], other_ref[0, 2 * part :, :]
-    rhs_left = jnp.where(first, rhs_own, rhs_other)
-    rhs_right = jnp.where(first, rhs_other, rhs_own)
-    p_left, p_right = prop[0], prop[1]
-    square_left = full(p_left, p_left, (0, 0))
-    square_right = full(p_right, p_right, (0, 0))
+
+    def ordered(own, other):
+        return jnp.where(first, own, other), jnp.where(first, other, own)
+
+    p_left, p_right = ordered(p_own[...], p_other[...])
+    info = ordered(
+        jnp.concatenate([s_own[t, :part, :] for t in range(tiles)], axis=0),
+        jnp.concatenate([s_other[t, :part, :] for t in range(tiles)], axis=0),
+    )
+    rhs_left, rhs_right = ordered(s_own[0, part:, :], s_other[0, part:, :])
+    square_left = dot(p_left, p_left, (0, 0))
+    square_right = dot(p_right, p_right, (0, 0))
     middle = (Q + 2 * RIDGE) * identity + info[0] + Q * square_right
     (back,) = inverses([middle])
-    toward_left = full(p_left, back, (0, 0))
-    toward_right = full(jnp.concatenate([p_right, rhs_left], axis=0), back)
+    toward_left = dot(p_left, back, (0, 0))
+    toward_right = dot(jnp.concatenate([p_right, rhs_left], axis=0), back)
     mid = toward_right[width:]
     toward_right = toward_right[:width]
-    by_left = full(jnp.concatenate([toward_left, mid], axis=0), p_left)
-    by_right = full(jnp.concatenate([toward_left, toward_right, mid], axis=0), p_right, (1, 1))
+    by_left = dot(jnp.concatenate([toward_left, mid], axis=0), p_left)
+    by_right = dot(jnp.concatenate([toward_left, toward_right, mid], axis=0), p_right, (1, 1))
     upper = Q * square_left + RIDGE * identity - (Q * Q) * by_left[:width]
     cross = -(Q * Q) * by_right[:width]
     lower = (Q + RIDGE) * identity + info[1] - (Q * Q) * by_right[width : 2 * width]
@@ -411,13 +463,13 @@
     mid_ref[...] = mid
 
 
-def merge_pair(core, own, other):
-    count, _, width = own.shape
+def merge_pair(core, *terms):
+    width = terms[0].shape[1]
     vmem = pl.BlockSpec(memory_space=pltpu.VMEM)
     block = jax.ShapeDtypeStruct((width, width), jnp.float32)
     return pl.pallas_call(
         pair_kernel,
-        in_specs=[pl.BlockSpec(memory_space=pltpu.SMEM), vmem, vmem],
+        in_specs=[pl.BlockSpec(memory_space=pltpu.SMEM)] + [vmem] * 4,
         out_specs=[vmem] * 5,
         out_shape=[
             jax.ShapeDtypeStruct((2, width + TAIL, width), jnp.float32),
@@ -426,15 +478,16 @@
             block,
             jax.ShapeDtypeStruct((TAIL, width), jnp.float32),
         ],
-        scratch_shapes=[pltpu.VMEM((2, width, width), jnp.float32)] * 2,
         name="merge_pair",
-    )(core, own, other)
+    )(core, *terms)
 
 
 def chain_kernel(
     place_ref, both_ref, m_prev, o_prev, m_next, o_next, m_far, o_far, left_ref, right_ref, mid_ref,
-    coeff_ref, blocks, states,
+    basis_ref, coeff_ref, end_ref, blocks, states, basis, weight, sem,
 ):
+    fetch = pltpu.make_async_copy(basis_ref, basis, sem)
+    fetch.start()
     core, chip = place_ref[0], place_ref[1]
     width = both_ref.shape[2]
     row, col = eye_mask(width)
@@ -457,52 +510,71 @@
     diag = [upper[0], lower[0] + upper[1], lower[1] + upper[2], lower[2] + upper[3], lower[3]]
     rhs = [head[0], tail[0] + head[1], tail[1] + head[2], tail[2] + head[3], tail[3]]
     inv0, inv2, inv4 = inverses([diag[0], diag[2], diag[4]])
-    t10 = full(cross[0], inv0, (0, 0))
-    t12 = full(cross[1], inv2)
-    t32 = full(cross[2], inv2, (0, 0))
-    t34 = full(cross[3], inv4)
-    z0, z2, z4 = full(rhs[0], inv0), full(rhs[2], inv2), full(rhs[4], inv4)
-    diag1 = diag[1] - full(t10, cross[0]) - full(t12, cross[1], (1, 1))
-    diag3 = diag[3] - full(t32, cross[2]) - full(t34, cross[3], (1, 1))
-    link = -full(t12, cross[2])
-    rhs1 = rhs[1] - full(z0, cross[0]) - full(z2, cross[1], (1, 1))
-    rhs3 = rhs[3] - full(z2, cross[2]) - full(z4, cross[3], (1, 1))
+    t10 = dot(cross[0], inv0, (0, 0))
+    t12 = dot(cross[1], inv2)
+    t32 = dot(cross[2], inv2, (0, 0))
+    t34 = dot(cross[3], inv4)
+    z0, z2, z4 = dot(rhs[0], inv0), dot(rhs[2], inv2), dot(rhs[4], inv4)
+    diag1 = diag[1] - dot(t10, cross[0]) - dot(t12, cross[1], (1, 1))
+    diag3 = diag[3] - dot(t32, cross[2]) - dot(t34, cross[3], (1, 1))
+    link = -dot(t12, cross[2])
+    rhs1 = rhs[1] - dot(z0, cross[0]) - dot(z2, cross[1], (1, 1))
+    rhs3 = rhs[3] - dot(z2, cross[2]) - dot(z4, cross[3], (1, 1))
     (inv1,) = inverses([diag1])
-    t31 = full(link, inv1, (0, 0))
-    z1 = full(rhs1, inv1)
-    diag3 = diag3 - full(t31, link)
-    rhs3 = rhs3 - full(z1, link)
+    t31 = dot(link, inv1, (0, 0))
+    z1 = dot(rhs1, inv1)
+    diag3 = diag3 - dot(t31, link)
+    rhs3 = rhs3 - dot(z1, link)
     (inv3,) = inverses([diag3])
-    y3 = full(rhs3, inv3)
-    y1 = z1 - full(y3, t31)
-    y0 = z0 - full(y1, t10)
-    y2 = z2 - full(y1, t12) - full(y3, t32)
-    y4 = z4 - full(y3, t34)
+    y3 = dot(rhs3, inv3)
+    y1 = z1 - dot(y3, t31)
+    y0 = z0 - dot(y1, t10)
+    y2 = z2 - dot(y1, t12) - dot(y3, t32)
+    y4 = z4 - dot(y3, t34)
     for c, state in enumerate((y0, y1, y2, y3, y4)):
         states[c] = state
     begin, finish = states[chip], states[chip + 1]
-    inner = mid_ref[...] + full(begin, left_ref[...]) + full(finish, right_ref[...])
+    inner = mid_ref[...] + dot(begin, left_ref[...]) + dot(finish, right_ref[...])
     first = core == 0
     start = jnp.where(first, begin, inner)
     end = jnp.where(first, inner, finish)
-    pick = lax.broadcasted_iota(jnp.int32, (TAIL, width), 0)
-    coeff_ref[...] = jnp.where(pick == 0, start, end)
-
-
-def solve_chain(place, both, received, left, right, mid):
+    coeff_ref[0, 0:1, :] = start[0:1]
+    coeff_ref[0, 1:2, :] = end[0:1]
+    weight[...] = jnp.concatenate([end] * (LANES // TAIL), axis=0).T
+    rows, columns = end_ref.shape[1:]
+    fetch.wait()
+
+    def add(k, total):
+        line = basis[pl.ds(pl.multiple_of(k * rows, rows), rows), :]
+        factor = jnp.broadcast_to(weight[pl.ds(k, 1), :], (rows, LANES))
+        return total + line * jnp.concatenate([factor] * (columns // LANES), axis=1)
+
+    end_ref[0] = lax.fori_loop(0, width, add, jnp.zeros((rows, columns), jnp.float32), unroll=8)
+
+
+def solve_chain(place, both, received, left, right, mid, basis2, rows):
     width = both.shape[2]
+    columns = basis2.shape[1]
     vmem = pl.BlockSpec(memory_space=pltpu.VMEM)
     return pl.pallas_call(
         chain_kernel,
-        in_specs=[pl.BlockSpec(memory_space=pltpu.SMEM)] + [vmem] * 10,
-        out_specs=vmem,
-        out_shape=jax.ShapeDtypeStruct((TAIL, width), jnp.float32),
+        in_specs=[pl.BlockSpec(memory_space=pltpu.SMEM)]
+        + [vmem] * 10
+        + [pl.BlockSpec(memory_space=pltpu.HBM)],
+        out_specs=[vmem, vmem],
+        out_shape=[
+            jax.ShapeDtypeStruct((1, 2, width), jnp.float32),
+            jax.ShapeDtypeStruct((1, rows, columns), jnp.float32),
+        ],
         scratch_shapes=[
             pltpu.VMEM((4, 2, width + TAIL, width), jnp.float32),
             pltpu.VMEM((5, TAIL, width), jnp.float32),
+            pltpu.VMEM(basis2.shape, jnp.float32),
+            pltpu.VMEM((width, LANES), jnp.float32),
+            pltpu.SemaphoreType.DMA,
         ],
         name="solve_chain",
-    )(place, both, *received, left, right, mid)
+    )(place, both, *received, left, right, mid, basis2)
 
 
 def shift(value, axis, step, wrap):
@@ -515,14 +587,10 @@
     return lax.ppermute(value, "tm", [(i, i ^ 1) for i in range(lax.axis_size("tm"))])
 
 
-def edge_rows(basis, model):
-    width, rows, columns = basis.shape
-    core = lax.axis_index("tm") & 1
-    half = lax.dynamic_slice_in_dim(basis, core * (width // 2), width // 2, axis=0)
-    half = jnp.concatenate([half, jnp.pad(model, ((0, TAIL - model.shape[0]), (0, 0), (0, 0)))], axis=0)
-    low = shift(jnp.swapaxes(half[:, rows - REACH :], 0, 1), "tile", 1, False)
-    high = shift(jnp.swapaxes(half[:, :REACH], 0, 1), "tile", -1, False)
-    return low, swap_core(low), high, swap_core(high)
+def tile_sum(pieces, scale):
+    slices = lax.all_to_all(pieces, "tile", 0, 0, tiled=True)
+    mine = jnp.sum(slices, axis=0) * scale
+    return lax.all_to_all(jnp.broadcast_to(mine[None], pieces.shape), "tile", 0, 0, tiled=True)
 
 
 def obs_maps(cells, values, rows, columns):
@@ -545,23 +613,22 @@
     core = group & 1
     chip = group >> 1
     basis2 = basis.reshape(width * rows, columns)
-    model = jnp.stack([diffusion[0], drift_x[0], drift_y[0], land_sea.astype(jnp.float32)])
-    edges = edge_rows(basis, model)
+    models = (diffusion, drift_x, drift_y, land_sea[None])
+    low_send, high_send, model = edge_terms(core[None], models, basis2, width, rows)
+    low = shift(low_send, "tile", 1, False)
+    high = shift(high_send, "tile", -1, False)
+    edges = (low, swap_core(low), high, swap_core(high))
     count, value = obs_maps(obs_cells[0], obs_values[0], rows, columns)
-    field, obs = lay_basis(basis2, count, value, width, rows)
+    field, obs = lay_basis(basis2, count, value, width, rows, tiles)
     place = jnp.stack([core, lax.axis_index("tile"), jnp.int32(tiles - 1)])
-    partial = prop_terms(place, model, field, edges, obs, tiles)
-
-    pieces = lax.all_to_all(partial, "tile", 0, 0, tiled=True)
-    reduced = jnp.sum(pieces, axis=0)
-    part = width // tiles
-    lines = lax.broadcasted_iota(jnp.int32, reduced.shape, 0)
-    scale = jnp.where(lines < part, 1.0 / float(tiles * rows * columns), 1.0 / float(NOBS))
-    spread = jnp.broadcast_to((reduced * scale)[None], partial.shape)
-    own = lax.all_to_all(spread, "tile", 0, 0, tiled=True)
-    other = swap_core(own)
-
-    both, send, left, right, mid = merge_pair(core[None], own, other)
+    s_own = tile_sum(obs, 1.0 / float(NOBS))
+    s_other = swap_core(s_own)
+    prop = prop_terms(place, model, field, edges)
+    cells = float(tiles * rows * columns)
+    p_own = tile_sum(prop.reshape(tiles, width // tiles, width), 1.0 / cells).reshape(width, width)
+    p_other = swap_core(p_own)
+
+    both, send, left, right, mid = merge_pair(core[None], p_own, p_other, s_own, s_other)
     prev_mine = shift(send, "tm", 2, True)
     next_mine = shift(send, "tm", -2, True)
     size = lax.axis_size("tm")
@@ -570,10 +637,8 @@
     received = []
     for mine in (prev_mine, next_mine, far_mine):
         received += [mine, swap_core(mine)]
-    coeffs = solve_chain(jnp.stack([core, chip]), both, received, left, right, mid)
-    group_coeffs = coeffs[:2][None]
-    end_fields = jnp.sum(basis * coeffs[1][:, None, None], axis=0)[None]
-    return (group_coeffs, end_fields)
+    place = jnp.stack([core, chip])
+    return tuple(solve_chain(place, both, received, left, right, mid, basis2, rows))
 
 
 def solution(mesh):

time: 196 us -> 191 us (0.974)
  starting transfers between devices: 29.4 us -> 48.2 us
  blocking collectives: 14.9 us -> 0 us
  local copies, waits for them, and re-layouts: 14.1 us -> 4.5 us
  other arithmetic: 7.59 us -> 1.31 us
  waiting for transfers between devices: 43 us -> 48.2 us
    all_to_all x1 -> x0, blocking collectives: 14.9 us -> none  [shards(): own = lax.all_to_all(spread, 'tile', 0, 0, tiled=True)]
    all_to_all x1 -> x4, starting transfers between devices: 10.7 us -> 23 us  [the longest x2 15.9 us: tile_sum(): slices = lax.all_to_all(pieces, 'tile', 0, 0, tiled=True)]
    all_to_all x1 -> x4, waiting for transfers between devices: 12.4 us -> 19.9 us  [the longest x2 12.4 us: tile_sum(): lax.all_to_all(jnp.broadcast_to(mine[None], pieces.shape), 'tile', 0, 0,...]
    unnamed x32 -> x30, local copies, waits for them, and re-layouts: 7.55 us -> 2.31 us
    reduce_sum x2, other arithmetic: 4.65 us -> 0.05 us  [tile_sum(): mine = jnp.sum(slices, axis=0) * scale]
    ppermute x6 -> x7, starting transfers between devices: 10.3 us -> 14.8 us  [swap_core(): lax.ppermute(value, 'tm', [(i, i ^ 1) for i in range(lax.axis_size('tm'))])]
    pallas_call x0 -> x1, Pallas kernels: none -> 4.47 us  [edge_terms(): pl.pallas_call(functools.partial(edge_kernel, rows), grid_spec=pltpu.Pref...]
    dynamic_slice x1 -> x0, local copies, waits for them, and re-layouts: 3.02 us -> none  [edge_rows(): lax.dynamic_slice_in_dim(basis, core * (width // 2), width // 2, axis=0)]
  transfers between devices with their start and end apart: 12 -> 16, of which waited for: 7 -> 9; matrix products, arithmetic and copies ran while one was open for 2% -> 1% of each run, Pallas kernels for 10% -> 27%
where the time goes in v2:
time: 191 us; the launch traced here: 190 us
  Pallas kernels  86.5 us (45%)
  starting transfers between devices  48.2 us (25%)
  waiting for transfers between devices  48.2 us (25%)
  local copies, waits for them, and re-layouts  4.5 us (2%)
    pallas_call x1, Pallas kernels, prop_terms(): pl.pallas_call(prop_kernel, grid_spec=pltpu.PrefetchScalarGridSpec(num_sc...  32.9 us
    pallas_call x1, Pallas kernels, solve_chain(): pl.pallas_call(chain_kernel, in_specs=[pl.BlockSpec(memory_space=pltpu.SM...  23.8 us
    ppermute x4, waiting for transfers between devices, shift(): return lax.ppermute(value, axis, pairs)  23.6 us
    pallas_call x1, Pallas kernels, lay_basis(): pl.pallas_call(functools.partial(lay_kernel, rows), grid=(width // block,...  18.6 us
    all_to_all x2, starting transfers between devices, tile_sum(): slices = lax.all_to_all(pieces, 'tile', 0, 0, tiled=True)  15.9 us
    ppermute x7, starting transfers between devices, swap_core(): lax.ppermute(value, 'tm', [(i, i ^ 1) for i in range(lax.axis_size('tm'))])  14.8 us
    all_to_all x2, waiting for transfers between devices, tile_sum(): lax.all_to_all(jnp.broadcast_to(mine[None], pieces.shape), 'tile', 0, 0,...  12.4 us
    ppermute x4, starting transfers between devices, shift(): return lax.ppermute(value, axis, pairs)  8.03 us
  transfers between devices with their start and end apart: 16, of which 9 were waited for; matrix products, arithmetic and copies ran while one was open for 1% of the time, Pallas kernels for 27%

profile of v2, /device:TPU:1, one launch (start us, length us, event | category | flops | bytes accessed | tf_op | source)
XLA Modules:
  0.0 190.3 jit_solution(3063692667071913369)
XLA Ops:
  0.7 4.5 %edge_terms.1 = (f32[3,136,512]{2,1,0:T(8,128)}, f32[3,136,512]{2,1,0:T(8,128)}, f32[4,16,512]{2,1,0:T(8,128)}) custom-call(s32[1]{0:T(128)} %bitcast.core_ref, f32[1,16,512]{2,1,0:T(8,128)} %refs_0_.1, f32[1,16,512]{2,1,0:T(8,128)} %refs_1_.1, f32[1,16,512]{2,1,0:T(8,128)} %refs_2_.1, s32[1,16,512]{2,1,0:T(8,128)} %bitcast.22, f32[4096,512]{1,0:T(8,128)} %bitcast.10, ...), custom_call_target="tpu_custom_call" | custom-call | tf_op jit(solution)/shard_map/edge_terms/pallas_call | solution.py:110
  5.1 4.1 %collective-permute-start = (f32[3,136,512]{2,1,0:T(8,128)}, f32[3,136,512]{2,1,0:T(8,128)S(1)}, u32[]{:S(2)}, u32[]{:S(2)}) collective-permute-start(f32[3,136,512]{2,1,0:T(8,128)} %get-tuple-element.14), channel_id=1, source_target_pairs={{0,1},{1,2},{2,3},{3,4},{4,5},{5,6},{6,7},{7,8},{8,9},{9,10},{10,1... | collective-permute-start | bytes 2506760 | tf_op jit(solution)/shard_map/ppermute | solution.py:583
  11.8 15.0 %collective-permute-done.low_mine = f32[3,136,512]{2,1,0:T(8,128)S(1)} collective-permute-done((f32[3,136,512]{2,1,0:T(8,128)}, f32[3,136,512]{2,1,0:T(8,128)S(1)}, u32[]{:S(2)}, u32[]{:S(2)}) %collective-permute-start) | collective-permute-done | bytes 835616 | tf_op jit(solution)/shard_map/ppermute | solution.py:583
  26.7 1.5 collective-permute-start.1
  28.3 2.2 %collective-permute-done.2.high_mine = f32[3,136,512]{2,1,0:T(8,128)S(1)} collective-permute-done((f32[3,136,512]{2,1,0:T(8,128)}, f32[3,136,512]{2,1,0:T(8,128)S(1)}, u32[]{:S(2)}, u32[]{:S(2)}) %collective-permute-start.2) | collective-permute-done | bytes 835616 | tf_op jit(solution)/shard_map/ppermute | solution.py:583
  30.5 1.8 collective-permute-start.3
  32.3 18.6 %lay_basis.1 = (f32[16,256,512]{2,1,0:T(8,128)}, f32[16,24,256]{2,1,0:T(8,128)}) custom-call(f32[16,512]{1,0:T(8,128)} %get-tuple-element.23.count_ref, f32[16,512]{1,0:T(8,128)} %get-tuple-element.22.value_ref, f32[4096,512]{1,0:T(8,128)} %bitcast.14, f32[4096,512]{1,0:T(8,128)} %bitcast.15, f32[4096,512]{1,0:T(8,128)} %bitcast.16, f32[4096,512]{1,0:T(8,128)} %bitcast.17), custom_call_target="tpu_custom_call" | custom-call | flops 20000000000 | bytes 17000000 | tf_op jit(solution)/shard_map/lay_basis/pallas_call | solution.py:179
  51.0 9.2 %all-to-all-start.2 = ((f32[16,24,256]{2,1,0:T(8,128)}), f32[16,24,256]{2,1,0:T(8,128)S(1)}, u32[]{:S(2)}, u32[]{:S(2)}) async-start(f32[16,24,256]{2,1,0:T(8,128)} %get-tuple-element.16), calls=%async_computation.2 | async-start | bytes 786432 | tf_op jit(solution)/shard_map/all_to_all | solution.py:591
  61.7 32.9 %prop_terms.1 = f32[256,256]{1,0:T(8,128)} custom-call(s32[3]{0:T(128)} %pad_add_fusion.1.place_ref, f32[4,16,512]{2,1,0:T(8,128)} %get-tuple-element.12.model_ref, f32[16,256,512]{2,1,0:T(8,128)} %get-tuple-element.13.field_ref, f32[3,136,512]{2,1,0:T(8,128)} %copy-done.12, f32[3,136,512]{2,1,0:T(8,128)} %copy-done.14, f32[3,136,512]{2,1,0:T(8,128)} %copy-done.13, ...), custom_call_target="tpu_custom_call" | custom-call | flops 35000000512 | bytes 12000000 | tf_op jit(solution)/shard_map/prop_terms/pallas_call | solution.py:334
  94.6 6.7 %all-to-all-start = ((f32[16,16,256]{2,1,0:T(8,128)}), f32[16,16,256]{2,1,0:T(8,128)S(1)}, u32[]{:S(2)}, u32[]{:S(2)}) async-start(f32[16,16,256]{2,1,0:T(8,128)} %bitcast.21), calls=%async_computation | async-start | bytes 524288 | tf_op jit(solution)/shard_map/all_to_all | solution.py:591
  101.3 7.5 %all-to-all-done = f32[16,16,256]{2,1,0:T(8,128)S(1)} async-done(((f32[16,16,256]{2,1,0:T(8,128)}), f32[16,16,256]{2,1,0:T(8,128)S(1)}, u32[]{:S(2)}, u32[]{:S(2)}) %all-to-all-start) | async-done | bytes 262176 | tf_op jit(solution)/shard_map/all_to_all | solution.py:591
  109.6 3.6 %all-to-all-start.3 = ((f32[16,24,256]{2,1,0:T(8,128)}), f32[16,24,256]{2,1,0:T(8,128)S(1)}, u32[]{:S(2)}, u32[]{:S(2)}) async-start(f32[16,24,256]{2,1,0:T(8,128)} %broadcast_in_dim.8), calls=%async_computation.3 | async-start | bytes 786432 | tf_op jit(solution)/shard_map/all_to_all | solution.py:593
  113.2 8.3 %all-to-all-done.3.s_own = f32[16,24,256]{2,1,0:T(8,128)S(1)} async-done(((f32[16,24,256]{2,1,0:T(8,128)}), f32[16,24,256]{2,1,0:T(8,128)S(1)}, u32[]{:S(2)}, u32[]{:S(2)}) %all-to-all-start.3) | async-done | bytes 393248 | tf_op jit(solution)/shard_map/all_to_all | solution.py:593
  122.2 3.5 %all-to-all-start.1 = ((f32[16,16,256]{2,1,0:T(8,128)}), f32[16,16,256]{2,1,0:T(8,128)S(1)}, u32[]{:S(2)}, u32[]{:S(2)}) async-start(f32[16,16,256]{2,1,0:T(8,128)} %broadcast_in_dim.7), calls=%async_computation.1 | async-start | bytes 524288 | tf_op jit(solution)/shard_map/all_to_all | solution.py:593
  125.8 3.4 %collective-permute-start.5 = (f32[16,24,256]{2,1,0:T(8,128)S(1)}, f32[16,24,256]{2,1,0:T(8,128)S(1)}, u32[]{:S(2)}, u32[]{:S(2)}) collective-permute-start(f32[16,24,256]{2,1,0:T(8,128)S(1)} %all-to-all-done.3.s_own), channel_id=1, source_target_pairs={{0,16},{16,0},{32,48},{48,32},{64,80},{80,64},{96,112},{112,96},{1... | collective-permute-start | bytes 1179656 | tf_op jit(solution)/shard_map/ppermute | solution.py:587
  129.1 4.1 %all-to-all-done.1 = f32[16,16,256]{2,1,0:T(8,128)S(1)} async-done(((f32[16,16,256]{2,1,0:T(8,128)}), f32[16,16,256]{2,1,0:T(8,128)S(1)}, u32[]{:S(2)}, u32[]{:S(2)}) %all-to-all-start.1) | async-done | bytes 262176 | tf_op jit(solution)/shard_map/all_to_all | solution.py:593
  133.3 4.4 %collective-permute-start.4 = (f32[256,256]{1,0:T(8,128)S(1)}, f32[256,256]{1,0:T(8,128)S(1)}, u32[]{:S(2)}, u32[]{:S(2)}) collective-permute-start(f32[256,256]{1,0:T(8,128)S(1)} %bitcast.19), channel_id=1, source_target_pairs={{0,16},{16,0},{32,48},{48,32},{64,80},{80,64},{96,112},{112,96},{1... | collective-permute-start | bytes 786440 | tf_op jit(solution)/shard_map/ppermute | solution.py:587
  139.6 6.8 %merge_pair.1 = (f32[2,264,256]{2,1,0:T(8,128)}, f32[264,256]{1,0:T(8,128)}, f32[256,256]{1,0:T(8,128)}, f32[256,256]{1,0:T(8,128)}, f32[8,256]{1,0:T(8,128)}) custom-call(s32[1]{0:T(128)} %bitcast.core_ref, f32[256,256]{1,0:T(8,128)} %bitcast.20, f32[256,256]{1,0:T(8,128)} %copy-done.9, f32[16,24,256]{2,1,0:T(8,128)} %copy-done, f32[16,24,256]{2,1,0:T(8,128)} %copy-done.4), custom_call_target="tpu_custom_call" | custom-call | tf_op jit(solution)/shard_map/merge_pair/pallas_call | solution.py:470
  147.6 1.5 collective-permute-start.8
  149.0 6.4 %collective-permute-done.6.m_prev = f32[264,256]{1,0:T(8,128)S(1)} collective-permute-done((f32[264,256]{1,0:T(8,128)}, f32[264,256]{1,0:T(8,128)S(1)}, u32[]{:S(2)}, u32[]{:S(2)}) %collective-permute-start.6) | collective-permute-done | bytes 270368 | tf_op jit(solution)/shard_map/ppermute | solution.py:583
  155.5 2.5 %collective-permute-start.10 = (f32[264,256]{1,0:T(8,128)S(1)}, f32[264,256]{1,0:T(8,128)S(1)}, u32[]{:S(2)}, u32[]{:S(2)}) collective-permute-start(f32[264,256]{1,0:T(8,128)S(1)} %broadcast_select_fusion), channel_id=1, source_target_pairs={{0,32},{16,112},{32,64},{48,16},{64,96},{80,48},{96,0},{112,80},{1... | collective-permute-start | bytes 811016 | tf_op jit(solution)/shard_map/ppermute | solution.py:636
  158.4 2.9 %collective-permute-done.10.m_far = f32[264,256]{1,0:T(8,128)S(1)} collective-permute-done((f32[264,256]{1,0:T(8,128)S(1)}, f32[264,256]{1,0:T(8,128)S(1)}, u32[]{:S(2)}, u32[]{:S(2)}) %collective-permute-start.10) | collective-permute-done | bytes 270368 | tf_op jit(solution)/shard_map/ppermute | solution.py:636
  161.3 3.1 %collective-permute-start.11 = (f32[264,256]{1,0:T(8,128)S(1)}, f32[264,256]{1,0:T(8,128)S(1)}, u32[]{:S(2)}, u32[]{:S(2)}) collective-permute-start(f32[264,256]{1,0:T(8,128)S(1)} %collective-permute-done.10.m_far), channel_id=1, source_target_pairs={{0,16},{16,0},{32,48},{48,32},{64,80},{80,64},{96,112},{112,96},{1... | collective-permute-start | bytes 811016 | tf_op jit(solution)/shard_map/ppermute | solution.py:587
  166.3 23.8 %solve_chain.1 = (f32[1,2,256]{2,1,0:T(2,128)}, f32[1,16,512]{2,1,0:T(8,128)}) custom-call(s32[2]{0:T(128)} %pad_add_fusion.place_ref, f32[2,264,256]{2,1,0:T(8,128)} %get-tuple-element.17.both_ref, f32[264,256]{1,0:T(8,128)} %copy-done.1, f32[264,256]{1,0:T(8,128)} %copy-done.6, f32[264,256]{1,0:T(8,128)} %copy-done.2, f32[264,256]{1,0:T(8,128)} %copy-done.7, ...), custom_call_target="tpu_custom_call" | custom-call | tf_op jit(solution)/shard_map/solve_chain/pallas_call | solution.py:559
  (58 shorter events, 11.1 us)
Async XLA Ops:
  0.6 9.9 %copy-start.11 = (s32[1,512]{1,0:T(1,128)S(1)}, s32[1,512]{1,0:T(1,128)}, u32[]{:S(2)}) copy-start(s32[1,512]{1,0:T(1,128)} %param.12) | copy-start | bytes 6148
  0.6 9.9 %copy-start.10 = (f32[1,512]{1,0:T(1,128)S(1)}, f32[1,512]{1,0:T(1,128)}, u32[]{:S(2)}) copy-start(f32[1,512]{1,0:T(1,128)} %param.13) | copy-start | bytes 6148
  5.1 21.6 %collective-permute-start = (f32[3,136,512]{2,1,0:T(8,128)}, f32[3,136,512]{2,1,0:T(8,128)S(1)}, u32[]{:S(2)}, u32[]{:S(2)}) collective-permute-start(f32[3,136,512]{2,1,0:T(8,128)} %get-tuple-element.14), channel_id=1, source_target_pairs={{0,1},{1,2},{2,3},{3,4},{4,5},{5,6},{6,7},{7,8},{8,9},{9,10},{10,1... | collective-permute-start | bytes 2506760 | tf_op jit(solution)/shard_map/ppermute | solution.py:583
  9.2 21.3 %collective-permute-start.2 = (f32[3,136,512]{2,1,0:T(8,128)}, f32[3,136,512]{2,1,0:T(8,128)S(1)}, u32[]{:S(2)}, u32[]{:S(2)}) collective-permute-start(f32[3,136,512]{2,1,0:T(8,128)} %get-tuple-element.15), channel_id=1, source_target_pairs={{1,0},{2,1},{3,2},{4,3},{5,4},{6,5},{7,6},{8,7},{9,8},{10,9},{11,1... | collective-permute-start | bytes 2506760 | tf_op jit(solution)/shard_map/ppermute | solution.py:583
  26.7 24.2 %copy-start.12 = (f32[3,136,512]{2,1,0:T(8,128)}, f32[3,136,512]{2,1,0:T(8,128)S(1)}, u32[]{:S(2)}) copy-start(f32[3,136,512]{2,1,0:T(8,128)S(1)} %collective-permute-done.low_mine) | copy-start | bytes 2506756
  26.7 34.1 %collective-permute-start.1 = (f32[3,136,512]{2,1,0:T(8,128)S(1)}, f32[3,136,512]{2,1,0:T(8,128)S(1)}, u32[]{:S(2)}, u32[]{:S(2)}) collective-permute-start(f32[3,136,512]{2,1,0:T(8,128)S(1)} %collective-permute-done.low_mine), channel_id=1, source_target_pairs={{0,16},{16,0},{32,48},{48,32},{64,80},{80,64},{96,112},{112,96},{1... | collective-permute-start | bytes 2506760 | tf_op jit(solution)/shard_map/ppermute | solution.py:587
  30.5 20.5 %copy-start.13 = (f32[3,136,512]{2,1,0:T(8,128)}, f32[3,136,512]{2,1,0:T(8,128)S(1)}, u32[]{:S(2)}) copy-start(f32[3,136,512]{2,1,0:T(8,128)S(1)} %collective-permute-done.2.high_mine) | copy-start | bytes 2506756
  30.5 30.3 %collective-permute-start.3 = (f32[3,136,512]{2,1,0:T(8,128)S(1)}, f32[3,136,512]{2,1,0:T(8,128)}, u32[]{:S(2)}, u32[]{:S(2)}) collective-permute-start(f32[3,136,512]{2,1,0:T(8,128)S(1)} %collective-permute-done.2.high_mine), channel_id=1, source_target_pairs={{0,16},{16,0},{32,48},{48,32},{64,80},{80,64},{96,112},{112,96},{1... | collective-permute-start | bytes 2506760 | tf_op jit(solution)/shard_map/ppermute | solution.py:587
  51.0 43.6 %all-to-all-start.2 = ((f32[16,24,256]{2,1,0:T(8,128)}), f32[16,24,256]{2,1,0:T(8,128)S(1)}, u32[]{:S(2)}, u32[]{:S(2)}) async-start(f32[16,24,256]{2,1,0:T(8,128)} %get-tuple-element.16), calls=%async_computation.2 | async-start | bytes 786432 | tf_op jit(solution)/shard_map/all_to_all | solution.py:591
  94.6 14.2 %all-to-all-start = ((f32[16,16,256]{2,1,0:T(8,128)}), f32[16,16,256]{2,1,0:T(8,128)S(1)}, u32[]{:S(2)}, u32[]{:S(2)}) async-start(f32[16,16,256]{2,1,0:T(8,128)} %bitcast.21), calls=%async_computation | async-start | bytes 524288 | tf_op jit(solution)/shard_map/all_to_all | solution.py:591
  109.6 11.9 %all-to-all-start.3 = ((f32[16,24,256]{2,1,0:T(8,128)}), f32[16,24,256]{2,1,0:T(8,128)S(1)}, u32[]{:S(2)}, u32[]{:S(2)}) async-start(f32[16,24,256]{2,1,0:T(8,128)} %broadcast_in_dim.8), calls=%async_computation.3 | async-start | bytes 786432 | tf_op jit(solution)/shard_map/all_to_all | solution.py:593
  121.5 17.4 %copy-start = (f32[16,24,256]{2,1,0:T(8,128)}, f32[16,24,256]{2,1,0:T(8,128)S(1)}, u32[]{:S(2)}) copy-start(f32[16,24,256]{2,1,0:T(8,128)S(1)} %all-to-all-done.3.s_own) | copy-start | bytes 1179652
  122.2 11.0 %all-to-all-start.1 = ((f32[16,16,256]{2,1,0:T(8,128)}), f32[16,16,256]{2,1,0:T(8,128)S(1)}, u32[]{:S(2)}, u32[]{:S(2)}) async-start(f32[16,16,256]{2,1,0:T(8,128)} %broadcast_in_dim.7), calls=%async_computation.1 | async-start | bytes 524288 | tf_op jit(solution)/shard_map/all_to_all | solution.py:593
  125.8 12.0 %collective-permute-start.5 = (f32[16,24,256]{2,1,0:T(8,128)S(1)}, f32[16,24,256]{2,1,0:T(8,128)S(1)}, u32[]{:S(2)}, u32[]{:S(2)}) collective-permute-start(f32[16,24,256]{2,1,0:T(8,128)S(1)} %all-to-all-done.3.s_own), channel_id=1, source_target_pairs={{0,16},{16,0},{32,48},{48,32},{64,80},{80,64},{96,112},{112,96},{1... | collective-permute-start | bytes 1179656 | tf_op jit(solution)/shard_map/ppermute | solution.py:587
  133.3 5.6 %copy-start.3 = (f32[16,16,256]{2,1,0:T(8,128)}, f32[16,16,256]{2,1,0:T(8,128)S(1)}, u32[]{:S(2)}) copy-start(f32[16,16,256]{2,1,0:T(8,128)S(1)} %all-to-all-done.1) | copy-start | bytes 786436
  133.3 5.6 %collective-permute-start.4 = (f32[256,256]{1,0:T(8,128)S(1)}, f32[256,256]{1,0:T(8,128)S(1)}, u32[]{:S(2)}, u32[]{:S(2)}) collective-permute-start(f32[256,256]{1,0:T(8,128)S(1)} %bitcast.19), channel_id=1, source_target_pairs={{0,16},{16,0},{32,48},{48,32},{64,80},{80,64},{96,112},{112,96},{1... | collective-permute-start | bytes 786440 | tf_op jit(solution)/shard_map/ppermute | solution.py:587
  146.3 9.1 %collective-permute-start.6 = (f32[264,256]{1,0:T(8,128)}, f32[264,256]{1,0:T(8,128)S(1)}, u32[]{:S(2)}, u32[]{:S(2)}) collective-permute-start(f32[264,256]{1,0:T(8,128)} %get-tuple-element.18), channel_id=1, source_target_pairs={{0,32},{16,48},{32,64},{48,80},{64,96},{80,112},{96,0},{112,16},{1... | collective-permute-start | bytes 811016 | tf_op jit(solution)/shard_map/ppermute | solution.py:583
  147.6 7.9 %collective-permute-start.8 = (f32[264,256]{1,0:T(8,128)}, f32[264,256]{1,0:T(8,128)S(1)}, u32[]{:S(2)}, u32[]{:S(2)}) collective-permute-start(f32[264,256]{1,0:T(8,128)} %get-tuple-element.18), channel_id=1, source_target_pairs={{0,96},{16,112},{32,0},{48,16},{64,32},{80,48},{96,64},{112,80},{1... | collective-permute-start | bytes 811016 | tf_op jit(solution)/shard_map/ppermute | solution.py:583
  155.4 10.2 %copy-start.1 = (f32[264,256]{1,0:T(8,128)}, f32[264,256]{1,0:T(8,128)S(1)}, u32[]{:S(2)}) copy-start(f32[264,256]{1,0:T(8,128)S(1)} %collective-permute-done.6.m_prev) | copy-start | bytes 811012
  155.4 10.2 %copy-start.2 = (f32[264,256]{1,0:T(8,128)}, f32[264,256]{1,0:T(8,128)S(1)}, u32[]{:S(2)}) copy-start(f32[264,256]{1,0:T(8,128)S(1)} %collective-permute-done.8.m_next) | copy-start | bytes 811012
  155.5 5.9 %collective-permute-start.10 = (f32[264,256]{1,0:T(8,128)S(1)}, f32[264,256]{1,0:T(8,128)S(1)}, u32[]{:S(2)}, u32[]{:S(2)}) collective-permute-start(f32[264,256]{1,0:T(8,128)S(1)} %broadcast_select_fusion), channel_id=1, source_target_pairs={{0,32},{16,112},{32,64},{48,16},{64,96},{80,48},{96,0},{112,80},{1... | collective-permute-start | bytes 811016 | tf_op jit(solution)/shard_map/ppermute | solution.py:636
  157.9 7.1 %collective-permute-start.7 = (f32[264,256]{1,0:T(8,128)S(1)}, f32[264,256]{1,0:T(8,128)S(1)}, u32[]{:S(2)}, u32[]{:S(2)}) collective-permute-start(f32[264,256]{1,0:T(8,128)S(1)} %collective-permute-done.6.m_prev), channel_id=1, source_target_pairs={{0,16},{16,0},{32,48},{48,32},{64,80},{80,64},{96,112},{112,96},{1... | collective-permute-start | bytes 811016 | tf_op jit(solution)/shard_map/ppermute | solution.py:587
  158.3 6.7 %collective-permute-start.9 = (f32[264,256]{1,0:T(8,128)S(1)}, f32[264,256]{1,0:T(8,128)S(1)}, u32[]{:S(2)}, u32[]{:S(2)}) collective-permute-start(f32[264,256]{1,0:T(8,128)S(1)} %collective-permute-done.8.m_next), channel_id=1, source_target_pairs={{0,16},{16,0},{32,48},{48,32},{64,80},{80,64},{96,112},{112,96},{1... | collective-permute-start | bytes 811016 | tf_op jit(solution)/shard_map/ppermute | solution.py:587
  161.3 4.3 %collective-permute-start.11 = (f32[264,256]{1,0:T(8,128)S(1)}, f32[264,256]{1,0:T(8,128)S(1)}, u32[]{:S(2)}, u32[]{:S(2)}) collective-permute-start(f32[264,256]{1,0:T(8,128)S(1)} %collective-permute-done.10.m_far), channel_id=1, source_target_pairs={{0,16},{16,0},{32,48},{48,32},{64,80},{80,64},{96,112},{112,96},{1... | collective-permute-start | bytes 811016 | tf_op jit(solution)/shard_map/ppermute | solution.py:587
  (7 other events, 9.3 us)

commit v3 on v2

--- a/solution.py
+++ b/solution.py
@@ -15,6 +15,7 @@
 SUB = 8
 LANES = 128
 TAIL = 8
+CHIPS = 4
 
 
 def split(value):
@@ -202,7 +203,7 @@
 
 
 def prop_kernel(
-    place_ref, model_ref, field_ref, low_mine, low_theirs, high_mine, high_theirs,
+    place_ref, model_ref, field_ref, low_mine, low_theirs, high_mine, high_theirs, obs_ref,
     out_ref, deal, model, wide, edges, fore, back,
 ):
     step_id = pl.program_id(0)
@@ -316,21 +317,28 @@
 
     @pl.when(step_id == steps - 1)
     def _():
-        out_ref[...] = jnp.zeros_like(out_ref)
+        tiles = out_ref.shape[0]
+        part = width // tiles
+        out_ref[:, :part, :] = jnp.zeros_like(out_ref[:, :part, :])
+        out_ref[:, part:, :] = obs_ref[...]
 
         def body(i, carry):
-            out_ref[...] += dot3(back[i], fore[i])
+            terms = dot3(back[i], fore[i])
+            for t in range(tiles):
+                out_ref[t, :part, :] += terms[t * part : (t + 1) * part]
             return carry
 
         lax.fori_loop(0, rows, body, 0)
 
 
-def prop_terms(place, model, field, edges):
+def prop_terms(place, model, field, edges, obs):
     rows, width, columns = field.shape
     block = 32
     steps = width // block
     ext = rows + 2 * REACH
     vmem = pl.BlockSpec(memory_space=pltpu.VMEM)
+    tiles, lines, _ = obs.shape
+    total = (tiles, width // tiles + lines, width)
     return pl.pallas_call(
         prop_kernel,
         grid_spec=pltpu.PrefetchScalarGridSpec(
@@ -346,8 +354,9 @@
                 vmem,
                 vmem,
                 vmem,
+                vmem,
             ],
-            out_specs=pl.BlockSpec((width, width), lambda k, place: (0, 0)),
+            out_specs=pl.BlockSpec(total, lambda k, place: (0, 0, 0)),
             scratch_shapes=[
                 pltpu.VMEM((3 * columns, columns), jnp.bfloat16),
                 pltpu.VMEM((4, -(-ext // SUB) * SUB, columns), jnp.float32),
@@ -357,10 +366,10 @@
                 pltpu.VMEM((rows, width, columns), jnp.float32),
             ],
         ),
-        out_shape=jax.ShapeDtypeStruct((width, width), jnp.float32),
+        out_shape=jax.ShapeDtypeStruct(total, jnp.float32),
         cost_estimate=pl.CostEstimate(flops=35 * 10**9, bytes_accessed=12 * 10**6, transcendentals=0),
         name="prop_terms",
-    )(place, model, field, *edges)
+    )(place, model, field, *edges, obs)
 
 
 def eye_mask(width):
@@ -390,7 +399,9 @@
     guesses = []
     for mat in mats:
         bound = jnp.max(jnp.sum(jnp.abs(mat), axis=0, keepdims=True), axis=1, keepdims=True)
-        guesses.append(identity * (1.7 / bound))
+        trace = jnp.sum(jnp.sum(identity * mat, axis=0, keepdims=True), axis=1, keepdims=True)
+        square = jnp.sum(jnp.sum(mat * mat, axis=0, keepdims=True), axis=1, keepdims=True)
+        guesses.append(identity * jnp.minimum(trace / square, 1.9 / bound))
 
     def stage(state, passes, goal, slowest):
         def more(state):
@@ -419,23 +430,24 @@
 
 
 def pair_kernel(
-    core_ref, p_own, p_other, s_own, s_other, both_ref, send_ref, left_ref, right_ref, mid_ref
+    place_ref, own_ref, other_ref, both_ref, send_ref, left_ref, right_ref, outer_ref, small_ref
 ):
-    tiles, _, width = s_own.shape
+    tiles, _, width = own_ref.shape
     part = width // tiles
-    first = core_ref[0] == 0
+    core, chip = place_ref[0], place_ref[1]
+    first = core == 0
     row, col = eye_mask(width)
     identity = jnp.where(row == col, 1.0, 0.0).astype(jnp.float32)
 
     def ordered(own, other):
         return jnp.where(first, own, other), jnp.where(first, other, own)
 
-    p_left, p_right = ordered(p_own[...], p_other[...])
-    info = ordered(
-        jnp.concatenate([s_own[t, :part, :] for t in range(tiles)], axis=0),
-        jnp.concatenate([s_other[t, :part, :] for t in range(tiles)], axis=0),
-    )
-    rhs_left, rhs_right = ordered(s_own[0, part:, :], s_other[0, part:, :])
+    def stacked(ref, at):
+        return jnp.concatenate([ref[t, at : at + part, :] for t in range(tiles)], axis=0)
+
+    p_left, p_right = ordered(stacked(own_ref, 0), stacked(other_ref, 0))
+    info = ordered(stacked(own_ref, part), stacked(other_ref, part))
+    rhs_left, rhs_right = ordered(own_ref[0, 2 * part :, :], other_ref[0, 2 * part :, :])
     square_left = dot(p_left, p_left, (0, 0))
     square_right = dot(p_right, p_right, (0, 0))
     middle = (Q + 2 * RIDGE) * identity + info[0] + Q * square_right
@@ -451,40 +463,71 @@
     lower = (Q + RIDGE) * identity + info[1] - (Q * Q) * by_right[width : 2 * width]
     head = Q * by_left[width:]
     tail = rhs_right + Q * by_right[2 * width :]
-    lower_diag = jnp.sum(jnp.where(row == col, lower, 0.0), axis=0, keepdims=True)
-    both_ref[0, :width, :] = jnp.where(row >= col, upper, lower)
-    small = lax.broadcasted_iota(jnp.int32, (TAIL, width), 0)
-    both_ref[0, width:, :] = jnp.where(small == 0, lower_diag, jnp.where(small == 1, head, tail))
     both_ref[1, :width, :] = cross
+    left_ref[...] = Q * toward_left
+    right_ref[...] = Q * toward_right
+    outer_ref[...] = jnp.zeros_like(outer_ref)
+    small_ref[...] = jnp.zeros_like(small_ref)
+    small_ref[0] = mid
+    lines = lax.broadcasted_iota(jnp.int32, (TAIL, width), 0)
+
+    def pack(upper, lower, head, tail):
+        lower_diag = jnp.sum(jnp.where(row == col, lower, 0.0), axis=0, keepdims=True)
+        both_ref[0, :width, :] = jnp.where(row >= col, upper, lower)
+        both_ref[0, width:, :] = jnp.where(lines == 0, lower_diag, jnp.where(lines == 1, head, tail))
+
+    opening, closing = chip == 0, chip == CHIPS - 1
+    outer = jnp.logical_or(opening, closing)
+
+    @pl.when(outer)
+    def _():
+        gone = jnp.where(opening, upper, lower)
+        kept = jnp.where(opening, lower, upper)
+        joint = jnp.where(opening, cross, cross.T)
+        gone_rhs = jnp.where(opening, head, tail)
+        kept_rhs = jnp.where(opening, tail, head)
+        (gone_back,) = inverses([gone])
+        toward = dot(joint, gone_back, (0, 0))
+        rest = dot(gone_rhs, gone_back)
+        both = dot(jnp.concatenate([toward, rest], axis=0), joint)
+        kept = kept - both[:width]
+        kept_rhs = kept_rhs - both[width:]
+        outer_ref[...] = toward
+        small_ref[1] = rest
+        pack(kept, kept, kept_rhs, kept_rhs)
+
+    @pl.when(jnp.logical_not(outer))
+    def _():
+        pack(upper, lower, head, tail)
+
     both_ref[1, width:, :] = jnp.zeros((TAIL, width), jnp.float32)
     send_ref[...] = jnp.where(first, both_ref[0], both_ref[1])
-    left_ref[...] = Q * toward_left
-    right_ref[...] = Q * toward_right
-    mid_ref[...] = mid
-
-
-def merge_pair(core, *terms):
-    width = terms[0].shape[1]
+
+
+def merge_pair(place, own, other):
+    width = own.shape[2]
     vmem = pl.BlockSpec(memory_space=pltpu.VMEM)
     block = jax.ShapeDtypeStruct((width, width), jnp.float32)
     return pl.pallas_call(
         pair_kernel,
-        in_specs=[pl.BlockSpec(memory_space=pltpu.SMEM)] + [vmem] * 4,
-        out_specs=[vmem] * 5,
+        in_specs=[pl.BlockSpec(memory_space=pltpu.SMEM)] + [vmem] * 2,
+        out_specs=[vmem] * 6,
         out_shape=[
             jax.ShapeDtypeStruct((2, width + TAIL, width), jnp.float32),
             jax.ShapeDtypeStruct((width + TAIL, width), jnp.float32),
             block,
             block,
-            jax.ShapeDtypeStruct((TAIL, width), jnp.float32),
+            block,
+            jax.ShapeDtypeStruct((2, TAIL, width), jnp.float32),
         ],
         name="merge_pair",
-    )(core, *terms)
+    )(place, own, other)
 
 
 def chain_kernel(
-    place_ref, both_ref, m_prev, o_prev, m_next, o_next, m_far, o_far, left_ref, right_ref, mid_ref,
-    basis_ref, coeff_ref, end_ref, blocks, states, basis, weight, sem,
+    place_ref, both_ref, m_prev, o_prev, m_next, o_next, m_far, o_far,
+    left_ref, right_ref, outer_ref, small_ref,
+    basis_ref, coeff_ref, end_ref, blocks, basis, weight, sem,
 ):
     fetch = pltpu.make_async_copy(basis_ref, basis, sem)
     fetch.start()
@@ -493,11 +536,11 @@
     row, col = eye_mask(width)
     blocks[chip] = both_ref[...]
     for mine, theirs, move in ((m_prev, o_prev, 3), (m_next, o_next, 1), (m_far, o_far, 2)):
-        at = lax.rem(chip + move, 4)
+        at = lax.rem(chip + move, CHIPS)
         blocks[at, core] = mine[...]
         blocks[at, 1 - core] = theirs[...]
-    upper, lower, cross, head, tail = [], [], [], [], []
-    for c in range(4):
+    upper, lower, head, tail = [], [], [], []
+    for c in range(CHIPS):
         packed = blocks[c, 0, :width, :]
         turned = packed.T
         small = blocks[c, 0, width:, :]
@@ -506,35 +549,27 @@
         lower.append(jnp.where(row == col, jnp.broadcast_to(small[0:1], (width, width)), off))
         head.append(jnp.broadcast_to(small[1:2], (TAIL, width)))
         tail.append(jnp.broadcast_to(small[2:3], (TAIL, width)))
-        cross.append(blocks[c, 1, :width, :])
-    diag = [upper[0], lower[0] + upper[1], lower[1] + upper[2], lower[2] + upper[3], lower[3]]
-    rhs = [head[0], tail[0] + head[1], tail[1] + head[2], tail[2] + head[3], tail[3]]
-    inv0, inv2, inv4 = inverses([diag[0], diag[2], diag[4]])
-    t10 = dot(cross[0], inv0, (0, 0))
-    t12 = dot(cross[1], inv2)
-    t32 = dot(cross[2], inv2, (0, 0))
-    t34 = dot(cross[3], inv4)
-    z0, z2, z4 = dot(rhs[0], inv0), dot(rhs[2], inv2), dot(rhs[4], inv4)
-    diag1 = diag[1] - dot(t10, cross[0]) - dot(t12, cross[1], (1, 1))
-    diag3 = diag[3] - dot(t32, cross[2]) - dot(t34, cross[3], (1, 1))
-    link = -dot(t12, cross[2])
-    rhs1 = rhs[1] - dot(z0, cross[0]) - dot(z2, cross[1], (1, 1))
-    rhs3 = rhs[3] - dot(z2, cross[2]) - dot(z4, cross[3], (1, 1))
-    (inv1,) = inverses([diag1])
-    t31 = dot(link, inv1, (0, 0))
-    z1 = dot(rhs1, inv1)
-    diag3 = diag3 - dot(t31, link)
-    rhs3 = rhs3 - dot(z1, link)
-    (inv3,) = inverses([diag3])
-    y3 = dot(rhs3, inv3)
-    y1 = z1 - dot(y3, t31)
-    y0 = z0 - dot(y1, t10)
-    y2 = z2 - dot(y1, t12) - dot(y3, t32)
-    y4 = z4 - dot(y3, t34)
-    for c, state in enumerate((y0, y1, y2, y3, y4)):
-        states[c] = state
-    begin, finish = states[chip], states[chip + 1]
-    inner = mid_ref[...] + dot(begin, left_ref[...]) + dot(finish, right_ref[...])
+    cross1, cross2 = blocks[1, 1, :width, :], blocks[2, 1, :width, :]
+    rhs1, rhs2, rhs3 = (tail[c] + head[c + 1] for c in range(3))
+    inv1, inv3 = inverses([lower[0] + upper[1], lower[2] + upper[3]])
+    toward1 = dot(cross1, inv1, (0, 0))
+    toward3 = dot(cross2, inv3)
+    z1, z3 = dot(rhs1, inv1), dot(rhs3, inv3)
+    by1 = dot(jnp.concatenate([toward1, z1], axis=0), cross1)
+    by3 = dot(jnp.concatenate([toward3, z3], axis=0), cross2, (1, 1))
+    (inv2,) = inverses([lower[1] + upper[2] - by1[:width] - by3[:width]])
+    y2 = dot(rhs2 - by1[width:] - by3[width:], inv2)
+    y1 = z1 - dot(y2, toward1)
+    y3 = z3 - dot(y2, toward3)
+    opening = chip == 0
+    y_outer = small_ref[1] - dot(jnp.where(opening, y1, y3), outer_ref[...])
+    begin = jnp.where(
+        opening, y_outer, jnp.where(chip == 1, y1, jnp.where(chip == 2, y2, y3))
+    )
+    finish = jnp.where(
+        opening, y1, jnp.where(chip == 1, y2, jnp.where(chip == 2, y3, y_outer))
+    )
+    inner = small_ref[0] + dot(begin, left_ref[...]) + dot(finish, right_ref[...])
     first = core == 0
     start = jnp.where(first, begin, inner)
     end = jnp.where(first, inner, finish)
@@ -552,14 +587,14 @@
     end_ref[0] = lax.fori_loop(0, width, add, jnp.zeros((rows, columns), jnp.float32), unroll=8)
 
 
-def solve_chain(place, both, received, left, right, mid, basis2, rows):
+def solve_chain(place, both, received, kept, basis2, rows):
     width = both.shape[2]
     columns = basis2.shape[1]
     vmem = pl.BlockSpec(memory_space=pltpu.VMEM)
     return pl.pallas_call(
         chain_kernel,
         in_specs=[pl.BlockSpec(memory_space=pltpu.SMEM)]
-        + [vmem] * 10
+        + [vmem] * 11
         + [pl.BlockSpec(memory_space=pltpu.HBM)],
         out_specs=[vmem, vmem],
         out_shape=[
@@ -567,14 +602,13 @@
             jax.ShapeDtypeStruct((1, rows, columns), jnp.float32),
         ],
         scratch_shapes=[
-            pltpu.VMEM((4, 2, width + TAIL, width), jnp.float32),
-            pltpu.VMEM((5, TAIL, width), jnp.float32),
+            pltpu.VMEM((CHIPS, 2, width + TAIL, width), jnp.float32),
             pltpu.VMEM(basis2.shape, jnp.float32),
             pltpu.VMEM((width, LANES), jnp.float32),
             pltpu.SemaphoreType.DMA,
         ],
         name="solve_chain",
-    )(place, both, *received, left, right, mid, basis2)
+    )(place, both, *received, *kept, basis2)
 
 
 def shift(value, axis, step, wrap):
@@ -585,12 +619,6 @@
 
 def swap_core(value):
     return lax.ppermute(value, "tm", [(i, i ^ 1) for i in range(lax.axis_size("tm"))])
-
-
-def tile_sum(pieces, scale):
-    slices = lax.all_to_all(pieces, "tile", 0, 0, tiled=True)
-    mine = jnp.sum(slices, axis=0) * scale
-    return lax.all_to_all(jnp.broadcast_to(mine[None], pieces.shape), "tile", 0, 0, tiled=True)
 
 
 def obs_maps(cells, values, rows, columns):
@@ -617,28 +645,27 @@
     low_send, high_send, model = edge_terms(core[None], models, basis2, width, rows)
     low = shift(low_send, "tile", 1, False)
     high = shift(high_send, "tile", -1, False)
-    edges = (low, swap_core(low), high, swap_core(high))
     count, value = obs_maps(obs_cells[0], obs_values[0], rows, columns)
     field, obs = lay_basis(basis2, count, value, width, rows, tiles)
+    low, high, obs = lax.optimization_barrier((low, high, obs))
+    edges = (low, swap_core(low), high, swap_core(high))
     place = jnp.stack([core, lax.axis_index("tile"), jnp.int32(tiles - 1)])
-    s_own = tile_sum(obs, 1.0 / float(NOBS))
-    s_other = swap_core(s_own)
-    prop = prop_terms(place, model, field, edges)
+    terms = prop_terms(place, model, field, edges, obs)
+
+    slices = jnp.sum(lax.all_to_all(terms, "tile", 0, 0, tiled=True), axis=0)
+    lines = lax.broadcasted_iota(jnp.int32, slices.shape, 0)
     cells = float(tiles * rows * columns)
-    p_own = tile_sum(prop.reshape(tiles, width // tiles, width), 1.0 / cells).reshape(width, width)
-    p_other = swap_core(p_own)
-
-    both, send, left, right, mid = merge_pair(core[None], p_own, p_other, s_own, s_other)
-    prev_mine = shift(send, "tm", 2, True)
-    next_mine = shift(send, "tm", -2, True)
-    size = lax.axis_size("tm")
-    onward = [(i, (i + (2 if i % 2 == 0 else size - 2)) % size) for i in range(size)]
-    far_mine = lax.ppermute(jnp.where(core == 0, prev_mine, next_mine), "tm", onward)
+    slices = slices * jnp.where(lines < width // tiles, 1.0 / cells, 1.0 / float(NOBS))
+    own = lax.all_to_all(jnp.broadcast_to(slices[None], terms.shape), "tile", 0, 0, tiled=True)
+    other = swap_core(own)
+
+    place = jnp.stack([core, chip])
+    both, send, *kept = merge_pair(place, own, other)
     received = []
-    for mine in (prev_mine, next_mine, far_mine):
+    for step in (2, -2, 4):
+        mine = shift(send, "tm", step, True)
         received += [mine, swap_core(mine)]
-    place = jnp.stack([core, chip])
-    return tuple(solve_chain(place, both, received, left, right, mid, basis2, rows))
+    return tuple(solve_chain(place, both, received, kept, basis2, rows))
 
 
 def solution(mesh):

time: 191 us -> 155 us (0.81)
  waiting for transfers between devices: 48.2 us -> 23.5 us
  starting transfers between devices: 48.2 us -> 28.4 us
  blocking collectives: 0 us -> 14.7 us
  Pallas kernels: 86.5 us -> 80.8 us
    ppermute x4 -> x5, waiting for transfers between devices: 23.6 us -> 6.56 us  [shift(): return lax.ppermute(value, axis, pairs)]
    all_to_all x0 -> x1, blocking collectives: none -> 14.7 us  [shards(): lax.all_to_all(jnp.broadcast_to(slices[None], terms.shape), 'tile', 0, 0,...]
    all_to_all x4 -> x1, starting transfers between devices: 23 us -> 9.19 us  [shards(): slices = jnp.sum(lax.all_to_all(terms, 'tile', 0, 0, tiled=True), axis=0)]
    pallas_call x1, Pallas kernels: 23.8 us -> 13.3 us  [solve_chain(): pl.pallas_call(chain_kernel, in_specs=[pl.BlockSpec(memory_space=pltpu.SM...]
    all_to_all x4 -> x1, waiting for transfers between devices: 19.9 us -> 12.1 us  [shards(): slices = jnp.sum(lax.all_to_all(terms, 'tile', 0, 0, tiled=True), axis=0)]
    pallas_call x1, Pallas kernels: 6.75 us -> 11.2 us  [merge_pair(): pl.pallas_call(pair_kernel, in_specs=[pl.BlockSpec(memory_space=pltpu.SME...]
    ppermute x7 -> x6, starting transfers between devices: 14.8 us -> 11.2 us  [swap_core(): lax.ppermute(value, 'tm', [(i, i ^ 1) for i in range(lax.axis_size('tm'))])]
    ppermute x7 -> x6, waiting for transfers between devices: 1.74 us -> 4.82 us  [swap_core(): lax.ppermute(value, 'tm', [(i, i ^ 1) for i in range(lax.axis_size('tm'))])]
  transfers between devices with their start and end apart: 16 -> 12, of which waited for: 9 -> 8; matrix products, arithmetic and copies ran while one was open for 1% -> 2% of each run, Pallas kernels for 27% -> 12%
where the time goes in v3:
time: 155 us; the launch traced here: 153 us
  Pallas kernels  80.8 us (52%)
  starting transfers between devices  28.4 us (18%)
  waiting for transfers between devices  23.5 us (15%)
  blocking collectives  14.7 us (9%)
  local copies, waits for them, and re-layouts  3.17 us (2%)
    pallas_call x1, Pallas kernels, prop_terms(): pl.pallas_call(prop_kernel, grid_spec=pltpu.PrefetchScalarGridSpec(num_sc...  33.2 us
    pallas_call x1, Pallas kernels, lay_basis(): pl.pallas_call(functools.partial(lay_kernel, rows), grid=(width // block,...  18.6 us
    all_to_all x1, blocking collectives, shards(): lax.all_to_all(jnp.broadcast_to(slices[None], terms.shape), 'tile', 0, 0,...  14.7 us
    pallas_call x1, Pallas kernels, solve_chain(): pl.pallas_call(chain_kernel, in_specs=[pl.BlockSpec(memory_space=pltpu.SM...  13.3 us
    all_to_all x1, waiting for transfers between devices, shards(): slices = jnp.sum(lax.all_to_all(terms, 'tile', 0, 0, tiled=True), axis=0)  12.1 us
    pallas_call x1, Pallas kernels, merge_pair(): pl.pallas_call(pair_kernel, in_specs=[pl.BlockSpec(memory_space=pltpu.SME...  11.2 us
    ppermute x6, starting transfers between devices, swap_core(): lax.ppermute(value, 'tm', [(i, i ^ 1) for i in range(lax.axis_size('tm'))])  11.2 us
    all_to_all x1, starting transfers between devices, shards(): slices = jnp.sum(lax.all_to_all(terms, 'tile', 0, 0, tiled=True), axis=0)  9.19 us
  transfers between devices with their start and end apart: 12, of which 8 were waited for; matrix products, arithmetic and copies ran while one was open for 2% of the time, Pallas kernels for 12%

profile of v3, /device:TPU:1, one launch (start us, length us, event | category | flops | bytes accessed | tf_op | source)
XLA Modules:
  0.0 153.4 jit_solution(12628331327730120671)
XLA Ops:
  0.7 4.5 %edge_terms.1 = (f32[3,136,512]{2,1,0:T(8,128)}, f32[3,136,512]{2,1,0:T(8,128)}, f32[4,16,512]{2,1,0:T(8,128)}) custom-call(s32[1]{0:T(128)} %bitcast.core_ref, f32[1,16,512]{2,1,0:T(8,128)} %refs_0_.1, f32[1,16,512]{2,1,0:T(8,128)} %refs_1_.1, f32[1,16,512]{2,1,0:T(8,128)} %refs_2_.1, s32[1,16,512]{2,1,0:T(8,128)} %bitcast.17, f32[4096,512]{1,0:T(8,128)} %bitcast.8, ...), custom_call_target="tpu_custom_call" | custom-call | tf_op jit(solution)/shard_map/edge_terms/pallas_call | solution.py:111
  5.1 4.1 %collective-permute-start = (f32[3,136,512]{2,1,0:T(8,128)}, f32[3,136,512]{2,1,0:T(8,128)S(1)}, u32[]{:S(2)}, u32[]{:S(2)}) collective-permute-start(f32[3,136,512]{2,1,0:T(8,128)} %get-tuple-element.18), channel_id=1, source_target_pairs={{0,1},{1,2},{2,3},{3,4},{4,5},{5,6},{6,7},{7,8},{8,9},{9,10},{10,1... | collective-permute-start | bytes 2506760 | tf_op jit(solution)/shard_map/ppermute | solution.py:617
  9.2 1.3 collective-permute-start.1
  11.1 0.6 fusion.12
  11.8 18.6 %lay_basis.1 = (f32[16,256,512]{2,1,0:T(8,128)}, f32[16,24,256]{2,1,0:T(8,128)}) custom-call(f32[16,512]{1,0:T(8,128)} %get-tuple-element.31.count_ref, f32[16,512]{1,0:T(8,128)} %get-tuple-element.30.value_ref, f32[4096,512]{1,0:T(8,128)} %bitcast.12, f32[4096,512]{1,0:T(8,128)} %bitcast.13, f32[4096,512]{1,0:T(8,128)} %bitcast.14, f32[4096,512]{1,0:T(8,128)} %bitcast.15), custom_call_target="tpu_custom_call" | custom-call | flops 20000000000 | bytes 17000000 | tf_op jit(solution)/shard_map/lay_basis/pallas_call | solution.py:180
  30.5 1.8 %collective-permute-start.2 = (f32[3,136,512]{2,1,0:T(8,128)S(1)}, f32[3,136,512]{2,1,0:T(8,128)S(1)}, u32[]{:S(2)}, u32[]{:S(2)}) collective-permute-start(f32[3,136,512]{2,1,0:T(8,128)S(1)} %collective-permute-done.low_mine), channel_id=1, source_target_pairs={{0,16},{16,0},{32,48},{48,32},{64,80},{80,64},{96,112},{112,96},{1... | collective-permute-start | bytes 2506760 | tf_op jit(solution)/shard_map/ppermute | solution.py:621
  32.9 1.4 collective-permute-done.2.low_theirs
  34.3 1.2 collective-permute-done.3.high_theirs
  35.5 0.9 copy-done.13
  36.4 33.2 %prop_terms.1 = f32[16,40,256]{2,1,0:T(8,128)} custom-call(s32[3]{0:T(128)} %pad_add_fusion.1.place_ref, f32[4,16,512]{2,1,0:T(8,128)} %get-tuple-element.16.model_ref, f32[16,256,512]{2,1,0:T(8,128)} %get-tuple-element.17.field_ref, f32[3,136,512]{2,1,0:T(8,128)} %copy-done.10, f32[3,136,512]{2,1,0:T(8,128)} %copy-done.12, f32[3,136,512]{2,1,0:T(8,128)} %copy-done.11, ...), custom_call_target="tpu_custom_call" | custom-call | flops 35000000512 | bytes 12000000 | tf_op jit(solution)/shard_map/prop_terms/pallas_call | solution.py:342
  69.5 9.2 %all-to-all-start = ((f32[16,40,256]{2,1,0:T(8,128)}), f32[16,40,256]{2,1,0:T(8,128)S(1)}, u32[]{:S(2)}, u32[]{:S(2)}) async-start(f32[16,40,256]{2,1,0:T(8,128)} %prop_terms.1), calls=%async_computation | async-start | bytes 1310720 | tf_op jit(solution)/shard_map/all_to_all | solution.py:655
  78.7 12.1 %all-to-all-done = f32[16,40,256]{2,1,0:T(8,128)S(1)} async-done(((f32[16,40,256]{2,1,0:T(8,128)}), f32[16,40,256]{2,1,0:T(8,128)S(1)}, u32[]{:S(2)}, u32[]{:S(2)}) %all-to-all-start) | async-done | bytes 655392 | tf_op jit(solution)/shard_map/all_to_all | solution.py:655
  91.0 14.7 %all_to_all.10.own_ref = f32[16,40,256]{2,1,0:T(8,128)S(1)} all-to-all(f32[16,40,256]{2,1,0:T(8,128)S(1)} %broadcast_in_dim.25), channel_id=1, replica_groups=mesh['tm'=8,'tile'=16] {'tile'}, dimensions={0} | all-to-all | bytes 1310720 | tf_op jit(solution)/shard_map/all_to_all | solution.py:659
  105.7 2.4 %collective-permute-start.4 = (f32[16,40,256]{2,1,0:T(8,128)S(1)}, f32[16,40,256]{2,1,0:T(8,128)S(1)}, u32[]{:S(2)}, u32[]{:S(2)}) collective-permute-start(f32[16,40,256]{2,1,0:T(8,128)S(1)} %all_to_all.10.own_ref), channel_id=1, source_target_pairs={{0,16},{16,0},{32,48},{48,32},{64,80},{80,64},{96,112},{112,96},{1... | collective-permute-start | bytes 1966088 | tf_op jit(solution)/shard_map/ppermute | solution.py:621
  108.2 0.7 pad_add_fusion.place_ref
  108.8 1.1 collective-permute-done.4.other_ref
  109.9 0.9 copy-done.1
  110.8 11.2 %merge_pair.1 = (f32[2,264,256]{2,1,0:T(8,128)}, f32[264,256]{1,0:T(8,128)}, f32[256,256]{1,0:T(8,128)}, f32[256,256]{1,0:T(8,128)}, f32[256,256]{1,0:T(8,128)}, /*index=5*/f32[2,8,256]{2,1,0:T(8,128)}) custom-call(s32[2]{0:T(128)} %pad_add_fusion.place_ref, f32[16,40,256]{2,1,0:T(8,128)} %copy-done, f32[16,40,256]{2,1,0:T(8,128)} %copy-done.1), custom_call_target="tpu_custom_call" | custom-call | tf_op jit(solution)/shard_map/merge_pair/pallas_call | solution.py:511
  122.0 2.7 %collective-permute-start.7 = (f32[264,256]{1,0:T(8,128)}, f32[264,256]{1,0:T(8,128)S(1)}, u32[]{:S(2)}, u32[]{:S(2)}) collective-permute-start(f32[264,256]{1,0:T(8,128)} %get-tuple-element.25), channel_id=1, source_target_pairs={{0,96},{16,112},{32,0},{48,16},{64,32},{80,48},{96,64},{112,80},{1... | collective-permute-start | bytes 811016 | tf_op jit(solution)/shard_map/ppermute | solution.py:617
  124.7 6.5 %collective-permute-done.5.m_prev = f32[264,256]{1,0:T(8,128)S(1)} collective-permute-done((f32[264,256]{1,0:T(8,128)}, f32[264,256]{1,0:T(8,128)S(1)}, u32[]{:S(2)}, u32[]{:S(2)}) %collective-permute-start.5) | collective-permute-done | bytes 270368 | tf_op jit(solution)/shard_map/ppermute | solution.py:617
  131.2 2.0 %collective-permute-start.6 = (f32[264,256]{1,0:T(8,128)S(1)}, f32[264,256]{1,0:T(8,128)S(1)}, u32[]{:S(2)}, u32[]{:S(2)}) collective-permute-start(f32[264,256]{1,0:T(8,128)S(1)} %collective-permute-done.5.m_prev), channel_id=1, source_target_pairs={{0,16},{16,0},{32,48},{48,32},{64,80},{80,64},{96,112},{112,96},{1... | collective-permute-start | bytes 811016 | tf_op jit(solution)/shard_map/ppermute | solution.py:621
  133.2 4.3 %collective-permute-start.8 = (f32[264,256]{1,0:T(8,128)S(1)}, f32[264,256]{1,0:T(8,128)S(1)}, u32[]{:S(2)}, u32[]{:S(2)}) collective-permute-start(f32[264,256]{1,0:T(8,128)S(1)} %collective-permute-done.7.m_next), channel_id=1, source_target_pairs={{0,16},{16,0},{32,48},{48,32},{64,80},{80,64},{96,112},{112,96},{1... | collective-permute-start | bytes 811016 | tf_op jit(solution)/shard_map/ppermute | solution.py:621
  138.7 0.6 collective-permute-done.10.o_far
  140.0 13.3 %solve_chain.1 = (f32[1,2,256]{2,1,0:T(2,128)}, f32[1,16,512]{2,1,0:T(8,128)}) custom-call(s32[2]{0:T(128)} %pad_add_fusion.place_ref, f32[2,264,256]{2,1,0:T(8,128)} %get-tuple-element.24.both_ref, f32[264,256]{1,0:T(8,128)} %copy-done.2, f32[264,256]{1,0:T(8,128)} %copy-done.5, f32[264,256]{1,0:T(8,128)} %copy-done.3, f32[264,256]{1,0:T(8,128)} %copy-done.6, ...), custom_call_target="tpu_custom_call" | custom-call | tf_op jit(solution)/shard_map/solve_chain/pallas_call | solution.py:594
  (46 shorter events, 3.3 us)
Async XLA Ops:
  0.6 9.9 %copy-start.9 = (s32[1,512]{1,0:T(1,128)S(1)}, s32[1,512]{1,0:T(1,128)}, u32[]{:S(2)}) copy-start(s32[1,512]{1,0:T(1,128)} %param.12) | copy-start | bytes 6148
  0.6 9.9 %copy-start.8 = (f32[1,512]{1,0:T(1,128)S(1)}, f32[1,512]{1,0:T(1,128)}, u32[]{:S(2)}) copy-start(f32[1,512]{1,0:T(1,128)} %param.13) | copy-start | bytes 6148
  5.1 25.3 %collective-permute-start = (f32[3,136,512]{2,1,0:T(8,128)}, f32[3,136,512]{2,1,0:T(8,128)S(1)}, u32[]{:S(2)}, u32[]{:S(2)}) collective-permute-start(f32[3,136,512]{2,1,0:T(8,128)} %get-tuple-element.18), channel_id=1, source_target_pairs={{0,1},{1,2},{2,3},{3,4},{4,5},{5,6},{6,7},{7,8},{8,9},{9,10},{10,1... | collective-permute-start | bytes 2506760 | tf_op jit(solution)/shard_map/ppermute | solution.py:617
  9.2 21.3 %collective-permute-start.1 = (f32[3,136,512]{2,1,0:T(8,128)}, f32[3,136,512]{2,1,0:T(8,128)S(1)}, u32[]{:S(2)}, u32[]{:S(2)}) collective-permute-start(f32[3,136,512]{2,1,0:T(8,128)} %get-tuple-element.19), channel_id=1, source_target_pairs={{1,0},{2,1},{3,2},{4,3},{5,4},{6,5},{7,6},{8,7},{9,8},{10,9},{11,1... | collective-permute-start | bytes 2506760 | tf_op jit(solution)/shard_map/ppermute | solution.py:617
  30.4 5.1 %copy-start.10 = (f32[3,136,512]{2,1,0:T(8,128)}, f32[3,136,512]{2,1,0:T(8,128)S(1)}, u32[]{:S(2)}) copy-start(f32[3,136,512]{2,1,0:T(8,128)S(1)} %collective-permute-done.low_mine) | copy-start | bytes 2506756
  30.5 5.0 %copy-start.11 = (f32[3,136,512]{2,1,0:T(8,128)}, f32[3,136,512]{2,1,0:T(8,128)S(1)}, u32[]{:S(2)}) copy-start(f32[3,136,512]{2,1,0:T(8,128)S(1)} %collective-permute-done.1.high_mine) | copy-start | bytes 2506756
  30.5 3.8 %collective-permute-start.2 = (f32[3,136,512]{2,1,0:T(8,128)S(1)}, f32[3,136,512]{2,1,0:T(8,128)S(1)}, u32[]{:S(2)}, u32[]{:S(2)}) collective-permute-start(f32[3,136,512]{2,1,0:T(8,128)S(1)} %collective-permute-done.low_mine), channel_id=1, source_target_pairs={{0,16},{16,0},{32,48},{48,32},{64,80},{80,64},{96,112},{112,96},{1... | collective-permute-start | bytes 2506760 | tf_op jit(solution)/shard_map/ppermute | solution.py:621
  32.3 3.2 %collective-permute-start.3 = (f32[3,136,512]{2,1,0:T(8,128)S(1)}, f32[3,136,512]{2,1,0:T(8,128)S(1)}, u32[]{:S(2)}, u32[]{:S(2)}) collective-permute-start(f32[3,136,512]{2,1,0:T(8,128)S(1)} %collective-permute-done.1.high_mine), channel_id=1, source_target_pairs={{0,16},{16,0},{32,48},{48,32},{64,80},{80,64},{96,112},{112,96},{1... | collective-permute-start | bytes 2506760 | tf_op jit(solution)/shard_map/ppermute | solution.py:621
  34.3 1.2 copy-start.12
  35.5 0.9 copy-start.13
  69.5 21.3 %all-to-all-start = ((f32[16,40,256]{2,1,0:T(8,128)}), f32[16,40,256]{2,1,0:T(8,128)S(1)}, u32[]{:S(2)}, u32[]{:S(2)}) async-start(f32[16,40,256]{2,1,0:T(8,128)} %prop_terms.1), calls=%async_computation | async-start | bytes 1310720 | tf_op jit(solution)/shard_map/all_to_all | solution.py:655
  105.7 4.2 %copy-start = (f32[16,40,256]{2,1,0:T(8,128)}, f32[16,40,256]{2,1,0:T(8,128)S(1)}, u32[]{:S(2)}) copy-start(f32[16,40,256]{2,1,0:T(8,128)S(1)} %all_to_all.10.own_ref) | copy-start | bytes 1966084
  105.7 4.2 %collective-permute-start.4 = (f32[16,40,256]{2,1,0:T(8,128)S(1)}, f32[16,40,256]{2,1,0:T(8,128)S(1)}, u32[]{:S(2)}, u32[]{:S(2)}) collective-permute-start(f32[16,40,256]{2,1,0:T(8,128)S(1)} %all_to_all.10.own_ref), channel_id=1, source_target_pairs={{0,16},{16,0},{32,48},{48,32},{64,80},{80,64},{96,112},{112,96},{1... | collective-permute-start | bytes 1966088 | tf_op jit(solution)/shard_map/ppermute | solution.py:621
  109.9 0.9 copy-start.1
  122.0 9.2 %collective-permute-start.5 = (f32[264,256]{1,0:T(8,128)}, f32[264,256]{1,0:T(8,128)S(1)}, u32[]{:S(2)}, u32[]{:S(2)}) collective-permute-start(f32[264,256]{1,0:T(8,128)} %get-tuple-element.25), channel_id=1, source_target_pairs={{0,32},{16,48},{32,64},{48,80},{64,96},{80,112},{96,0},{112,16},{1... | collective-permute-start | bytes 811016 | tf_op jit(solution)/shard_map/ppermute | solution.py:617
  122.0 11.2 %collective-permute-start.7 = (f32[264,256]{1,0:T(8,128)}, f32[264,256]{1,0:T(8,128)S(1)}, u32[]{:S(2)}, u32[]{:S(2)}) collective-permute-start(f32[264,256]{1,0:T(8,128)} %get-tuple-element.25), channel_id=1, source_target_pairs={{0,96},{16,112},{32,0},{48,16},{64,32},{80,48},{96,64},{112,80},{1... | collective-permute-start | bytes 811016 | tf_op jit(solution)/shard_map/ppermute | solution.py:617
  124.7 12.8 %collective-permute-start.9 = (f32[264,256]{1,0:T(8,128)}, f32[264,256]{1,0:T(8,128)S(1)}, u32[]{:S(2)}, u32[]{:S(2)}) collective-permute-start(f32[264,256]{1,0:T(8,128)} %get-tuple-element.25), channel_id=1, source_target_pairs={{0,64},{16,80},{32,96},{48,112},{64,0},{80,16},{96,32},{112,48},{1... | collective-permute-start | bytes 811016 | tf_op jit(solution)/shard_map/ppermute | solution.py:617
  131.2 8.1 %copy-start.2 = (f32[264,256]{1,0:T(8,128)}, f32[264,256]{1,0:T(8,128)S(1)}, u32[]{:S(2)}) copy-start(f32[264,256]{1,0:T(8,128)S(1)} %collective-permute-done.5.m_prev) | copy-start | bytes 811012
  131.2 7.0 %collective-permute-start.6 = (f32[264,256]{1,0:T(8,128)S(1)}, f32[264,256]{1,0:T(8,128)S(1)}, u32[]{:S(2)}, u32[]{:S(2)}) collective-permute-start(f32[264,256]{1,0:T(8,128)S(1)} %collective-permute-done.5.m_prev), channel_id=1, source_target_pairs={{0,16},{16,0},{32,48},{48,32},{64,80},{80,64},{96,112},{112,96},{1... | collective-permute-start | bytes 811016 | tf_op jit(solution)/shard_map/ppermute | solution.py:621
  133.2 6.1 %copy-start.3 = (f32[264,256]{1,0:T(8,128)}, f32[264,256]{1,0:T(8,128)S(1)}, u32[]{:S(2)}) copy-start(f32[264,256]{1,0:T(8,128)S(1)} %collective-permute-done.7.m_next) | copy-start | bytes 811012
  133.2 5.5 %collective-permute-start.8 = (f32[264,256]{1,0:T(8,128)S(1)}, f32[264,256]{1,0:T(8,128)S(1)}, u32[]{:S(2)}, u32[]{:S(2)}) collective-permute-start(f32[264,256]{1,0:T(8,128)S(1)} %collective-permute-done.7.m_next), channel_id=1, source_target_pairs={{0,16},{16,0},{32,48},{48,32},{64,80},{80,64},{96,112},{112,96},{1... | collective-permute-start | bytes 811016 | tf_op jit(solution)/shard_map/ppermute | solution.py:621
  137.5 1.8 %copy-start.4 = (f32[264,256]{1,0:T(8,128)}, f32[264,256]{1,0:T(8,128)S(1)}, u32[]{:S(2)}) copy-start(f32[264,256]{1,0:T(8,128)S(1)} %collective-permute-done.9.m_far) | copy-start | bytes 811012
  137.5 1.8 %collective-permute-start.10 = (f32[264,256]{1,0:T(8,128)S(1)}, f32[264,256]{1,0:T(8,128)S(1)}, u32[]{:S(2)}, u32[]{:S(2)}) collective-permute-start(f32[264,256]{1,0:T(8,128)S(1)} %collective-permute-done.9.m_far), channel_id=1, source_target_pairs={{0,16},{16,0},{32,48},{48,32},{64,80},{80,64},{96,112},{112,96},{1... | collective-permute-start | bytes 811016 | tf_op jit(solution)/shard_map/ppermute | solution.py:621
  138.1 1.2 copy-start.5
  (2 other events, 1.4 us)

commit v4 on v3

--- a/solution.py
+++ b/solution.py
@@ -396,12 +396,16 @@
     width = mats[0].shape[0]
     row, col = eye_mask(width)
     identity = jnp.where(row == col, 1.0, 0.0).astype(jnp.float32)
-    guesses = []
+    found = []
+    error = jnp.float32(0.0)
     for mat in mats:
         bound = jnp.max(jnp.sum(jnp.abs(mat), axis=0, keepdims=True), axis=1, keepdims=True)
         trace = jnp.sum(jnp.sum(identity * mat, axis=0, keepdims=True), axis=1, keepdims=True)
         square = jnp.sum(jnp.sum(mat * mat, axis=0, keepdims=True), axis=1, keepdims=True)
-        guesses.append(identity * jnp.minimum(trace / square, 1.9 / bound))
+        scale = jnp.minimum(trace / square, 1.9 / bound)
+        rest = identity - scale * mat
+        found.append(scale * (identity + rest))
+        error = jnp.maximum(error, jnp.sum(rest * rest))
 
     def stage(state, passes, goal, slowest):
         def more(state):
@@ -420,21 +424,21 @@
 
         return lax.while_loop(more, improve, state)
 
-    found = guesses
     turn = jnp.int32(0)
-    large = jnp.float32(1e30)
     for passes, goal, slowest in (((1, 1), 2.0, 0.5), ((3, 1), 1e-3, 0.5), ((6, 3), 1e-6, 2.0)):
-        state = stage((turn, large, jnp.float32(0.0), *found), passes, goal, slowest)
-        turn, found = state[0], state[3:]
+        begin = jnp.maximum(error, 2.0 * goal) if passes[0] == 6 else error
+        state = stage((turn, begin, jnp.float32(0.0), *found), passes, goal, slowest)
+        turn, error, found = state[0], state[1], state[3:]
     return found
 
 
 def pair_kernel(
-    place_ref, own_ref, other_ref, both_ref, send_ref, left_ref, right_ref, outer_ref, small_ref
+    own_ref, other_ref, both_ref, send_ref, left_ref, right_ref, outer_ref, small_ref
 ):
     tiles, _, width = own_ref.shape
     part = width // tiles
-    core, chip = place_ref[0], place_ref[1]
+    group = lax.axis_index("tm")
+    core, chip = group & 1, group >> 1
     first = core == 0
     row, col = eye_mask(width)
     identity = jnp.where(row == col, 1.0, 0.0).astype(jnp.float32)
@@ -504,34 +508,35 @@
     send_ref[...] = jnp.where(first, both_ref[0], both_ref[1])
 
 
-def merge_pair(place, own, other):
+def merge_pair(own, other):
     width = own.shape[2]
     vmem = pl.BlockSpec(memory_space=pltpu.VMEM)
-    block = jax.ShapeDtypeStruct((width, width), jnp.float32)
+    block = pltpu.VMEM((width, width), jnp.float32)
     return pl.pallas_call(
         pair_kernel,
-        in_specs=[pl.BlockSpec(memory_space=pltpu.SMEM)] + [vmem] * 2,
+        in_specs=[vmem] * 2,
         out_specs=[vmem] * 6,
         out_shape=[
-            jax.ShapeDtypeStruct((2, width + TAIL, width), jnp.float32),
-            jax.ShapeDtypeStruct((width + TAIL, width), jnp.float32),
+            pltpu.VMEM((2, width + TAIL, width), jnp.float32),
+            pltpu.VMEM((width + TAIL, width), jnp.float32),
             block,
             block,
             block,
-            jax.ShapeDtypeStruct((2, TAIL, width), jnp.float32),
+            pltpu.VMEM((2, TAIL, width), jnp.float32),
         ],
         name="merge_pair",
-    )(place, own, other)
+    )(own, other)
 
 
 def chain_kernel(
-    place_ref, both_ref, m_prev, o_prev, m_next, o_next, m_far, o_far,
+    both_ref, m_prev, o_prev, m_next, o_next, m_far, o_far,
     left_ref, right_ref, outer_ref, small_ref,
     basis_ref, coeff_ref, end_ref, blocks, basis, weight, sem,
 ):
     fetch = pltpu.make_async_copy(basis_ref, basis, sem)
     fetch.start()
-    core, chip = place_ref[0], place_ref[1]
+    group = lax.axis_index("tm")
+    core, chip = group & 1, group >> 1
     width = both_ref.shape[2]
     row, col = eye_mask(width)
     blocks[chip] = both_ref[...]
@@ -587,14 +592,13 @@
     end_ref[0] = lax.fori_loop(0, width, add, jnp.zeros((rows, columns), jnp.float32), unroll=8)
 
 
-def solve_chain(place, both, received, kept, basis2, rows):
+def solve_chain(both, received, kept, basis2, rows):
     width = both.shape[2]
     columns = basis2.shape[1]
     vmem = pl.BlockSpec(memory_space=pltpu.VMEM)
     return pl.pallas_call(
         chain_kernel,
-        in_specs=[pl.BlockSpec(memory_space=pltpu.SMEM)]
-        + [vmem] * 11
+        in_specs=[vmem] * 11
         + [pl.BlockSpec(memory_space=pltpu.HBM)],
         out_specs=[vmem, vmem],
         out_shape=[
@@ -608,13 +612,17 @@
             pltpu.SemaphoreType.DMA,
         ],
         name="solve_chain",
-    )(place, both, *received, *kept, basis2)
+    )(both, *received, *kept, basis2)
 
 
 def shift(value, axis, step, wrap):
     size = lax.axis_size(axis)
     pairs = [(i, (i + step) % size) for i in range(size) if wrap or 0 <= i + step < size]
     return lax.ppermute(value, axis, pairs)
+
+
+def resident(value):
+    return pltpu.with_memory_space_constraint(value, pltpu.VMEM)
 
 
 def swap_core(value):
@@ -659,13 +667,13 @@
     own = lax.all_to_all(jnp.broadcast_to(slices[None], terms.shape), "tile", 0, 0, tiled=True)
     other = swap_core(own)
 
-    place = jnp.stack([core, chip])
-    both, send, *kept = merge_pair(place, own, other)
+    both, send, *kept = merge_pair(own, other)
     received = []
     for step in (2, -2, 4):
         mine = shift(send, "tm", step, True)
-        received += [mine, swap_core(mine)]
-    return tuple(solve_chain(place, both, received, kept, basis2, rows))
+        received += [resident(mine), resident(swap_core(mine))]
+    kept = [resident(value) for value in kept]
+    return tuple(solve_chain(resident(both), received, kept, basis2, rows))
 
 
 def solution(mesh):

time: 155 us -> 150 us (0.968)
  waiting for transfers between devices: 23.5 us -> 28.5 us
  starting transfers between devices: 28.4 us -> 24.4 us
  Pallas kernels: 80.8 us -> 77.4 us
    ppermute x6, starting transfers between devices: 11.2 us -> 7.03 us  [swap_core(): lax.ppermute(value, 'tm', [(i, i ^ 1) for i in range(lax.axis_size('tm'))])]
    ppermute x5, waiting for transfers between devices: 6.56 us -> 10.6 us  [shift(): return lax.ppermute(value, axis, pairs)]
    pallas_call x2, Pallas kernels: 24.5 us -> 21.1 us  [the longest x1 11 us: solve_chain(): pl.pallas_call(chain_kernel, in_specs=[vmem] * 11 + [pl.BlockSpec(memory_...]
  transfers between devices with their start and end apart: 12 -> 12, of which waited for: 8 -> 9; matrix products, arithmetic and copies ran while one was open for 2% -> 1% of each run, Pallas kernels for 12% -> 12%
where the time goes in v4:
time: 150 us
  Pallas kernels  77.4 us (52%)
  waiting for transfers between devices  28.5 us (19%)
  starting transfers between devices  24.4 us (16%)
  blocking collectives  14.7 us (10%)
  local copies, waits for them, and re-layouts  2.44 us (2%)
    pallas_call x1, Pallas kernels, prop_terms(): pl.pallas_call(prop_kernel, grid_spec=pltpu.PrefetchScalarGridSpec(num_sc...  33.2 us
    pallas_call x1, Pallas kernels, lay_basis(): pl.pallas_call(functools.partial(lay_kernel, rows), grid=(width // block,...  18.6 us
    all_to_all x1, blocking collectives, shards(): lax.all_to_all(jnp.broadcast_to(slices[None], terms.shape), 'tile', 0, 0,...  14.7 us
    all_to_all x1, waiting for transfers between devices, shards(): slices = jnp.sum(lax.all_to_all(terms, 'tile', 0, 0, tiled=True), axis=0)  12.1 us
    pallas_call x1, Pallas kernels, solve_chain(): pl.pallas_call(chain_kernel, in_specs=[vmem] * 11 + [pl.BlockSpec(memory_...  11 us
    ppermute x5, waiting for transfers between devices, shift(): return lax.ppermute(value, axis, pairs)  10.6 us
    pallas_call x1, Pallas kernels, merge_pair(): pl.pallas_call(pair_kernel, in_specs=[vmem] * 2, out_specs=[vmem] * 6, ou...  10.1 us
    all_to_all x1, starting transfers between devices, shards(): slices = jnp.sum(lax.all_to_all(terms, 'tile', 0, 0, tiled=True), axis=0)  9.19 us
  transfers between devices with their start and end apart: 12, of which 9 were waited for; matrix products, arithmetic and copies ran while one was open for 1% of the time, Pallas kernels for 12%

profile of v4, /device:TPU:1, one launch (start us, length us, event | category | flops | bytes accessed | tf_op | source)
XLA Modules:
  0.0 149.7 jit_solution(2924271004665313356)
XLA Ops:
  0.7 4.5 %edge_terms.1 = (f32[3,136,512]{2,1,0:T(8,128)}, f32[3,136,512]{2,1,0:T(8,128)}, f32[4,16,512]{2,1,0:T(8,128)}) custom-call(s32[1]{0:T(128)} %bitcast.core_ref, f32[1,16,512]{2,1,0:T(8,128)} %refs_0_.1, f32[1,16,512]{2,1,0:T(8,128)} %refs_1_.1, f32[1,16,512]{2,1,0:T(8,128)} %refs_2_.1, s32[1,16,512]{2,1,0:T(8,128)} %bitcast.16, f32[4096,512]{1,0:T(8,128)} %bitcast.7, ...), custom_call_target="tpu_custom_call" | custom-call | tf_op jit(solution)/shard_map/edge_terms/pallas_call | solution.py:111
  5.1 4.1 %collective-permute-start = (f32[3,136,512]{2,1,0:T(8,128)}, f32[3,136,512]{2,1,0:T(8,128)S(1)}, u32[]{:S(2)}, u32[]{:S(2)}) collective-permute-start(f32[3,136,512]{2,1,0:T(8,128)} %get-tuple-element.18), channel_id=1, source_target_pairs={{0,1},{1,2},{2,3},{3,4},{4,5},{5,6},{6,7},{7,8},{8,9},{9,10},{10,1... | collective-permute-start | bytes 2506760 | tf_op jit(solution)/shard_map/ppermute | solution.py:621
  9.2 1.3 collective-permute-start.1
  11.8 18.6 %lay_basis.1 = (f32[16,256,512]{2,1,0:T(8,128)}, f32[16,24,256]{2,1,0:T(8,128)}) custom-call(f32[16,512]{1,0:T(8,128)} %get-tuple-element.31.count_ref, f32[16,512]{1,0:T(8,128)} %get-tuple-element.30.value_ref, f32[4096,512]{1,0:T(8,128)} %bitcast.11, f32[4096,512]{1,0:T(8,128)} %bitcast.12, f32[4096,512]{1,0:T(8,128)} %bitcast.13, f32[4096,512]{1,0:T(8,128)} %bitcast.14), custom_call_target="tpu_custom_call" | custom-call | flops 20000000000 | bytes 17000000 | tf_op jit(solution)/shard_map/lay_basis/pallas_call | solution.py:180
  30.5 1.8 %collective-permute-start.2 = (f32[3,136,512]{2,1,0:T(8,128)S(1)}, f32[3,136,512]{2,1,0:T(8,128)S(1)}, u32[]{:S(2)}, u32[]{:S(2)}) collective-permute-start(f32[3,136,512]{2,1,0:T(8,128)S(1)} %collective-permute-done.low_mine), channel_id=1, source_target_pairs={{0,16},{16,0},{32,48},{48,32},{64,80},{80,64},{96,112},{112,96},{1... | collective-permute-start | bytes 2506760 | tf_op jit(solution)/shard_map/ppermute | solution.py:629
  32.9 1.4 collective-permute-done.2.low_theirs
  34.3 1.2 collective-permute-done.3.high_theirs
  35.5 0.9 copy-done.7
  36.4 33.2 %prop_terms.1 = f32[16,40,256]{2,1,0:T(8,128)} custom-call(s32[3]{0:T(128)} %pad_add_fusion.place_ref, f32[4,16,512]{2,1,0:T(8,128)} %get-tuple-element.16.model_ref, f32[16,256,512]{2,1,0:T(8,128)} %get-tuple-element.17.field_ref, f32[3,136,512]{2,1,0:T(8,128)} %copy-done.4, f32[3,136,512]{2,1,0:T(8,128)} %copy-done.6, f32[3,136,512]{2,1,0:T(8,128)} %copy-done.5, ...), custom_call_target="tpu_custom_call" | custom-call | flops 35000000512 | bytes 12000000 | tf_op jit(solution)/shard_map/prop_terms/pallas_call | solution.py:342
  69.6 9.2 %all-to-all-start = ((f32[16,40,256]{2,1,0:T(8,128)}), f32[16,40,256]{2,1,0:T(8,128)S(1)}, u32[]{:S(2)}, u32[]{:S(2)}) async-start(f32[16,40,256]{2,1,0:T(8,128)} %prop_terms.1), calls=%async_computation | async-start | bytes 1310720 | tf_op jit(solution)/shard_map/all_to_all | solution.py:663
  78.8 12.1 %all-to-all-done = f32[16,40,256]{2,1,0:T(8,128)S(1)} async-done(((f32[16,40,256]{2,1,0:T(8,128)}), f32[16,40,256]{2,1,0:T(8,128)S(1)}, u32[]{:S(2)}, u32[]{:S(2)}) %all-to-all-start) | async-done | bytes 655392 | tf_op jit(solution)/shard_map/all_to_all | solution.py:663
  91.1 14.7 %all_to_all.10.own_ref = f32[16,40,256]{2,1,0:T(8,128)S(1)} all-to-all(f32[16,40,256]{2,1,0:T(8,128)S(1)} %broadcast_in_dim.25), channel_id=1, replica_groups=mesh['tm'=8,'tile'=16] {'tile'}, dimensions={0} | all-to-all | bytes 1310720 | tf_op jit(solution)/shard_map/all_to_all | solution.py:667
  105.8 2.4 %collective-permute-start.4 = (f32[16,40,256]{2,1,0:T(8,128)S(1)}, f32[16,40,256]{2,1,0:T(8,128)S(1)}, u32[]{:S(2)}, u32[]{:S(2)}) collective-permute-start(f32[16,40,256]{2,1,0:T(8,128)S(1)} %all_to_all.10.own_ref), channel_id=1, source_target_pairs={{0,16},{16,0},{32,48},{48,32},{64,80},{80,64},{96,112},{112,96},{1... | collective-permute-start | bytes 1966088 | tf_op jit(solution)/shard_map/ppermute | solution.py:629
  108.2 1.7 %collective-permute-done.4.other_ref = f32[16,40,256]{2,1,0:T(8,128)S(1)} collective-permute-done((f32[16,40,256]{2,1,0:T(8,128)S(1)}, f32[16,40,256]{2,1,0:T(8,128)S(1)}, u32[]{:S(2)}, u32[]{:S(2)}) %collective-permute-start.4) | collective-permute-done | bytes 655392 | tf_op jit(solution)/shard_map/ppermute | solution.py:629
  109.9 0.9 copy-done.1
  110.8 10.1 %merge_pair.1 = (f32[2,264,256]{2,1,0:T(8,128)S(1)}, f32[264,256]{1,0:T(8,128)S(1)}, f32[256,256]{1,0:T(8,128)S(1)}, f32[256,256]{1,0:T(8,128)S(1)}, f32[256,256]{1,0:T(8,128)S(1)}, /*index=5*/f32[2,8,256]{2,1,0:T(8,128)S(1)}) custom-call(f32[16,40,256]{2,1,0:T(8,128)} %copy-done, f32[16,40,256]{2,1,0:T(8,128)} %copy-done.1), custom_call_target="tpu_custom_call" | custom-call | tf_op jit(solution)/shard_map/merge_pair/pallas_call | solution.py:515
  121.0 1.5 %collective-permute-start.5 = (f32[264,256]{1,0:T(8,128)S(1)}, f32[264,256]{1,0:T(8,128)S(1)}, u32[]{:S(2)}, u32[]{:S(2)}) collective-permute-start(f32[264,256]{1,0:T(8,128)S(1)} %get-tuple-element.25), channel_id=1, source_target_pairs={{0,32},{16,48},{32,64},{48,80},{64,96},{80,112},{96,0},{112,16},{1... | collective-permute-start | bytes 811016 | tf_op jit(solution)/shard_map/ppermute | solution.py:621
  122.5 1.2 collective-permute-start.7
  123.7 6.5 %collective-permute-done.9.m_far = f32[264,256]{1,0:T(8,128)S(1)} collective-permute-done((f32[264,256]{1,0:T(8,128)S(1)}, f32[264,256]{1,0:T(8,128)S(1)}, u32[]{:S(2)}, u32[]{:S(2)}) %collective-permute-start.9) | collective-permute-done | bytes 270368 | tf_op jit(solution)/shard_map/ppermute | solution.py:621
  130.2 2.1 %collective-permute-start.10 = (f32[264,256]{1,0:T(8,128)S(1)}, f32[264,256]{1,0:T(8,128)S(1)}, u32[]{:S(2)}, u32[]{:S(2)}) collective-permute-start(f32[264,256]{1,0:T(8,128)S(1)} %collective-permute-done.9.m_far), channel_id=1, source_target_pairs={{0,16},{16,0},{32,48},{48,32},{64,80},{80,64},{96,112},{112,96},{1... | collective-permute-start | bytes 811016 | tf_op jit(solution)/shard_map/ppermute | solution.py:629
  132.3 4.0 %collective-permute-done.5.m_prev = f32[264,256]{1,0:T(8,128)S(1)} collective-permute-done((f32[264,256]{1,0:T(8,128)S(1)}, f32[264,256]{1,0:T(8,128)S(1)}, u32[]{:S(2)}, u32[]{:S(2)}) %collective-permute-start.5) | collective-permute-done | bytes 270368 | tf_op jit(solution)/shard_map/ppermute | solution.py:621
  136.3 0.7 collective-permute-start.6
  137.0 1.2 collective-permute-done.6.o_prev
  138.5 11.0 %solve_chain.1 = (f32[1,2,256]{2,1,0:T(2,128)}, f32[1,16,512]{2,1,0:T(8,128)}) custom-call(f32[2,264,256]{2,1,0:T(8,128)S(1)} %get-tuple-element.24.both_ref, f32[264,256]{1,0:T(8,128)S(1)} %collective-permute-done.5.m_prev, f32[264,256]{1,0:T(8,128)S(1)} %collective-permute-done.6.o_prev, f32[264,256]{1,0:T(8,128)S(1)} %collective-permute-done.7.m_next, ...), custom_call_target="tpu_custom_call" | custom-call | tf_op jit(solution)/shard_map/solve_chain/pallas_call | solution.py:599
  (33 shorter events, 2.6 us)
Async XLA Ops:
  0.6 9.9 %copy-start.3 = (s32[1,512]{1,0:T(1,128)S(1)}, s32[1,512]{1,0:T(1,128)}, u32[]{:S(2)}) copy-start(s32[1,512]{1,0:T(1,128)} %param.12) | copy-start | bytes 6148
  0.6 9.9 %copy-start.2 = (f32[1,512]{1,0:T(1,128)S(1)}, f32[1,512]{1,0:T(1,128)}, u32[]{:S(2)}) copy-start(f32[1,512]{1,0:T(1,128)} %param.13) | copy-start | bytes 6148
  5.1 25.3 %collective-permute-start = (f32[3,136,512]{2,1,0:T(8,128)}, f32[3,136,512]{2,1,0:T(8,128)S(1)}, u32[]{:S(2)}, u32[]{:S(2)}) collective-permute-start(f32[3,136,512]{2,1,0:T(8,128)} %get-tuple-element.18), channel_id=1, source_target_pairs={{0,1},{1,2},{2,3},{3,4},{4,5},{5,6},{6,7},{7,8},{8,9},{9,10},{10,1... | collective-permute-start | bytes 2506760 | tf_op jit(solution)/shard_map/ppermute | solution.py:621
  9.2 21.3 %collective-permute-start.1 = (f32[3,136,512]{2,1,0:T(8,128)}, f32[3,136,512]{2,1,0:T(8,128)S(1)}, u32[]{:S(2)}, u32[]{:S(2)}) collective-permute-start(f32[3,136,512]{2,1,0:T(8,128)} %get-tuple-element.19), channel_id=1, source_target_pairs={{1,0},{2,1},{3,2},{4,3},{5,4},{6,5},{7,6},{8,7},{9,8},{10,9},{11,1... | collective-permute-start | bytes 2506760 | tf_op jit(solution)/shard_map/ppermute | solution.py:621
  30.4 5.1 %copy-start.4 = (f32[3,136,512]{2,1,0:T(8,128)}, f32[3,136,512]{2,1,0:T(8,128)S(1)}, u32[]{:S(2)}) copy-start(f32[3,136,512]{2,1,0:T(8,128)S(1)} %collective-permute-done.low_mine) | copy-start | bytes 2506756
  30.5 5.0 %copy-start.5 = (f32[3,136,512]{2,1,0:T(8,128)}, f32[3,136,512]{2,1,0:T(8,128)S(1)}, u32[]{:S(2)}) copy-start(f32[3,136,512]{2,1,0:T(8,128)S(1)} %collective-permute-done.1.high_mine) | copy-start | bytes 2506756
  30.5 3.8 %collective-permute-start.2 = (f32[3,136,512]{2,1,0:T(8,128)S(1)}, f32[3,136,512]{2,1,0:T(8,128)S(1)}, u32[]{:S(2)}, u32[]{:S(2)}) collective-permute-start(f32[3,136,512]{2,1,0:T(8,128)S(1)} %collective-permute-done.low_mine), channel_id=1, source_target_pairs={{0,16},{16,0},{32,48},{48,32},{64,80},{80,64},{96,112},{112,96},{1... | collective-permute-start | bytes 2506760 | tf_op jit(solution)/shard_map/ppermute | solution.py:629
  32.3 3.2 %collective-permute-start.3 = (f32[3,136,512]{2,1,0:T(8,128)S(1)}, f32[3,136,512]{2,1,0:T(8,128)S(1)}, u32[]{:S(2)}, u32[]{:S(2)}) collective-permute-start(f32[3,136,512]{2,1,0:T(8,128)S(1)} %collective-permute-done.1.high_mine), channel_id=1, source_target_pairs={{0,16},{16,0},{32,48},{48,32},{64,80},{80,64},{96,112},{112,96},{1... | collective-permute-start | bytes 2506760 | tf_op jit(solution)/shard_map/ppermute | solution.py:629
  34.3 1.2 copy-start.6
  35.5 0.9 copy-start.7
  69.6 21.3 %all-to-all-start = ((f32[16,40,256]{2,1,0:T(8,128)}), f32[16,40,256]{2,1,0:T(8,128)S(1)}, u32[]{:S(2)}, u32[]{:S(2)}) async-start(f32[16,40,256]{2,1,0:T(8,128)} %prop_terms.1), calls=%async_computation | async-start | bytes 1310720 | tf_op jit(solution)/shard_map/all_to_all | solution.py:663
  105.7 4.2 %copy-start = (f32[16,40,256]{2,1,0:T(8,128)}, f32[16,40,256]{2,1,0:T(8,128)S(1)}, u32[]{:S(2)}) copy-start(f32[16,40,256]{2,1,0:T(8,128)S(1)} %all_to_all.10.own_ref) | copy-start | bytes 1966084
  105.8 4.2 %collective-permute-start.4 = (f32[16,40,256]{2,1,0:T(8,128)S(1)}, f32[16,40,256]{2,1,0:T(8,128)S(1)}, u32[]{:S(2)}, u32[]{:S(2)}) collective-permute-start(f32[16,40,256]{2,1,0:T(8,128)S(1)} %all_to_all.10.own_ref), channel_id=1, source_target_pairs={{0,16},{16,0},{32,48},{48,32},{64,80},{80,64},{96,112},{112,96},{1... | collective-permute-start | bytes 1966088 | tf_op jit(solution)/shard_map/ppermute | solution.py:629
  109.9 0.9 copy-start.1
  120.9 9.3 %collective-permute-start.9 = (f32[264,256]{1,0:T(8,128)S(1)}, f32[264,256]{1,0:T(8,128)S(1)}, u32[]{:S(2)}, u32[]{:S(2)}) collective-permute-start(f32[264,256]{1,0:T(8,128)S(1)} %get-tuple-element.25), channel_id=1, source_target_pairs={{0,64},{16,80},{32,96},{48,112},{64,0},{80,16},{96,32},{112,48},{1... | collective-permute-start | bytes 811016 | tf_op jit(solution)/shard_map/ppermute | solution.py:621
  121.0 15.3 %collective-permute-start.5 = (f32[264,256]{1,0:T(8,128)S(1)}, f32[264,256]{1,0:T(8,128)S(1)}, u32[]{:S(2)}, u32[]{:S(2)}) collective-permute-start(f32[264,256]{1,0:T(8,128)S(1)} %get-tuple-element.25), channel_id=1, source_target_pairs={{0,32},{16,48},{32,64},{48,80},{64,96},{80,112},{96,0},{112,16},{1... | collective-permute-start | bytes 811016 | tf_op jit(solution)/shard_map/ppermute | solution.py:621
  122.5 14.4 %collective-permute-start.7 = (f32[264,256]{1,0:T(8,128)S(1)}, f32[264,256]{1,0:T(8,128)S(1)}, u32[]{:S(2)}, u32[]{:S(2)}) collective-permute-start(f32[264,256]{1,0:T(8,128)S(1)} %get-tuple-element.25), channel_id=1, source_target_pairs={{0,96},{16,112},{32,0},{48,16},{64,32},{80,48},{96,64},{112,80},{1... | collective-permute-start | bytes 811016 | tf_op jit(solution)/shard_map/ppermute | solution.py:621
  130.2 6.8 %collective-permute-start.10 = (f32[264,256]{1,0:T(8,128)S(1)}, f32[264,256]{1,0:T(8,128)S(1)}, u32[]{:S(2)}, u32[]{:S(2)}) collective-permute-start(f32[264,256]{1,0:T(8,128)S(1)} %collective-permute-done.9.m_far), channel_id=1, source_target_pairs={{0,16},{16,0},{32,48},{48,32},{64,80},{80,64},{96,112},{112,96},{1... | collective-permute-start | bytes 811016 | tf_op jit(solution)/shard_map/ppermute | solution.py:629
  136.3 1.9 %collective-permute-start.6 = (f32[264,256]{1,0:T(8,128)S(1)}, f32[264,256]{1,0:T(8,128)S(1)}, u32[]{:S(2)}, u32[]{:S(2)}) collective-permute-start(f32[264,256]{1,0:T(8,128)S(1)} %collective-permute-done.5.m_prev), channel_id=1, source_target_pairs={{0,16},{16,0},{32,48},{48,32},{64,80},{80,64},{96,112},{112,96},{1... | collective-permute-start | bytes 811016 | tf_op jit(solution)/shard_map/ppermute | solution.py:629
  137.0 1.6 %collective-permute-start.8 = (f32[264,256]{1,0:T(8,128)S(1)}, f32[264,256]{1,0:T(8,128)S(1)}, u32[]{:S(2)}, u32[]{:S(2)}) collective-permute-start(f32[264,256]{1,0:T(8,128)S(1)} %collective-permute-done.7.m_next), channel_id=1, source_target_pairs={{0,16},{16,0},{32,48},{48,32},{64,80},{80,64},{96,112},{112,96},{1... | collective-permute-start | bytes 811016 | tf_op jit(solution)/shard_map/ppermute | solution.py:629
